TPU v7x, 32 devices: a whole 2x2x4 slice. The times are simulated.
32 devices in a mesh: sp: 8 (over z, x), rep: 4 (over y, core).
Axes of the slice: x: 2, y: 2, z: 4, core: 2. Of those that a mesh axis runs over, the one named last changes fastest.
Arguments:
- incoming_embeddings: bfloat16 [4, 16, 256, 512], P('rep', 'sp'), may hold values from -16 to 16
- output_sensitivity: bfloat16 [4, 16, 256, 512], P('rep', 'sp'), may hold values from -6 to 6
- mixing_prenormal_multiplier: float32 [512], replicated, may hold values from 0.5 to 1.5
- triple_mapping_matrix: bfloat16 [512, 1536], replicated, may hold values from -1 to 1
- head_sharpness: float32 [8], replicated, may hold values from 0.5 to 300
- output_mapping_matrix: bfloat16 [512, 512], replicated, may hold values from -0.25 to 0.25
- residual_arm_factors: float32 [2, 512], replicated, may hold values from 0.5 to 1.5
- locality_prenormal_multiplier: float32 [512], replicated, may hold values from 0.5 to 1.5
- separable_kernel_pair: float32 [2, 3, 3, 512], replicated, may hold values from -2 to 2
Outputs:
- grad_input: bfloat16 [4, 16, 256, 512], P('rep', 'sp')
- grad_qkv: float32 [512, 1536], P('rep')
- grad_proj: float32 [512, 512], P('rep')
- grad_conv: float32 [2, 3, 3, 512], replicated
- grad_scale: float32 [2, 512], replicated
All inputs are finite; a program needn't handle non-finite values.
Results may differ from a plain program's by a relative error of at most 0.0095.
Values may be sent and summed in bfloat16 or wider, within the bound.
No kernel may reach another device: no remote copies, remote signals or barrier semaphores. Data moves between devices by JAX's collectives and lax.ppermute only.
A program may use at most 64 MiB of HBM per device.

v0:
```python
import jax
import jax.numpy as jnp
from jax import lax
from jax.sharding import PartitionSpec as P

D = 512
HEADS = 8
HEAD_DIM = 64
WIDTH = 256


EPS = 1e-06


def shifted_2(value, axis, steps):
    count = lax.axis_size(axis)
    leading, last = (max(0, -steps), min(count, count - steps))
    return lax.ppermute(value, axis, [(source, source + steps) for source in range(leading, last)])


def padded_2(block, sides, width):
    for axis, dim in sides:
        count = lax.axis_size(axis)
        forward = [(i, i + 1) for i in range(count - 1)]
        backward = [(target, source) for source, target in forward]
        low = lax.ppermute(
            lax.slice_in_dim(block, block.shape[dim] - width, None, axis=dim), axis, forward
        )
        high = lax.ppermute(lax.slice_in_dim(block, 0, width, axis=dim), axis, backward)
        block = jnp.concatenate([low, block, high], axis=dim)
    return block


def conv_valid(padded, kernel):
    row_count = padded.shape[0] - 2
    col_count = padded.shape[1] - 2
    total = jnp.zeros((row_count, col_count, padded.shape[2]), jnp.float32)
    for offset_row in range(3):
        for offset_col in range(3):
            total = (
                total
                + padded[offset_row : offset_row + row_count, offset_col : offset_col + col_count]
                * kernel[offset_row, offset_col]
            )
    return total


def gelu_grad(values):
    cumul = 0.5 * (1.0 + lax.erf(values * 0.7071067811865476))
    density = jnp.exp(-0.5 * values * values) * 0.3989422804014327
    return cumul + values * density


def norm_rows(values, gain_vec):
    floated = values.astype(jnp.float32)
    centre = jnp.mean(floated, -1, keepdims=True)
    centred = floated - centre
    variance = jnp.mean(centred * centred, -1, keepdims=True)
    inverse = lax.rsqrt(variance + EPS)
    normed = centred * inverse
    return (normed * gain_vec, normed, inverse)


def norm_back(upstream, gain_vec, normed, inverse):
    scaled = upstream * gain_vec
    return inverse * (
        scaled
        - jnp.mean(scaled, -1, keepdims=True)
        - normed * jnp.mean(scaled * normed, -1, keepdims=True)
    )


def pad_cols(field):
    return jnp.pad(field.astype(jnp.float32), ((0, 0), (1, 1), (0, 0)))


def fold_rims(grad_rows, rim_width):
    top_rim = grad_rows[:rim_width]
    bottom_rim = grad_rows[-rim_width:]
    from_below = shifted_2(top_rim, "sp", -1)
    from_above = shifted_2(bottom_rim, "sp", 1)
    core_rows = grad_rows[rim_width:-rim_width]
    core_rows = core_rows.at[:rim_width].add(from_above)
    return core_rows.at[-rim_width:].add(from_below)


def local_mix(act_image, separable_kernel_pair, up_two):
    extended = padded_2(act_image, (("sp", 0),), 1)
    padded_in = pad_cols(extended)
    h_one, back_one = jax.vjp(conv_valid, padded_in, separable_kernel_pair[0])
    hidden = jax.nn.gelu(h_one, approximate=False).astype(jnp.bfloat16)
    hidden_ext = padded_2(hidden, (("sp", 0),), 1)
    padded_hid = pad_cols(hidden_ext)
    spatial, back_two = jax.vjp(conv_valid, padded_hid, separable_kernel_pair[1])
    d_pad_hid, grad_w_two = back_two(up_two)
    d_hidden = fold_rims(d_pad_hid[:, 1:-1], 1)
    d_h_one = d_hidden * gelu_grad(h_one)
    d_pad_in, grad_w_one = back_one(d_h_one)
    d_act = fold_rims(d_pad_in[:, 1:-1], 1)
    return (spatial, d_act, jnp.stack([grad_w_one, grad_w_two]))


def shards(
    incoming_embeddings,
    output_sensitivity,
    mixing_prenormal_multiplier,
    triple_mapping_matrix,
    head_sharpness,
    output_mapping_matrix,
    residual_arm_factors,
    locality_prenormal_multiplier,
    separable_kernel_pair,
):
    f32 = jnp.float32
    row_count = incoming_embeddings.shape[1]
    token_count = row_count * WIDTH
    flat_rows = incoming_embeddings.reshape(token_count, D)
    act_one, normed_one, inverse_one = norm_rows(flat_rows, mixing_prenormal_multiplier)
    act_one = act_one.astype(jnp.bfloat16)
    mixed_rows = jnp.dot(act_one, triple_mapping_matrix, preferred_element_type=f32).astype(
        jnp.bfloat16
    )
    query_rows = mixed_rows[:, :D].reshape(token_count, HEADS, HEAD_DIM)
    key_rows = mixed_rows[:, D : 2 * D].reshape(token_count, HEADS, HEAD_DIM)
    value_rows = mixed_rows[:, 2 * D :].reshape(token_count, HEADS, HEAD_DIM)
    query_f = query_rows.astype(f32)
    key_f = key_rows.astype(f32)
    query_sq = jnp.sum(query_f * query_f, 0)
    key_sq = jnp.sum(key_f * key_f, 0)
    gram_part = jnp.einsum("mhc,mhe->hce", query_rows, key_rows, preferred_element_type=f32)
    covariance_accumulated, query_sq, key_sq = lax.psum((gram_part, query_sq, key_sq), "sp")
    query_norm = jnp.sqrt(query_sq + EPS)
    key_norm = jnp.sqrt(key_sq + EPS)
    softmax_divisor = query_norm[:, :, None] * key_norm[:, None, :]
    feature_affinity_logits = (
        head_sharpness[:, None, None] * covariance_accumulated / softmax_divisor
    )
    shifted = feature_affinity_logits - jnp.max(feature_affinity_logits, -1, keepdims=True)
    exponent = jnp.exp(shifted)
    attn_prob = exponent / jnp.sum(exponent, -1, keepdims=True)
    prob_low = attn_prob.astype(jnp.bfloat16)
    attended = jnp.einsum("hce,mhe->mhc", prob_low, value_rows, preferred_element_type=f32)
    attended = attended.reshape(token_count, D).astype(jnp.bfloat16)
    projected = jnp.dot(attended, output_mapping_matrix, preferred_element_type=f32)
    residual = (flat_rows.astype(f32) + residual_arm_factors[0] * projected).astype(jnp.bfloat16)
    act_two, normed_two, inverse_two = norm_rows(residual, locality_prenormal_multiplier)
    act_two = act_two.astype(jnp.bfloat16)
    upstream = output_sensitivity[0].astype(f32)
    spatial, d_act_image, grad_conv_part = local_mix(
        act_two.reshape(row_count, WIDTH, D),
        separable_kernel_pair,
        residual_arm_factors[1] * upstream,
    )
    up_flat = upstream.reshape(token_count, D)
    scale_two = jnp.sum(spatial.reshape(token_count, D) * up_flat, 0)
    d_residual = up_flat + norm_back(
        d_act_image.reshape(token_count, D), locality_prenormal_multiplier, normed_two, inverse_two
    )
    scale_one = jnp.sum(projected * d_residual, 0)
    d_proj = (residual_arm_factors[0] * d_residual).astype(jnp.bfloat16)
    grad_proj = jnp.einsum("md,me->de", attended, d_proj, preferred_element_type=f32)
    d_attended = lax.dot_general(
        d_proj, output_mapping_matrix, (((1,), (1,)), ((), ())), preferred_element_type=f32
    ).astype(jnp.bfloat16)
    d_att_heads = d_attended.reshape(token_count, HEADS, HEAD_DIM)
    prob_part = jnp.einsum("mhc,mhe->hce", d_att_heads, value_rows, preferred_element_type=f32)
    d_value = jnp.einsum("hce,mhc->mhe", prob_low, d_att_heads, preferred_element_type=f32)
    prob_grad = lax.psum(prob_part, "sp")
    logit_sensitivity = attn_prob * (prob_grad - jnp.sum(attn_prob * prob_grad, -1, keepdims=True))
    covariance_sensitivity = (
        logit_sensitivity * head_sharpness[:, None, None] / softmax_divisor
    ).astype(jnp.bfloat16)
    weighted = logit_sensitivity * feature_affinity_logits
    d_qsq = -jnp.sum(weighted, -1) / (2.0 * query_norm * query_norm)
    d_ksq = -jnp.sum(weighted, 1) / (2.0 * key_norm * key_norm)
    d_query = (
        jnp.einsum("hce,mhe->mhc", covariance_sensitivity, key_rows, preferred_element_type=f32)
        + 2.0 * d_qsq * query_f
    )
    d_key = (
        jnp.einsum("hce,mhc->mhe", covariance_sensitivity, query_rows, preferred_element_type=f32)
        + 2.0 * d_ksq * key_f
    )
    d_mixed = jnp.concatenate(
        [
            d_query.reshape(token_count, D),
            d_key.reshape(token_count, D),
            d_value.reshape(token_count, D),
        ],
        -1,
    ).astype(jnp.bfloat16)
    grad_qkv = jnp.einsum("md,me->de", act_one, d_mixed, preferred_element_type=f32)
    d_act_one = lax.dot_general(
        d_mixed, triple_mapping_matrix, (((1,), (1,)), ((), ())), preferred_element_type=f32
    )
    d_tokens = (
        d_residual + norm_back(d_act_one, mixing_prenormal_multiplier, normed_one, inverse_one)
    ).astype(jnp.bfloat16)
    grad_conv, grad_scale = lax.psum(
        (grad_conv_part, jnp.stack([scale_one, scale_two])), ("sp", "rep")
    )
    summed = lax.psum((grad_qkv, grad_proj), "sp")
    grad_qkv, grad_proj = (
        lax.psum_scatter(summed[0], "rep", scatter_dimension=0, tiled=True),
        lax.psum_scatter(summed[1], "rep", scatter_dimension=0, tiled=True),
    )
    return (d_tokens.reshape(1, row_count, WIDTH, D), grad_qkv, grad_proj, grad_conv, grad_scale)


def solution(mesh):
    placed = (
        P("rep", "sp", None, None),
        P("rep", "sp", None, None),
        P(),
        P(),
        P(),
        P(),
        P(),
        P(),
        P(),
    )
    return jax.shard_map(
        shards,
        mesh=mesh,
        in_specs=placed,
        out_specs=(P("rep", "sp", None, None), P("rep", None), P("rep", None), P(), P()),
        check_vma=False,
    )
```

profile of v0, /device:TPU:0, one launch (start us, length us, event | category | flops | bytes accessed | tf_op | source)
XLA Modules:
  0.0 406.8 jit_solution(5633907822766687097)
XLA Ops:
  7.2 0.9 fusion.95
  8.2 0.8 fusion.98
  9.0 2.3 fusion.63
  11.2 1.2 pad_add_fusion.1
  12.5 1.1 fusion.92
  13.6 5.7 %collective-permute-start = (f32[1,256,512]{2,1,0:T(8,128)}, f32[1,256,512]{2,1,0:T(8,128)}, u32[]{:S(2)}, u32[]{:S(2)}) collective-permute-start(f32[1,256,512]{2,1,0:T(8,128)} %get-tuple-element.97), channel_id=1, source_target_pairs={{0,4},{4,8},{8,12},{12,16},{16,20},{20,24},{24,28},{1,5},{5,9},{9,... | collective-permute-start | bytes 1572872 | tf_op jit(solution)/shard_map/ppermute | solution.py:18
  19.4 0.3 fusion.31
  19.7 0.2 fusion.36
  20.0 1.0 convolution_convert_fusion
  21.0 1.2 fusion.93
  22.3 0.3 copy-done.6
  22.5 0.2 copy.25
  22.8 1.4 copy.26
  24.2 1.0 fusion.100
  25.3 1.4 multiply_reduce_fusion.21
  26.9 19.2 %all-reduce.39 = (f32[8,64]{1,0:T(8,128)S(1)}, f32[8,64]{1,0:T(8,128)S(1)}) all-reduce(f32[8,64]{1,0:T(8,128)S(1)} %reduce_sum.314, f32[8,64]{1,0:T(8,128)S(1)} %reduce_sum.309), channel_id=1, replica_groups=mesh['sp'=8,'rep'=4] {'sp'}, use_global_device_ids=true, to_apply=%region_6.0 | all-reduce | flops 1024 | bytes 8192 | tf_op jit(solution)/shard_map/psum | solution.py:131
  46.1 2.1 copy.24
  48.2 47.8 %all-reduce.45.cloned.1.call-done = f32[8,64,64]{2,1,0:T(8,128)} async-done(((f32[8,64,64]{2,1,0:T(8,128)}), f32[8,64,64]{2,1,0:T(8,128)}) %all-reduce.45.cloned.1.call-update) | async-done | bytes 131088 | tf_op jit(solution)/shard_map/psum | solution.py:131
  96.0 3.7 fusion.99
  99.7 3.5 convolution_convert_fusion.1
  103.3 0.6 convert_reduce_fusion
  103.9 0.3 fusion.20
  104.2 0.2 fusion.15
  104.5 2.6 collective-permute-start.2
  107.1 1.3 collective-permute-start.3
  108.4 1.3 collective-permute-start.1
  109.9 17.9 %collective-permute-done.2 = bf16[1,256,512]{2,1,0:T(8,128)(2,1)S(1)} collective-permute-done((bf16[1,256,512]{2,1,0:T(8,128)(2,1)S(1)}, bf16[1,256,512]{2,1,0:T(8,128)(2,1)S(1)}, u32[]{:S(2)}, u32[]{:S(2)}) %collective-permute-start.2) | collective-permute-done | bytes 262176 | tf_op jit(solution)/shard_map/ppermute | solution.py:26
  127.8 0.2 maximum_convert_fusion
  128.0 1.2 fusion.54
  129.3 3.2 multiply_reduce_fusion.18
  132.5 1.3 broadcast_multiply_fusion
  133.9 1.2 pad_add_fusion
  135.2 4.4 %collective-permute-start.4 = (f32[1,256,512]{2,1,0:T(8,128)S(1)}, f32[1,256,512]{2,1,0:T(8,128)S(1)}, u32[]{:S(2)}, u32[]{:S(2)}) collective-permute-start(f32[1,256,512]{2,1,0:T(8,128)S(1)} %get-tuple-element.95), channel_id=1, source_target_pairs={{0,4},{4,8},{8,12},{12,16},{16,20},{20,24},{24,28},{1,5},{5,9},{9,... | collective-permute-start | bytes 1572872 | tf_op jit(solution)/shard_map/ppermute | solution.py:18
  139.6 1.5 collective-permute-start.5
  141.3 16.3 %collective-permute-done.4 = f32[1,256,512]{2,1,0:T(8,128)S(1)} collective-permute-done((f32[1,256,512]{2,1,0:T(8,128)S(1)}, f32[1,256,512]{2,1,0:T(8,128)S(1)}, u32[]{:S(2)}, u32[]{:S(2)}) %collective-permute-start.4) | collective-permute-done | bytes 524320 | tf_op jit(solution)/shard_map/ppermute | solution.py:18
  157.8 0.2 multiply_reduce_fusion.19
  157.9 0.4 fusion.16
  158.4 0.3 copy-done.4
  158.7 0.5 multiply_reduce_fusion
  159.2 0.2 copy-done.9
  159.4 0.5 convolution_convert_fusion.3
  159.9 0.8 copy-done.7
  160.7 1.0 fusion.101
  161.8 2.5 fusion.66
  164.3 4.5 %convolution_convert_fusion.2 = bf16[8,512,64]{1,2,0:T(8,128)(2,1)} fusion(bf16[512,8,64]{0,2,1:T(8,128)(2,1)} %bitcast.184, f32[8,64]{1,0:T(8,128)S(1)} %get-tuple-element.147, f32[8,64,64]{2,1,0:T(8,128)} %all-reduce.45.cloned.1.call-done, f32[8,64]{1,0:T(8,128)S(1)} %add_sqrt_fusion, f32[8,64]{1,0:T(8,128)S(1)} %add_sqrt_fusion.1, f32[8]{0:T(128)S(1)} %copy-done.18), kind=kOutput, calls=%fused_computation.28 | convolution fusion | flops 34013760 | bytes 1185824 | tf_op jit(solution)/shard_map/hce,mhc->mhe/dot_general | solution.py:167
  168.8 69.6 %all-reduce.47.cloned.1.call-done = f32[8,64,64]{2,1,0:T(8,128)} async-done(((f32[8,64,64]{2,1,0:T(8,128)}), f32[8,64,64]{2,1,0:T(8,128)}) %all-reduce.47.cloned.1.call-update) | async-done | bytes 131088 | tf_op jit(solution)/shard_map/psum | solution.py:168
  238.4 3.9 multiply_reduce_fusion.24
  242.3 4.8 %fusion.5 = bf16[512,8,64]{0,2,1:T(8,128)(2,1)} fusion(bf16[512,8,64]{0,2,1:T(8,128)(2,1)} %bitcast.189, bf16[512,8,64]{0,2,1:T(8,128)(2,1)} %bitcast.186, f32[8,64]{1,0:T(8,128)S(1)} %get-tuple-element.151, f32[8,64]{1,0:T(8,128)S(1)} %add_sqrt_fusion, f32[8,64]{1,0:T(8,128)S(1)} %add_sqrt_fusion.1, f32[8]{0:T(128)S(1)} %copy-done.18, ...), kind=kOutput, calls=%fused_computation.31 | convolution fusion | flops 34898496 | bytes 1843232 | tf_op jit(solution)/shard_map/hce,mhe->mhc/dot_general | solution.py:177
  247.1 5.2 %fusion.4 = bf16[512,8,64]{0,2,1:T(8,128)(2,1)} fusion(bf16[512,8,64]{0,2,1:T(8,128)(2,1)} %bitcast.187, bf16[512,8,64]{0,2,1:T(8,128)(2,1)} %bitcast.190, f32[8,64]{1,0:T(8,128)S(1)} %get-tuple-element.152, f32[8,64]{1,0:T(8,128)S(1)} %add_sqrt_fusion, f32[8,64]{1,0:T(8,128)S(1)} %add_sqrt_fusion.1, f32[8]{0:T(128)S(1)} %copy-done.18, ...), kind=kOutput, calls=%fused_computation.30 | convolution fusion | flops 34898496 | bytes 1843232 | tf_op jit(solution)/shard_map/hce,mhc->mhe/dot_general | solution.py:181
  252.3 4.2 %fusion.50 = f32[512,1536]{1,0:T(8,128)} fusion(bf16[512,512]{1,0:T(8,128)(2,1)} %copy-done.14, bf16[512,512]{0,1:T(8,128)(2,1)} %bitcast.266, bf16[512,512]{0,1:T(8,128)(2,1)} %bitcast.270, bf16[512,512]{0,1:T(8,128)(2,1)} %bitcast.268), kind=kOutput, calls=%fused_computation.117 | convolution fusion | flops 810024960 | bytes 5242880 | tf_op jit(solution)/shard_map/md,me->de/dot_general | solution.py:192
  256.6 3.5 fusion.28
  260.2 2.9 collective-permute-start.6
  263.1 1.3 collective-permute-start.7
  264.4 8.2 %collective-permute-done.6 = bf16[1,256,512]{2,1,0:T(8,128)(2,1)S(1)} collective-permute-done((bf16[1,256,512]{2,1,0:T(8,128)(2,1)S(1)}, bf16[1,256,512]{2,1,0:T(8,128)(2,1)S(1)}, u32[]{:S(2)}, u32[]{:S(2)}) %collective-permute-start.6) | collective-permute-done | bytes 262176 | tf_op jit(solution)/shard_map/ppermute | solution.py:26
  272.6 0.2 maximum_convert_fusion.1
  272.7 1.0 multiply_reduce_fusion.9
  273.8 1.0 fusion.29
  274.8 42.4 %all-reduce.38 = (f32[2,3,3,512]{3,2,1,0:T(4,128)S(1)}, f32[2,512]{1,0:T(2,128)}) all-reduce(f32[2,3,3,512]{3,2,1,0:T(4,128)S(1)} %pad_maximum_fusion.3, f32[2,512]{1,0:T(2,128)S(1)} %pad_maximum_fusion.4), channel_id=1, replica_groups=mesh['sp'=8,'rep'=4] {'sp','rep'}, use_global_device_ids=true, to_apply=%region_41.42 | all-reduce | flops 10240 | bytes 81920 | tf_op jit(solution)/shard_map/psum | solution.py:199
  317.2 0.6 copy.29
  317.9 2.7 fusion.87
  320.6 1.2 fusion.41
  321.7 74.8 %all-reduce.49.cloned.1.call-done = (f32[128,1536]{1,0:T(8,128)}, f32[128,512]{1,0:T(8,128)}) async-done(((f32[128,1536]{1,0:T(8,128)}, f32[128,512]{1,0:T(8,128)}), (f32[128,1536]{1,0:T(8,128)}, f32[128,512]{1,0:T(8,128)})) %all-reduce.49.cloned.1.call-update) | async-done | bytes 1048592 | tf_op jit(solution)/shard_map/psum | solution.py:202
  396.5 2.1 copy.49
  398.6 1.7 copy.50
  (83 shorter events, 1.7 us)
Async XLA Ops:
  7.2 12.8 %copy-start = (bf16[512,1536]{1,0:T(8,128)(2,1)S(1)}, bf16[512,1536]{1,0:T(8,128)(2,1)}, u32[]{:S(2)}) copy-start(bf16[512,1536]{1,0:T(8,128)(2,1)} %param.20) | copy-start | bytes 4718596
  7.2 88.8 %all-reduce.45.cloned.1.call-start = ((), (), s32[]{:S(2)}) async-start(), calls=%async_computation.2 | async-start | bytes 524288 | tf_op jit(solution)/shard_map/psum | solution.py:131
  12.4 8.6 %copy-start.2 = (f32[4,258,512]{2,1,0:T(8,128)}, f32[4,258,512]{2,1,0:T(8,128)S(1)}, u32[]{:S(2)}) copy-start(f32[4,258,512]{2,1,0:T(8,128)S(1)} %pad_add_fusion.1) | copy-start | bytes 6340612
  12.4 6.8 %copy-start.1 = (bf16[1,2,256,512]{3,2,1,0:T(8,128)(2,1)S(1)}, bf16[1,2,256,512]{3,2,1,0:T(8,128)(2,1)}, u32[]{:S(2)}) copy-start(bf16[1,2,256,512]{3,2,1,0:T(8,128)(2,1)} %param.17) | copy-start | bytes 1572868
  12.5 7.3 %copy-start.17 = (f32[512]{0:T(512)S(1)}, f32[512]{0:T(512)}, u32[]{:S(2)}) copy-start(f32[512]{0:T(512)} %param.19) | copy-start | bytes 6148
  13.6 114.5 %collective-permute-start = (f32[1,256,512]{2,1,0:T(8,128)}, f32[1,256,512]{2,1,0:T(8,128)}, u32[]{:S(2)}, u32[]{:S(2)}) collective-permute-start(f32[1,256,512]{2,1,0:T(8,128)} %get-tuple-element.97), channel_id=1, source_target_pairs={{0,4},{4,8},{8,12},{12,16},{16,20},{20,24},{24,28},{1,5},{5,9},{9,... | collective-permute-start | bytes 1572872 | tf_op jit(solution)/shard_map/ppermute | solution.py:18
  20.0 1.0 copy-start.14
  21.0 1.5 copy-start.6
  22.8 2.5 copy-start.10
  22.8 73.2 %copy-start.18 = (f32[8]{0:T(128)S(1)}, f32[8]{0:T(128)}, u32[]{:S(2)}) copy-start(f32[8]{0:T(128)} %param.21) | copy-start | bytes 100
  24.2 75.5 %copy-start.11 = (bf16[512,512]{0,1:T(8,128)(2,1)}, bf16[512,512]{0,1:T(8,128)(2,1)S(1)}, u32[]{:S(2)}) copy-start(bf16[512,512]{0,1:T(8,128)(2,1)S(1)} %copy.26) | copy-start | bytes 1572868
  25.2 213.1 %all-reduce.47.cloned.1.call-start = ((), (), s32[]{:S(2)}) async-start(), calls=%async_computation.3 | async-start | bytes 524288 | tf_op jit(solution)/shard_map/psum | solution.py:168
  26.7 76.5 %copy-start.8 = (bf16[512,512]{1,0:T(8,128)(2,1)S(1)}, bf16[512,512]{1,0:T(8,128)(2,1)}, u32[]{:S(2)}) copy-start(bf16[512,512]{1,0:T(8,128)(2,1)} %param.22) | copy-start | bytes 1572868
  103.3 1.2 copy-start.13
  103.3 0.9 copy-start.16
  103.3 5.1 %copy-start.15 = (f32[1,256,512]{2,1,0:T(8,128)S(1)}, f32[1,256,512]{2,1,0:T(8,128)}, u32[]{:S(2)}) copy-start(f32[1,256,512]{2,1,0:T(8,128)} %get-tuple-element.96) | copy-start | bytes 1572868
  103.3 6.5 %copy-start.3 = (f32[4,258,512]{2,1,0:T(8,128)S(1)}, f32[4,258,512]{2,1,0:T(8,128)}, u32[]{:S(2)}) copy-start(f32[4,258,512]{2,1,0:T(8,128)} %copy-done.2) | copy-start | bytes 6340612
  104.5 23.3 %collective-permute-start.2 = (bf16[1,256,512]{2,1,0:T(8,128)(2,1)S(1)}, bf16[1,256,512]{2,1,0:T(8,128)(2,1)S(1)}, u32[]{:S(2)}, u32[]{:S(2)}) collective-permute-start(bf16[1,256,512]{2,1,0:T(8,128)(2,1)S(1)} %get-tuple-element.121), channel_id=1, source_target_pairs={{0,4},{4,8},{8,12},{12,16},{16,20},{20,24},{24,28},{1,5},{5,9},{9,... | collective-permute-start | bytes 786440 | tf_op jit(solution)/shard_map/ppermute | solution.py:26
  107.1 20.7 %collective-permute-start.3 = (bf16[1,256,512]{2,1,0:T(8,128)(2,1)S(1)}, bf16[1,256,512]{2,1,0:T(8,128)(2,1)S(1)}, u32[]{:S(2)}, u32[]{:S(2)}) collective-permute-start(bf16[1,256,512]{2,1,0:T(8,128)(2,1)S(1)} %get-tuple-element.122), channel_id=1, source_target_pairs={{4,0},{8,4},{12,8},{16,12},{20,16},{24,20},{28,24},{5,1},{9,5},{13... | collective-permute-start | bytes 786440 | tf_op jit(solution)/shard_map/ppermute | solution.py:29
  108.4 20.7 %collective-permute-start.1 = (f32[1,256,512]{2,1,0:T(8,128)S(1)}, f32[1,256,512]{2,1,0:T(8,128)S(1)}, u32[]{:S(2)}, u32[]{:S(2)}) collective-permute-start(f32[1,256,512]{2,1,0:T(8,128)S(1)} %copy-done.15), channel_id=1, source_target_pairs={{4,0},{8,4},{12,8},{16,12},{20,16},{24,20},{28,24},{5,1},{9,5},{13... | collective-permute-start | bytes 1572872 | tf_op jit(solution)/shard_map/ppermute | solution.py:18
  135.2 22.3 %collective-permute-start.4 = (f32[1,256,512]{2,1,0:T(8,128)S(1)}, f32[1,256,512]{2,1,0:T(8,128)S(1)}, u32[]{:S(2)}, u32[]{:S(2)}) collective-permute-start(f32[1,256,512]{2,1,0:T(8,128)S(1)} %get-tuple-element.95), channel_id=1, source_target_pairs={{0,4},{4,8},{8,12},{12,16},{16,20},{20,24},{24,28},{1,5},{5,9},{9,... | collective-permute-start | bytes 1572872 | tf_op jit(solution)/shard_map/ppermute | solution.py:18
  139.6 18.0 %collective-permute-start.5 = (f32[1,256,512]{2,1,0:T(8,128)S(1)}, f32[1,256,512]{2,1,0:T(8,128)S(1)}, u32[]{:S(2)}, u32[]{:S(2)}) collective-permute-start(f32[1,256,512]{2,1,0:T(8,128)S(1)} %get-tuple-element.94), channel_id=1, source_target_pairs={{4,0},{8,4},{12,8},{16,12},{20,16},{24,20},{28,24},{5,1},{9,5},{13... | collective-permute-start | bytes 1572872 | tf_op jit(solution)/shard_map/ppermute | solution.py:18
  157.6 1.0 copy-start.4
  158.3 1.1 copy-start.9
  158.7 2.1 copy-start.12
  159.9 0.8 copy-start.7
  161.7 156.1 %reduce-scatter.5.cloned.1.call-start = ((), (), s32[]{:S(2)}) async-start(), calls=%async_computation.5 | async-start | bytes 1310720 | tf_op jit(solution)/shard_map/reduce_scatter | solution.py:205
  164.3 153.6 %reduce-scatter.3.cloned.1.call-start = ((), (), s32[]{:S(2)}) async-start(), calls=%async_computation.4 | async-start | bytes 3932160 | tf_op jit(solution)/shard_map/reduce_scatter | solution.py:204
  256.6 139.9 %all-reduce.49.cloned.1.call-start = ((), (), s32[]{:S(2)}) async-start(), calls=%async_computation.6 | async-start | bytes 2097152 | tf_op jit(solution)/shard_map/psum | solution.py:202
  260.1 12.6 %copy-start.5 = (bf16[1,2,256,512]{3,2,1,0:T(8,128)(2,1)S(1)}, bf16[1,2,256,512]{3,2,1,0:T(8,128)(2,1)}, u32[]{:S(2)}) copy-start(bf16[1,2,256,512]{3,2,1,0:T(8,128)(2,1)} %param.18) | copy-start | bytes 1572868
  260.2 12.4 %collective-permute-start.6 = (bf16[1,256,512]{2,1,0:T(8,128)(2,1)S(1)}, bf16[1,256,512]{2,1,0:T(8,128)(2,1)S(1)}, u32[]{:S(2)}, u32[]{:S(2)}) collective-permute-start(bf16[1,256,512]{2,1,0:T(8,128)(2,1)S(1)} %get-tuple-element.119), channel_id=1, source_target_pairs={{0,4},{4,8},{8,12},{12,16},{16,20},{20,24},{24,28},{1,5},{5,9},{9,... | collective-permute-start | bytes 786440 | tf_op jit(solution)/shard_map/ppermute | solution.py:26
  263.1 9.5 %collective-permute-start.7 = (bf16[1,256,512]{2,1,0:T(8,128)(2,1)S(1)}, bf16[1,256,512]{2,1,0:T(8,128)(2,1)S(1)}, u32[]{:S(2)}, u32[]{:S(2)}) collective-permute-start(bf16[1,256,512]{2,1,0:T(8,128)(2,1)S(1)} %get-tuple-element.120), channel_id=1, source_target_pairs={{4,0},{8,4},{12,8},{16,12},{20,16},{24,20},{28,24},{5,1},{9,5},{13... | collective-permute-start | bytes 786440 | tf_op jit(solution)/shard_map/ppermute | solution.py:29
Sparse Core Ops, SparseCore 0:
  25.4 70.5 all-reduce.44
  161.9 76.4 all-reduce.46
  240.9 24.1 reduce-scatter.4
  267.5 38.0 reduce-scatter.2
  318.0 78.4 all-reduce.48
where the time goes:
time: 408 us; the launch traced here: 407 us
  waiting for transfers between devices  235 us (58%)
  blocking collectives  61.6 us (15%)
  matrix products  31.4 us (8%)
  other arithmetic  29.1 us (7%)
  starting transfers between devices  21.1 us (5%)
  local copies, waits for them, and re-layouts  14.4 us (4%)
  between operations  14.4 us (4%)
    psum x1, waiting for transfers between devices, shards(): summed = lax.psum((grad_qkv, grad_proj), 'sp')  74.8 us
    psum x1, waiting for transfers between devices, shards(): prob_grad = lax.psum(prob_part, 'sp')  69.6 us
    psum x1, waiting for transfers between devices, shards(): lax.psum((gram_part, query_sq, key_sq), 'sp')  47.8 us
    psum x1, blocking collectives, shards(): lax.psum((grad_conv_part, jnp.stack([scale_one, scale_two])), ('sp', 'rep'))  42.4 us
    ppermute x2, waiting for transfers between devices, padded_2(): lax.ppermute(lax.slice_in_dim(block, block.shape[dim] - width, None, axis...  26.1 us
    psum x1, blocking collectives, shards(): lax.psum((gram_part, query_sq, key_sq), 'sp')  19.2 us
    ppermute x4, waiting for transfers between devices, shifted_2(): lax.ppermute(value, axis, [(source, source + steps) for source in range(l...  16.3 us
    ppermute x4, starting transfers between devices, shifted_2(): lax.ppermute(value, axis, [(source, source + steps) for source in range(l...  12.9 us
  transfers between devices with their start and end apart: 13, of which 6 were waited for; matrix products, arithmetic and copies ran while one was open for 13% of the time, Pallas kernels for 0%

commit v1 on v0

v1 whole, which is shorter than its diff:
```python
import jax
import jax.numpy as jnp
from jax import lax
from jax.sharding import PartitionSpec as P

EPS = 1e-06
F32 = jnp.float32
BF16 = jnp.bfloat16


def swap_bit(value, axis, bit):
    count = lax.axis_size(axis)
    return lax.ppermute(value, axis, [(i, i ^ bit) for i in range(count)])


def bits_of(axis):
    count = lax.axis_size(axis)
    bits = []
    bit = 1
    while bit < count:
        bits.append(bit)
        bit *= 2
    return bits


def all_sum(value, axis):
    for bit in bits_of(axis):
        value = value + swap_bit(value, axis, bit)
    return value


def own_bit(axis, bit):
    return (lax.axis_index(axis) // bit) % 2


def halve(value, axis, bit, dim):
    mine = own_bit(axis, bit)
    keep = lax.dynamic_index_in_dim(value, mine, dim, False)
    give = lax.dynamic_index_in_dim(value, 1 - mine, dim, False)
    got = swap_bit(give, axis, bit)
    return (keep.astype(F32) + got.astype(F32)).astype(BF16)


def reduce_rows(part):
    rows, cols = part.shape
    rep_bits = bits_of("rep")
    value = part.astype(BF16).reshape((2,) * len(rep_bits) + (-1, cols))
    for bit in rep_bits:
        depth = value.ndim - 3
        value = halve(value, "rep", bit, depth)
    for bit in bits_of("sp"):
        value = halve(value.reshape(2, -1, cols), "sp", bit, 0)
    for bit in reversed(bits_of("sp")):
        other = swap_bit(value, "sp", bit)
        mine = own_bit("sp", bit)
        value = jnp.where(
            mine == 0, jnp.concatenate([value, other]), jnp.concatenate([other, value])
        )
    return value.astype(F32)


def neighbours(value):
    count = lax.axis_size("sp")
    beside = swap_bit(value, "sp", 1)
    hops = [(i, i - 2) for i in range(count) if i % 2 == 1 and i >= 2]
    hops += [(i, i + 2) for i in range(count) if i % 2 == 0 and i + 2 < count]
    beyond = lax.ppermute(beside, "sp", hops)
    even = lax.axis_index("sp") % 2 == 0
    return jnp.where(even, beyond, beside), jnp.where(even, beside, beyond)


def norm_stats(values):
    centred = values - jnp.mean(values, -1, keepdims=True)
    inverse = lax.rsqrt(jnp.mean(centred * centred, -1, keepdims=True) + EPS)
    return centred * inverse, inverse


def norm_back(upstream, gain_vec, normed, inverse):
    scaled = upstream * gain_vec
    return inverse * (
        scaled
        - jnp.mean(scaled, -1, keepdims=True)
        - normed * jnp.mean(scaled * normed, -1, keepdims=True)
    )


def heads_of(rows, heads):
    return rows.reshape(rows.shape[0], heads, -1)


def shift_cols(field, step):
    if step == 0:
        return field
    zeros = jnp.zeros_like(field[:, :1])
    if step > 0:
        return jnp.concatenate([field[:, 1:], zeros], 1)
    return jnp.concatenate([zeros, field[:, :-1]], 1)


def dot32(a, b, dims):
    return lax.dot_general(a, b, (dims, ((), ())), preferred_element_type=F32)


def shards(x4, up4, gain_one, w_qkv, sharp, w_out, factors, gain_two, kernels):
    row_count, width, dim = x4.shape[1:]
    heads = sharp.shape[0]
    tokens = row_count * width
    x_own, up_own = x4[0], up4[0]
    x_above, x_below = neighbours(x_own)
    up_above, up_below = neighbours(up_own)

    flat = x_own.reshape(tokens, dim).astype(F32)
    normed_one, inverse_one = norm_stats(flat)
    act_one = (normed_one * gain_one).astype(BF16)
    mixed = dot32(act_one, w_qkv, ((1,), (0,))).astype(BF16)
    query, key, value = (mixed[:, i * dim : (i + 1) * dim] for i in range(3))
    query_f, key_f = query.astype(F32), key.astype(F32)
    gram = jnp.einsum(
        "mhc,mhe->che", heads_of(query, heads), heads_of(key, heads), preferred_element_type=F32
    ).reshape(-1, dim)
    pack = jnp.concatenate(
        [gram, jnp.sum(query_f * query_f, 0)[None], jnp.sum(key_f * key_f, 0)[None]]
    )
    pack = all_sum(pack, "sp")
    head_dim = dim // heads
    gram = pack[:head_dim].reshape(head_dim, heads, head_dim).transpose(1, 0, 2)
    query_norm = jnp.sqrt(pack[head_dim] + EPS).reshape(heads, head_dim)
    key_norm = jnp.sqrt(pack[head_dim + 1] + EPS).reshape(heads, head_dim)
    divisor = query_norm[:, :, None] * key_norm[:, None, :]
    scores = sharp[:, None, None] * gram / divisor
    prob = jax.nn.softmax(scores, -1)
    prob_low = prob.astype(BF16)

    def token_part(value_rows, flat_rows):
        attended = jnp.einsum(
            "hce,mhe->mhc", prob_low, heads_of(value_rows, heads), preferred_element_type=F32
        ).reshape(-1, dim).astype(BF16)
        projected = dot32(attended, w_out, ((1,), (0,)))
        residual = (flat_rows + factors[0] * projected).astype(BF16).astype(F32)
        normed, inverse = norm_stats(residual)
        act_two = (normed * gain_two).astype(BF16)
        return attended, projected, normed, inverse, act_two

    def edge_part(x_rows):
        flat_rows = x_rows.reshape(-1, dim).astype(F32)
        act = (norm_stats(flat_rows)[0] * gain_one).astype(BF16)
        value_rows = dot32(act, w_qkv[:, 2 * dim :], ((1,), (0,))).astype(BF16)
        return token_part(value_rows, flat_rows)[4].reshape(-1, width, dim)

    attended, projected, normed_two, inverse_two, act_two = token_part(value, flat)
    act_ext = jnp.concatenate(
        [edge_part(x_above[-2:]), act_two.reshape(row_count, width, dim), edge_part(x_below[:2])]
    ).astype(F32)
    up_ext = jnp.concatenate([up_above[-2:], up_own, up_below[:2]]).astype(F32)
    up_two = up_ext * factors[1]
    mid = row_count + 2

    def conv(field, kernel, flip):
        total = 0.0
        for j in range(3):
            column = 0.0
            for i in range(3):
                row = 2 - i if flip else i
                column = column + field[row : row + field.shape[0] - 2] * kernel[i, j]
            total = total + shift_cols(column, 1 - j if flip else j - 1)
        return total

    h_one = conv(act_ext, kernels[0], False)
    d_hidden = conv(up_two, kernels[1], True)
    cumul = 0.5 * (1.0 + lax.erf(h_one * 0.7071067811865476))
    density = jnp.exp(-0.5 * h_one * h_one) * 0.3989422804014327
    d_h = d_hidden * (cumul + h_one * density)
    index = lax.axis_index("sp")
    keep_top = (index > 0).astype(F32)
    keep_bottom = (index < lax.axis_size("sp") - 1).astype(F32)
    keep = jnp.concatenate([keep_top[None], jnp.ones((row_count,), F32), keep_bottom[None]])
    d_h = jnp.where(keep[:, None, None] > 0, d_h, 0.0)
    hidden = (h_one * cumul)[1:-1].astype(BF16).astype(F32)
    d_act = conv(d_h, kernels[0], True).reshape(tokens, dim)
    d_h_own = d_h[1:-1]
    conv_one, conv_two = [], []
    for i in range(3):
        for j in range(3):
            conv_one.append(
                jnp.sum(shift_cols(d_h_own, 1 - j) * act_ext[1 + i : 1 + i + row_count], (0, 1))
            )
            conv_two.append(
                jnp.sum(shift_cols(hidden, j - 1) * up_ext[3 - i : 3 - i + row_count], (0, 1))
            )
    conv_one = jnp.stack(conv_one)
    conv_raw = jnp.stack(conv_two)
    scale_two = jnp.sum(kernels[1].reshape(9, dim) * conv_raw, 0)
    d_res = up_own.reshape(tokens, dim).astype(F32) + norm_back(
        d_act, gain_two, normed_two, inverse_two
    )
    scale_one = jnp.sum(projected * d_res, 0)
    d_proj = (factors[0] * d_res).astype(BF16)
    grad_proj = dot32(attended, d_proj, ((0,), (0,)))
    d_att = dot32(d_proj, w_out, ((1,), (1,))).astype(BF16)
    prob_part = jnp.einsum(
        "mhc,mhe->che", heads_of(d_att, heads), heads_of(value, heads), preferred_element_type=F32
    ).reshape(-1, dim)
    d_value = jnp.einsum(
        "hce,mhc->mhe", prob_low, heads_of(d_att, heads), preferred_element_type=F32
    ).reshape(tokens, dim).astype(BF16)
    grad_v = dot32(act_one, d_value, ((0,), (0,)))
    small = jnp.concatenate(
        [conv_one, conv_raw * factors[1], scale_one[None], scale_two[None]]
    )
    pack = all_sum(jnp.concatenate([prob_part, small]), "sp")
    early = reduce_rows(jnp.concatenate([grad_v, grad_proj], 1))
    small = all_sum(pack[head_dim:], "rep")
    prob_grad = pack[:head_dim].reshape(head_dim, heads, head_dim).transpose(1, 0, 2)
    d_scores = prob * (prob_grad - jnp.sum(prob * prob_grad, -1, keepdims=True))
    d_gram = (d_scores * sharp[:, None, None] / divisor).astype(BF16)
    weighted = d_scores * scores
    d_qsq = -jnp.sum(weighted, -1) / (2.0 * query_norm * query_norm)
    d_ksq = -jnp.sum(weighted, 1) / (2.0 * key_norm * key_norm)
    d_query = (
        jnp.einsum("hce,mhe->mhc", d_gram, heads_of(key, heads), preferred_element_type=F32)
        .reshape(tokens, dim) + 2.0 * d_qsq.reshape(dim) * query_f
    )
    d_key = (
        jnp.einsum("hce,mhc->mhe", d_gram, heads_of(query, heads), preferred_element_type=F32)
        .reshape(tokens, dim) + 2.0 * d_ksq.reshape(dim) * key_f
    )
    d_qk = jnp.concatenate([d_query, d_key], -1).astype(BF16)
    late = reduce_rows(dot32(act_one, d_qk, ((0,), (0,))))
    d_act_one = dot32(d_qk, w_qkv[:, : 2 * dim], ((1,), (1,))) + dot32(
        d_value, w_qkv[:, 2 * dim :], ((1,), (1,))
    )
    grad_input = (d_res + norm_back(d_act_one, gain_one, normed_one, inverse_one)).astype(BF16)
    return (
        grad_input.reshape(1, row_count, width, dim),
        jnp.concatenate([late, early[:, :dim]], 1),
        early[:, dim:],
        small[:18].reshape(2, 3, 3, dim),
        small[18:20],
    )


def solution(mesh):
    rows = P("rep", "sp", None, None)
    return jax.shard_map(
        shards,
        mesh=mesh,
        in_specs=(rows, rows) + (P(),) * 7,
        out_specs=(rows, P("rep", None), P("rep", None), P(), P()),
        check_vma=False,
    )
```

time: 408 us -> 198 us (0.49)
  waiting for transfers between devices: 235 us -> 51.8 us
  blocking collectives: 61.6 us -> 0 us
  starting transfers between devices: 21.1 us -> 46.4 us
  local copies, waits for them, and re-layouts: 14.4 us -> 36.7 us
  between operations: 14.4 us -> 2.09 us
  matrix products: 31.4 us -> 19.4 us
  other arithmetic: 29.1 us -> 40.5 us
    psum x3 -> x0, waiting for transfers between devices: 192 us -> none  [the longest x1 74.8 us: shards(): summed = lax.psum((grad_qkv, grad_proj), 'sp')]
    psum x2 -> x0, blocking collectives: 61.6 us -> none  [the longest x1 42.4 us: shards(): lax.psum((grad_conv_part, jnp.stack([scale_one, scale_two])), ('sp', 'rep'))]
    ppermute x8 -> x28, starting transfers between devices: 20.9 us -> 46.4 us  [the longest x26 37.8 us: swap_bit(): return lax.ppermute(value, axis, [(i, i ^ bit) for i in range(count)])]
    dot_general x12 -> x20, matrix products: 31.4 us -> 19.4 us  [the longest x12 9.84 us: dot32(): return lax.dot_general(a, b, (dims, ((), ())), preferred_element_type=F32)]
    ppermute x8 -> x28, waiting for transfers between devices: 42.3 us -> 51.8 us  [the longest x26 51.8 us: swap_bit(): return lax.ppermute(value, axis, [(i, i ^ bit) for i in range(count)])]
    slice x14 -> x18, local copies, waits for them, and re-layouts: 8.23 us -> 15.5 us  [the longest x4 6.77 us: shards(): query, key, value = (mixed[:, i * dim:(i + 1) * dim] for i in range(3))]
    add x0 -> x11, other arithmetic: none -> 6.88 us  [the longest x3 6.72 us: conv(): column = column + field[row:row + field.shape[0] - 2] * kernel[i, j]]
    reshape x0 -> x7, local copies, waits for them, and re-layouts: none -> 6.29 us  [the longest x1 2.55 us: shards(): d_query = jnp.einsum('hce,mhe->mhc', d_gram, heads_of(key, heads), prefer...]
  transfers between devices with their start and end apart: 13 -> 28, of which waited for: 6 -> 18; matrix products, arithmetic and copies ran while one was open for 13% -> 28% of each run, Pallas kernels for 0% -> 0%
where the time goes in v1:
time: 198 us; the launch traced here: 197 us
  waiting for transfers between devices  51.8 us (26%)
  starting transfers between devices  46.4 us (23%)
  other arithmetic  40.5 us (20%)
  local copies, waits for them, and re-layouts  36.7 us (19%)
  matrix products  19.4 us (10%)
  between operations  2.09 us (1%)
    ppermute x26, waiting for transfers between devices, swap_bit(): return lax.ppermute(value, axis, [(i, i ^ bit) for i in range(count)])  51.8 us
    ppermute x26, starting transfers between devices, swap_bit(): return lax.ppermute(value, axis, [(i, i ^ bit) for i in range(count)])  37.8 us
    dot_general x12, matrix products, dot32(): return lax.dot_general(a, b, (dims, ((), ())), preferred_element_type=F32)  9.84 us
    unnamed x137, local copies, waits for them, and re-layouts  9.01 us
    ppermute x2, starting transfers between devices, neighbours(): beyond = lax.ppermute(beside, 'sp', hops)  8.55 us
    slice x4, local copies, waits for them, and re-layouts, shards(): query, key, value = (mixed[:, i * dim:(i + 1) * dim] for i in range(3))  6.77 us
    add x3, other arithmetic, conv(): column = column + field[row:row + field.shape[0] - 2] * kernel[i, j]  6.72 us
    slice x5, local copies, waits for them, and re-layouts, conv(): column = column + field[row:row + field.shape[0] - 2] * kernel[i, j]  4.79 us
  transfers between devices with their start and end apart: 28, of which 18 were waited for; matrix products, arithmetic and copies ran while one was open for 28% of the time, Pallas kernels for 0%

profile of v1, /device:TPU:0, one launch (start us, length us, event | category | flops | bytes accessed | tf_op | source)
XLA Modules:
  0.0 196.9 jit_solution(14400267695845081186)
XLA Ops:
  0.7 3.0 %collective-permute-start.5 = (bf16[2,256,512]{2,1,0:T(8,128)(2,1)}, bf16[2,256,512]{2,1,0:T(8,128)(2,1)S(1)}, u32[]{:S(2)}, u32[]{:S(2)}) collective-permute-start(bf16[2,256,512]{2,1,0:T(8,128)(2,1)} %bitcast.284), channel_id=1, source_target_pairs={{0,4},{4,0},{8,12},{12,8},{16,20},{20,16},{24,28},{28,24},{1,5},{5... | collective-permute-start | bytes 1572872 | tf_op jit(solution)/shard_map/ppermute | solution.py:13
  5.0 1.3 fusion.67
  6.5 1.5 fusion.143
  8.0 1.3 fusion.69
  10.3 6.4 %collective-permute-done.5 = bf16[2,256,512]{2,1,0:T(8,128)(2,1)S(1)} collective-permute-done((bf16[2,256,512]{2,1,0:T(8,128)(2,1)}, bf16[2,256,512]{2,1,0:T(8,128)(2,1)S(1)}, u32[]{:S(2)}, u32[]{:S(2)}) %collective-permute-start.5) | collective-permute-done | bytes 524320 | tf_op jit(solution)/shard_map/ppermute | solution.py:13
  16.7 4.0 %collective-permute-start.6 = (bf16[2,256,512]{2,1,0:T(8,128)(2,1)S(1)}, bf16[2,256,512]{2,1,0:T(8,128)(2,1)S(1)}, u32[]{:S(2)}, u32[]{:S(2)}) collective-permute-start(bf16[2,256,512]{2,1,0:T(8,128)(2,1)S(1)} %collective-permute-done.5), channel_id=1, source_target_pairs={{12,4},{20,12},{28,20},{0,8},{8,16},{16,24},{13,5},{21,13},{29,21}... | collective-permute-start | bytes 1572872 | tf_op jit(solution)/shard_map/ppermute | solution.py:67
  22.5 4.6 %collective-permute-done.3 = bf16[2,256,512]{2,1,0:T(8,128)(2,1)} collective-permute-done((bf16[2,256,512]{2,1,0:T(8,128)(2,1)}, bf16[2,256,512]{2,1,0:T(8,128)(2,1)}, u32[]{:S(2)}, u32[]{:S(2)}) %collective-permute-start.3) | collective-permute-done | bytes 524320 | tf_op jit(solution)/shard_map/ppermute | solution.py:13
  27.2 4.5 %collective-permute-start.4 = (bf16[2,256,512]{2,1,0:T(8,128)(2,1)}, bf16[2,256,512]{2,1,0:T(8,128)(2,1)}, u32[]{:S(2)}, u32[]{:S(2)}) collective-permute-start(bf16[2,256,512]{2,1,0:T(8,128)(2,1)} %collective-permute-done.3), channel_id=1, source_target_pairs={{12,4},{20,12},{28,20},{0,8},{8,16},{16,24},{13,5},{21,13},{29,21}... | collective-permute-start | bytes 1572872 | tf_op jit(solution)/shard_map/ppermute | solution.py:67
  32.9 1.5 fusion.64
  35.4 1.2 fusion.140
  36.6 1.3 copy.32
  37.9 2.2 %copy.33 = bf16[512,512]{0,1:T(8,128)(2,1)} copy(bf16[512,512]{1,0:T(8,128)(2,1)} %get-tuple-element.81) | data formatting | bytes 1048576 | tf_op jit(solution)/shard_map/slice | solution.py:116
  40.1 1.3 fusion.148
  43.1 2.1 %copy.31 = bf16[512,512]{0,1:T(8,128)(2,1)} copy(bf16[512,512]{1,0:T(8,128)(2,1)} %get-tuple-element.83) | data formatting | bytes 1048576 | tf_op jit(solution)/shard_map/slice | solution.py:116
  45.2 1.3 broadcast_select_fusion.3
  46.8 2.9 %fusion.136 = (f32[4,256,512]{2,1,0:T(8,128)S(1)}, f32[4,256,512]{2,1,0:T(8,128)}, f32[4,256,512]{2,1,0:T(8,128)}) fusion(f32[6,256,512]{2,1,0:T(8,128)S(1)} %broadcast_multiply_fusion), kind=kLoop, calls=%fused_computation.274 | loop fusion | bytes 12582912 | tf_op jit(solution)/shard_map/slice | solution.py:164
  50.1 1.3 convolution_convert_fusion.7
  51.4 1.6 collective-permute-start.1
  53.1 1.3 convolution_convert_fusion.9
  54.4 2.3 %collective-permute-done.1 = f32[66,512]{1,0:T(8,128)S(1)} collective-permute-done((f32[66,512]{1,0:T(8,128)S(1)}, f32[66,512]{1,0:T(8,128)S(1)}, u32[]{:S(2)}, u32[]{:S(2)}) %collective-permute-start.1) | collective-permute-done | bytes 135200 | tf_op jit(solution)/shard_map/ppermute | solution.py:13
  56.7 3.1 %collective-permute-start.2 = (f32[66,512]{1,0:T(8,128)S(1)}, f32[66,512]{1,0:T(8,128)S(1)}, u32[]{:S(2)}, u32[]{:S(2)}) collective-permute-start(f32[66,512]{1,0:T(8,128)S(1)} %add.339), channel_id=1, source_target_pairs={{0,16},{4,20},{8,24},{12,28},{16,0},{20,4},{24,8},{28,12},{1,17},{... | collective-permute-start | bytes 405512 | tf_op jit(solution)/shard_map/ppermute | solution.py:13
  59.7 1.9 maximum_convert_fusion
  61.7 2.8 %collective-permute-done.2 = f32[66,512]{1,0:T(8,128)S(1)} collective-permute-done((f32[66,512]{1,0:T(8,128)S(1)}, f32[66,512]{1,0:T(8,128)S(1)}, u32[]{:S(2)}, u32[]{:S(2)}) %collective-permute-start.2) | collective-permute-done | bytes 135200 | tf_op jit(solution)/shard_map/ppermute | solution.py:13
  67.4 1.9 fusion.147
  70.0 1.4 convolution_convert_fusion.6
  72.8 1.5 convert_reduce_fusion.2
  78.8 1.5 add_multiply_fusion
  81.6 1.3 copy-done.10
  84.5 5.0 %fusion.14 = (f32[4,255,512]{2,1,0:T(8,128)S(1)}, f32[4,255,512]{2,1,0:T(8,128)S(1)}) fusion(f32[4,256,512]{2,1,0:T(8,128)} %get-tuple-element.67, f32[4,256,512]{2,1,0:T(8,128)} %get-tuple-element.68, f32[4,256,512]{2,1,0:T(8,128)S(1)} %get-tuple-element.66, f32[512]{0:T(512)S(1)} %bitcast.389, f32[512]{0:T(512)S(1)} %bitcast.390, f32[512]{0:T(512)S(1)} %bitcast.391, ...), kind=kLoop, calls=%fused_computation.26 | loop fusion | flops 5222400 | bytes 16723968 | tf_op jit(solution)/shard_map/add | solution.py:164
  89.6 1.9 fusion.7
  93.7 1.3 copy-done.2
  95.1 1.9 multiply_reduce_fusion.10
  100.5 3.0 %concatenate.134 = f32[84,512]{1,0:T(8,128)S(1)} concatenate(f32[64,512]{1,0:T(8,128)S(1)} %copy.40, f32[1,512]{1,0:T(1,128)} %bitcast.382, f32[1,512]{1,0:T(1,128)} %bitcast.380, f32[1,512]{1,0:T(1,128)} %bitcast.377, f32[1,512]{1,0:T(1,128)} %bitcast.383, f32[1,512]{1,0:T(1,128)} %bitcast.379, f32[1,512]{1,0:T(1,128)} %bitcast.378, f32[1,512]{1,0:T(1,128)} %bitcast.384, ...), dimensions={0} | concatenate | bytes 344064 | tf_op jit(solution)/shard_map/concatenate | solution.py:210
  103.5 1.4 collective-permute-start.7
  105.4 3.7 %collective-permute-done.7 = f32[84,512]{1,0:T(8,128)S(1)} collective-permute-done((f32[84,512]{1,0:T(8,128)S(1)}, f32[84,512]{1,0:T(8,128)S(1)}, u32[]{:S(2)}, u32[]{:S(2)}) %collective-permute-start.7) | collective-permute-done | bytes 172064 | tf_op jit(solution)/shard_map/ppermute | solution.py:13
  109.9 5.5 %collective-permute-done.8 = f32[84,512]{1,0:T(8,128)S(1)} collective-permute-done((f32[84,512]{1,0:T(8,128)S(1)}, f32[84,512]{1,0:T(8,128)S(1)}, u32[]{:S(2)}, u32[]{:S(2)}) %collective-permute-start.8) | collective-permute-done | bytes 172064 | tf_op jit(solution)/shard_map/ppermute | solution.py:13
  115.4 2.3 %collective-permute-start.9 = (f32[84,512]{1,0:T(8,128)S(1)}, f32[84,512]{1,0:T(8,128)S(1)}, u32[]{:S(2)}, u32[]{:S(2)}) collective-permute-start(f32[84,512]{1,0:T(8,128)S(1)} %add.381), channel_id=1, source_target_pairs={{0,16},{4,20},{8,24},{12,28},{16,0},{20,4},{24,8},{28,12},{1,17},{... | collective-permute-start | bytes 516104 | tf_op jit(solution)/shard_map/ppermute | solution.py:13
  119.9 3.9 %collective-permute-done.9 = f32[84,512]{1,0:T(8,128)S(1)} collective-permute-done((f32[84,512]{1,0:T(8,128)S(1)}, f32[84,512]{1,0:T(8,128)S(1)}, u32[]{:S(2)}, u32[]{:S(2)}) %collective-permute-start.9) | collective-permute-done | bytes 172064 | tf_op jit(solution)/shard_map/ppermute | solution.py:13
  124.7 2.7 %fusion.120 = f32[8,512,64]{1,2,0:T(8,128)} fusion(bf16[512,8,64]{0,2,1:T(8,128)(2,1)} %bitcast.302, f32[8]{0:T(128)S(1)} %copy-done.63, f32[8,64]{1,0:T(8,128)S(1)} %copy-done.60, f32[8,64]{1,0:T(8,128)S(1)} %copy-done.58, f32[8,64,64]{1,2,0:T(8,128)} %bitcast.332, f32[8,64,64]{1,2,0:T(8,128)} %copy-done.37, f32[8,64]{1,0:T(8,128)S(1)} %copy-done.56), kind=kOutput, calls=%fused_computation.270 | convolution fusion | flops 33849920 | bytes 1841184 | tf_op jit(solution)/shard_map/hce,mhc->mhe/dot_general | solution.py:224
  127.4 1.5 multiply_reduce_fusion.24
  129.0 2.9 %fusion.122 = f32[8,512,64]{1,2,0:T(8,128)} fusion(bf16[512,8,64]{0,2,1:T(8,128)(2,1)} %bitcast.300, f32[8]{0:T(128)S(1)} %copy-done.63, f32[8,64]{1,0:T(8,128)S(1)} %copy-done.60, f32[8,64]{1,0:T(8,128)S(1)} %copy-done.58, f32[8,64,64]{1,2,0:T(8,128)} %bitcast.334, f32[8,64,64]{1,2,0:T(8,128)} %copy-done.37, f32[8,64]{1,0:T(8,128)S(1)} %copy-done.56), kind=kOutput, calls=%fused_computation.271 | convolution fusion | flops 33849920 | bytes 1841184 | tf_op jit(solution)/shard_map/hce,mhe->mhc/dot_general | solution.py:220
  131.8 2.5 %copy.44 = f32[512,512]{1,0:T(8,128)} copy(f32[512,512]{0,1:T(8,128)} %bitcast.310) | data formatting | bytes 2097152 | tf_op jit(solution)/shard_map/reshape | solution.py:225
  134.6 2.5 %copy.43 = f32[512,512]{1,0:T(8,128)} copy(f32[512,512]{0,1:T(8,128)} %bitcast.309) | data formatting | bytes 2097152 | tf_op jit(solution)/shard_map/reshape | solution.py:221
  137.9 2.3 %fusion.48 = (bf16[512,512]{1,0:T(8,128)(2,1)S(1)}, bf16[512,512]{1,0:T(8,128)(2,1)S(1)}) fusion(f32[512,512]{1,0:T(8,128)} %copy.43, f32[512]{0:T(512)S(1)} %bitcast.374, bf16[512,1536]{1,0:T(8,128)(2,1)} %copy-done.11, f32[512,512]{1,0:T(8,128)} %copy.44, f32[512]{0:T(512)S(1)} %bitcast.375), kind=kLoop, calls=%fused_computation.94 | loop fusion | flops 2097152 | bytes 4198400 | tf_op jit(solution)/shard_map/convert.18
  143.4 1.2 fusion.57
  144.7 1.6 collective-permute-start.19
  146.3 7.2 %collective-permute-done.19 = bf16[128,1024]{1,0:T(8,128)(2,1)S(1)} collective-permute-done((bf16[128,1024]{1,0:T(8,128)(2,1)S(1)}, bf16[128,1024]{1,0:T(8,128)(2,1)S(1)}, u32[]{:S(2)}, u32[]{:S(2)}) %collective-permute-start.19) | collective-permute-done | bytes 262176 | tf_op jit(solution)/shard_map/ppermute | solution.py:13
  153.5 1.9 collective-permute-start.20
  155.5 1.6 collective-permute-start.27
  157.1 1.7 collective-permute-done.20
  159.4 1.6 collective-permute-start.11
  161.0 2.2 %collective-permute-done.21 = bf16[32,1024]{1,0:T(8,128)(2,1)S(1)} collective-permute-done((bf16[32,1024]{1,0:T(8,128)(2,1)S(1)}, bf16[32,1024]{1,0:T(8,128)(2,1)S(1)}, u32[]{:S(2)}, u32[]{:S(2)}) %collective-permute-start.21) | collective-permute-done | bytes 65568 | tf_op jit(solution)/shard_map/ppermute | solution.py:13
  163.2 1.6 collective-permute-start.22
  164.9 1.5 collective-permute-done.11
  166.5 1.7 collective-permute-start.12
  168.5 1.9 collective-permute-start.23
  171.6 1.8 collective-permute-start.13
  173.5 1.7 collective-permute-start.24
  176.3 2.9 %collective-permute-start.14 = (bf16[16,1024]{1,0:T(8,128)(2,1)S(1)}, bf16[16,1024]{1,0:T(8,128)(2,1)S(1)}, u32[]{:S(2)}, u32[]{:S(2)}) collective-permute-start(bf16[16,1024]{1,0:T(8,128)(2,1)S(1)} %dynamic-slice_bitcast_fusion.8), channel_id=1, source_target_pairs={{0,16},{4,20},{8,24},{12,28},{16,0},{20,4},{24,8},{28,12},{1,17},{... | collective-permute-start | bytes 98312 | tf_op jit(solution)/shard_map/ppermute | solution.py:13
  179.9 1.3 collective-permute-done.14
  181.2 2.9 %collective-permute-start.15 = (bf16[16,1024]{1,0:T(8,128)(2,1)S(1)}, bf16[16,1024]{1,0:T(8,128)(2,1)S(1)}, u32[]{:S(2)}, u32[]{:S(2)}) collective-permute-start(bf16[16,1024]{1,0:T(8,128)(2,1)S(1)} %fusion.102), channel_id=1, source_target_pairs={{0,16},{4,20},{8,24},{12,28},{16,0},{20,4},{24,8},{28,12},{1,17},{... | collective-permute-start | bytes 98312 | tf_op jit(solution)/shard_map/ppermute | solution.py:13
  187.7 3.1 %collective-permute-done.16 = bf16[32,1024]{1,0:T(8,128)(2,1)S(1)} collective-permute-done((bf16[32,1024]{1,0:T(8,128)(2,1)S(1)}, bf16[32,1024]{1,0:T(8,128)(2,1)S(1)}, u32[]{:S(2)}, u32[]{:S(2)}) %collective-permute-start.16) | collective-permute-done | bytes 65568 | tf_op jit(solution)/shard_map/ppermute | solution.py:13
  190.9 1.2 collective-permute-start.17
  192.9 3.1 %collective-permute-done.17 = bf16[64,1024]{1,0:T(8,128)(2,1)S(1)} collective-permute-done((bf16[64,1024]{1,0:T(8,128)(2,1)S(1)}, bf16[64,1024]{1,0:T(8,128)(2,1)S(1)}, u32[]{:S(2)}, u32[]{:S(2)}) %collective-permute-start.17) | collective-permute-done | bytes 131104 | tf_op jit(solution)/shard_map/ppermute | solution.py:13
  (272 shorter events, 44.2 us)
Async XLA Ops:
  0.6 70.8 %copy-start = (bf16[512,512]{1,0:T(8,128)(2,1)S(1)}, bf16[512,512]{1,0:T(8,128)(2,1)}, u32[]{:S(2)}) copy-start(bf16[512,512]{1,0:T(8,128)(2,1)} %param.14) | copy-start | bytes 1572868
  0.6 20.7 %copy-start.61 = (f32[2,512]{1,0:T(2,128)S(1)}, f32[2,512]{1,0:T(2,128)}, u32[]{:S(2)}) copy-start(f32[2,512]{1,0:T(2,128)} %param.15) | copy-start | bytes 12292
  0.7 16.0 %collective-permute-start.5 = (bf16[2,256,512]{2,1,0:T(8,128)(2,1)}, bf16[2,256,512]{2,1,0:T(8,128)(2,1)S(1)}, u32[]{:S(2)}, u32[]{:S(2)}) collective-permute-start(bf16[2,256,512]{2,1,0:T(8,128)(2,1)} %bitcast.284), channel_id=1, source_target_pairs={{0,4},{4,0},{8,12},{12,8},{16,20},{20,16},{24,28},{28,24},{1,5},{5... | collective-permute-start | bytes 1572872 | tf_op jit(solution)/shard_map/ppermute | solution.py:13
  3.7 23.5 %collective-permute-start.3 = (bf16[2,256,512]{2,1,0:T(8,128)(2,1)}, bf16[2,256,512]{2,1,0:T(8,128)(2,1)}, u32[]{:S(2)}, u32[]{:S(2)}) collective-permute-start(bf16[2,256,512]{2,1,0:T(8,128)(2,1)} %bitcast.285), channel_id=1, source_target_pairs={{0,4},{4,0},{8,12},{12,8},{16,20},{20,16},{24,28},{28,24},{1,5},{5... | collective-permute-start | bytes 1572872 | tf_op jit(solution)/shard_map/ppermute | solution.py:13
  9.3 23.6 %copy-start.5 = (bf16[1,2,256,512]{3,2,1,0:T(8,128)(2,1)S(1)}, bf16[1,2,256,512]{3,2,1,0:T(8,128)(2,1)}, u32[]{:S(2)}) copy-start(bf16[1,2,256,512]{3,2,1,0:T(8,128)(2,1)} %param.9) | copy-start | bytes 1572868
  9.3 23.6 %copy-start.53 = (f32[512]{0:T(512)S(1)}, f32[512]{0:T(512)}, u32[]{:S(2)}) copy-start(f32[512]{0:T(512)} %param.11) | copy-start | bytes 6148
  16.7 15.0 %collective-permute-start.6 = (bf16[2,256,512]{2,1,0:T(8,128)(2,1)S(1)}, bf16[2,256,512]{2,1,0:T(8,128)(2,1)S(1)}, u32[]{:S(2)}, u32[]{:S(2)}) collective-permute-start(bf16[2,256,512]{2,1,0:T(8,128)(2,1)S(1)} %collective-permute-done.5), channel_id=1, source_target_pairs={{12,4},{20,12},{28,20},{0,8},{8,16},{16,24},{13,5},{21,13},{29,21}... | collective-permute-start | bytes 1572872 | tf_op jit(solution)/shard_map/ppermute | solution.py:67
  27.2 18.0 %collective-permute-start.4 = (bf16[2,256,512]{2,1,0:T(8,128)(2,1)}, bf16[2,256,512]{2,1,0:T(8,128)(2,1)}, u32[]{:S(2)}, u32[]{:S(2)}) collective-permute-start(bf16[2,256,512]{2,1,0:T(8,128)(2,1)} %collective-permute-done.3), channel_id=1, source_target_pairs={{12,4},{20,12},{28,20},{0,8},{8,16},{16,24},{13,5},{21,13},{29,21}... | collective-permute-start | bytes 1572872 | tf_op jit(solution)/shard_map/ppermute | solution.py:67
  32.2 2.2 %copy-start.23 = (bf16[2,256,512]{2,1,0:T(8,128)(2,1)}, bf16[2,256,512]{2,1,0:T(8,128)(2,1)S(1)}, u32[]{:S(2)}) copy-start(bf16[2,256,512]{2,1,0:T(8,128)(2,1)S(1)} %get-tuple-element.55) | copy-start | bytes 1572868
  32.2 2.2 %copy-start.25 = (bf16[2,256,512]{2,1,0:T(8,128)(2,1)}, bf16[2,256,512]{2,1,0:T(8,128)(2,1)S(1)}, u32[]{:S(2)}) copy-start(bf16[2,256,512]{2,1,0:T(8,128)(2,1)S(1)} %get-tuple-element.87) | copy-start | bytes 1572868
  32.2 2.2 %copy-start.38 = (bf16[512,1536]{1,0:T(8,128)(2,1)S(1)}, bf16[512,1536]{1,0:T(8,128)(2,1)}, u32[]{:S(2)}) copy-start(bf16[512,1536]{1,0:T(8,128)(2,1)} %param.12) | copy-start | bytes 4718596
  35.4 6.2 %copy-start.11 = (bf16[512,1536]{1,0:T(8,128)(2,1)}, bf16[512,1536]{1,0:T(8,128)(2,1)S(1)}, u32[]{:S(2)}) copy-start(bf16[512,1536]{1,0:T(8,128)(2,1)S(1)} %convolution_convert_fusion) | copy-start | bytes 4718596
  37.9 3.6 %copy-start.29 = (bf16[512,512]{0,1:T(8,128)(2,1)}, bf16[512,512]{0,1:T(8,128)(2,1)S(1)}, u32[]{:S(2)}) copy-start(bf16[512,512]{0,1:T(8,128)(2,1)S(1)} %copy.32) | copy-start | bytes 1572868
  41.6 4.8 %copy-start.12 = (bf16[1,2,256,512]{3,2,1,0:T(8,128)(2,1)S(1)}, bf16[1,2,256,512]{3,2,1,0:T(8,128)(2,1)}, u32[]{:S(2)}) copy-start(bf16[1,2,256,512]{3,2,1,0:T(8,128)(2,1)} %param.10) | copy-start | bytes 1572868
  41.6 4.8 %copy-start.51 = (f32[1,512]{1,0:T(1,128)S(1)}, f32[1,512]{1,0:T(1,128)}, u32[]{:S(2)}) copy-start(f32[1,512]{1,0:T(1,128)} %get-tuple-element.116) | copy-start | bytes 6148
  42.5 8.9 %collective-permute-start = (f32[66,512]{1,0:T(8,128)}, f32[66,512]{1,0:T(8,128)S(1)}, u32[]{:S(2)}, u32[]{:S(2)}) collective-permute-start(f32[66,512]{1,0:T(8,128)} %pad_maximum_fusion.4), channel_id=1, source_target_pairs={{0,4},{4,0},{8,12},{12,8},{16,20},{20,16},{24,28},{28,24},{1,5},{5... | collective-permute-start | bytes 405512 | tf_op jit(solution)/shard_map/ppermute | solution.py:13
  46.8 3.3 %copy-start.3 = (f32[6,256,512]{2,1,0:T(8,128)}, f32[6,256,512]{2,1,0:T(8,128)S(1)}, u32[]{:S(2)}) copy-start(f32[6,256,512]{2,1,0:T(8,128)S(1)} %broadcast_multiply_fusion) | copy-start | bytes 9437188
  46.8 3.3 %copy-start.35 = (bf16[512,512]{1,0:T(8,128)(2,1)S(1)}, bf16[512,512]{1,0:T(8,128)(2,1)}, u32[]{:S(2)}) copy-start(bf16[512,512]{1,0:T(8,128)(2,1)} %get-tuple-element.124) | copy-start | bytes 1572868
  46.8 3.3 %copy-start.39 = (bf16[512,1536]{1,0:T(8,128)(2,1)S(1)}, bf16[512,1536]{1,0:T(8,128)(2,1)}, u32[]{:S(2)}) copy-start(bf16[512,1536]{1,0:T(8,128)(2,1)} %param.12) | copy-start | bytes 4718596
  46.8 6.3 %copy-start.34 = (bf16[512,512]{1,0:T(8,128)(2,1)S(1)}, bf16[512,512]{1,0:T(8,128)(2,1)}, u32[]{:S(2)}) copy-start(bf16[512,512]{1,0:T(8,128)(2,1)} %get-tuple-element.123) | copy-start | bytes 1572868
  50.1 9.6 %copy-start.13 = (bf16[1,2,256,512]{3,2,1,0:T(8,128)(2,1)S(1)}, bf16[1,2,256,512]{3,2,1,0:T(8,128)(2,1)}, u32[]{:S(2)}) copy-start(bf16[1,2,256,512]{3,2,1,0:T(8,128)(2,1)} %param.10) | copy-start | bytes 1572868
  51.4 5.2 %collective-permute-start.1 = (f32[66,512]{1,0:T(8,128)S(1)}, f32[66,512]{1,0:T(8,128)S(1)}, u32[]{:S(2)}, u32[]{:S(2)}) collective-permute-start(f32[66,512]{1,0:T(8,128)S(1)} %fusion.118), channel_id=1, source_target_pairs={{0,8},{4,12},{8,0},{12,4},{16,24},{20,28},{24,16},{28,20},{1,9},{5... | collective-permute-start | bytes 405512 | tf_op jit(solution)/shard_map/ppermute | solution.py:13
  56.7 7.8 %collective-permute-start.2 = (f32[66,512]{1,0:T(8,128)S(1)}, f32[66,512]{1,0:T(8,128)S(1)}, u32[]{:S(2)}, u32[]{:S(2)}) collective-permute-start(f32[66,512]{1,0:T(8,128)S(1)} %add.339), channel_id=1, source_target_pairs={{0,16},{4,20},{8,24},{12,28},{16,0},{20,4},{24,8},{28,12},{1,17},{... | collective-permute-start | bytes 405512 | tf_op jit(solution)/shard_map/ppermute | solution.py:13
  65.9 6.2 %copy-start.36 = (f32[64,512]{0,1:T(8,128)}, f32[64,512]{0,1:T(8,128)S(1)}, u32[]{:S(2)}) copy-start(f32[64,512]{0,1:T(8,128)S(1)} %copy.54) | copy-start | bytes 393220
  66.7 2.7 %copy-start.57 = (f32[8,64]{1,0:T(8,128)}, f32[8,64]{1,0:T(8,128)S(1)}, u32[]{:S(2)}) copy-start(f32[8,64]{1,0:T(8,128)S(1)} %sqrt.27) | copy-start | bytes 6148
  67.4 4.0 %copy-start.26 = (bf16[2,256,512]{2,1,0:T(8,128)(2,1)S(1)}, bf16[2,256,512]{2,1,0:T(8,128)(2,1)}, u32[]{:S(2)}) copy-start(bf16[2,256,512]{2,1,0:T(8,128)(2,1)} %copy-done.25) | copy-start | bytes 1572868
  70.0 2.4 %copy-start.19 = (bf16[512,512]{0,1:T(8,128)(2,1)S(1)}, bf16[512,512]{0,1:T(8,128)(2,1)}, u32[]{:S(2)}) copy-start(bf16[512,512]{0,1:T(8,128)(2,1)} %copy.31) | copy-start | bytes 1572868
  72.7 2.2 %copy-start.21 = (bf16[8,512,64]{1,2,0:T(8,128)(2,1)}, bf16[8,512,64]{1,2,0:T(8,128)(2,1)S(1)}, u32[]{:S(2)}) copy-start(bf16[8,512,64]{1,2,0:T(8,128)(2,1)S(1)} %convolution_convert_fusion.10) | copy-start | bytes 1572868
  72.8 2.2 %copy-start.24 = (bf16[2,256,512]{2,1,0:T(8,128)(2,1)S(1)}, bf16[2,256,512]{2,1,0:T(8,128)(2,1)}, u32[]{:S(2)}) copy-start(bf16[2,256,512]{2,1,0:T(8,128)(2,1)} %copy-done.23) | copy-start | bytes 1572868
  76.7 2.1 %copy-start.1 = (f32[6,256,512]{2,1,0:T(8,128)}, f32[6,256,512]{2,1,0:T(8,128)S(1)}, u32[]{:S(2)}) copy-start(f32[6,256,512]{2,1,0:T(8,128)S(1)} %maximum_convert_fusion.1) | copy-start | bytes 9437188
  80.6 2.4 %copy-start.10 = (f32[6,256,512]{2,1,0:T(8,128)S(1)}, f32[6,256,512]{2,1,0:T(8,128)}, u32[]{:S(2)}) copy-start(f32[6,256,512]{2,1,0:T(8,128)} %maximum_convert_fusion) | copy-start | bytes 9437188
  84.5 5.1 %copy-start.4 = (f32[6,256,512]{2,1,0:T(8,128)S(1)}, f32[6,256,512]{2,1,0:T(8,128)}, u32[]{:S(2)}) copy-start(f32[6,256,512]{2,1,0:T(8,128)} %copy-done.3) | copy-start | bytes 9437188
  84.5 5.1 %copy-start.9 = (f32[4,256,512]{2,1,0:T(8,128)S(1)}, f32[4,256,512]{2,1,0:T(8,128)}, u32[]{:S(2)}) copy-start(f32[4,256,512]{2,1,0:T(8,128)} %copy-done.8) | copy-start | bytes 6291460
  84.5 5.1 %copy-start.62 = (pred[4]{0:T(512)(128)(4,1)S(1)}, pred[4]{0:T(512)(128)(4,1)}, u32[]{:S(2)}) copy-start(pred[4]{0:T(512)(128)(4,1)} %maximum_compare_fusion) | copy-start | bytes 16
  95.1 2.4 %copy-start.14 = (bf16[1,2,256,512]{3,2,1,0:T(8,128)(2,1)S(1)}, bf16[1,2,256,512]{3,2,1,0:T(8,128)(2,1)}, u32[]{:S(2)}) copy-start(bf16[1,2,256,512]{3,2,1,0:T(8,128)(2,1)} %param.10) | copy-start | bytes 1572868
  98.8 6.1 %copy-start.22 = (bf16[8,512,64]{1,2,0:T(8,128)(2,1)S(1)}, bf16[8,512,64]{1,2,0:T(8,128)(2,1)}, u32[]{:S(2)}) copy-start(bf16[8,512,64]{1,2,0:T(8,128)(2,1)} %copy-done.21) | copy-start | bytes 1572868
  103.5 6.2 %copy-start.18 = (bf16[512,512]{0,1:T(8,128)(2,1)S(1)}, bf16[512,512]{0,1:T(8,128)(2,1)}, u32[]{:S(2)}) copy-start(bf16[512,512]{0,1:T(8,128)(2,1)} %copy-done.17) | copy-start | bytes 1572868
  103.5 5.6 %collective-permute-start.7 = (f32[84,512]{1,0:T(8,128)S(1)}, f32[84,512]{1,0:T(8,128)S(1)}, u32[]{:S(2)}, u32[]{:S(2)}) collective-permute-start(f32[84,512]{1,0:T(8,128)S(1)} %concatenate.134), channel_id=1, source_target_pairs={{0,4},{4,0},{8,12},{12,8},{16,20},{20,16},{24,28},{28,24},{1,5},{5... | collective-permute-start | bytes 516104 | tf_op jit(solution)/shard_map/ppermute | solution.py:13
  104.9 12.8 %copy-start.28 = (bf16[512,512]{1,0:T(8,128)(2,1)S(1)}, bf16[512,512]{1,0:T(8,128)(2,1)}, u32[]{:S(2)}) copy-start(bf16[512,512]{1,0:T(8,128)(2,1)} %copy.45) | copy-start | bytes 1572868
  109.1 6.4 %collective-permute-start.8 = (f32[84,512]{1,0:T(8,128)S(1)}, f32[84,512]{1,0:T(8,128)S(1)}, u32[]{:S(2)}, u32[]{:S(2)}) collective-permute-start(f32[84,512]{1,0:T(8,128)S(1)} %add.380), channel_id=1, source_target_pairs={{0,8},{4,12},{8,0},{12,4},{16,24},{20,28},{24,16},{28,20},{1,9},{5... | collective-permute-start | bytes 516104 | tf_op jit(solution)/shard_map/ppermute | solution.py:13
  115.4 8.4 %collective-permute-start.9 = (f32[84,512]{1,0:T(8,128)S(1)}, f32[84,512]{1,0:T(8,128)S(1)}, u32[]{:S(2)}, u32[]{:S(2)}) collective-permute-start(f32[84,512]{1,0:T(8,128)S(1)} %add.381), channel_id=1, source_target_pairs={{0,16},{4,20},{8,24},{12,28},{16,0},{20,4},{24,8},{28,12},{1,17},{... | collective-permute-start | bytes 516104 | tf_op jit(solution)/shard_map/ppermute | solution.py:13
  117.8 7.0 %copy-start.56 = (f32[8,64]{1,0:T(8,128)S(1)}, f32[8,64]{1,0:T(8,128)}, u32[]{:S(2)}) copy-start(f32[8,64]{1,0:T(8,128)} %copy-done.55) | copy-start | bytes 6148
  117.8 7.0 %copy-start.58 = (f32[8,64]{1,0:T(8,128)S(1)}, f32[8,64]{1,0:T(8,128)}, u32[]{:S(2)}) copy-start(f32[8,64]{1,0:T(8,128)} %copy-done.57) | copy-start | bytes 6148
  117.8 7.0 %copy-start.60 = (f32[8,64]{1,0:T(8,128)S(1)}, f32[8,64]{1,0:T(8,128)}, u32[]{:S(2)}) copy-start(f32[8,64]{1,0:T(8,128)} %copy-done.59) | copy-start | bytes 6148
  117.8 7.0 %copy-start.63 = (f32[8]{0:T(128)S(1)}, f32[8]{0:T(128)}, u32[]{:S(2)}) copy-start(f32[8]{0:T(128)} %param.13) | copy-start | bytes 100
  119.9 23.3 %collective-permute-start.18 = (bf16[2,128,1024]{2,1,0:T(8,128)(2,1)}, bf16[2,128,1024]{2,1,0:T(8,128)(2,1)}, u32[]{:S(2)}, u32[]{:S(2)}) collective-permute-start(bf16[2,128,1024]{2,1,0:T(8,128)(2,1)} %fusion.84), channel_id=1, source_target_pairs={{0,1},{1,0},{2,3},{3,2},{4,5},{5,4},{6,7},{7,6},{8,9},{9,8},{10,11... | collective-permute-start | bytes 1572872 | tf_op jit(solution)/shard_map/ppermute | solution.py:13
  131.8 23.6 %collective-permute-start.26 = (f32[20,512]{1,0:T(8,128)S(1)}, f32[20,512]{1,0:T(8,128)S(1)}, u32[]{:S(2)}, u32[]{:S(2)}) collective-permute-start(f32[20,512]{1,0:T(8,128)S(1)} %slice.373), channel_id=1, source_target_pairs={{0,1},{1,0},{2,3},{3,2},{4,5},{5,4},{6,7},{7,6},{8,9},{9,8},{10,11... | collective-permute-start | bytes 122888 | tf_op jit(solution)/shard_map/ppermute | solution.py:13
  137.9 2.3 %copy-start.33 = (bf16[512,512]{1,0:T(8,128)(2,1)S(1)}, bf16[512,512]{1,0:T(8,128)(2,1)}, u32[]{:S(2)}) copy-start(bf16[512,512]{1,0:T(8,128)(2,1)} %copy-done.32) | copy-start | bytes 1572868
  141.0 18.1 %collective-permute-start.10 = (bf16[2,128,1024]{2,1,0:T(8,128)(2,1)S(1)}, bf16[2,128,1024]{2,1,0:T(8,128)(2,1)S(1)}, u32[]{:S(2)}, u32[]{:S(2)}) collective-permute-start(bf16[2,128,1024]{2,1,0:T(8,128)(2,1)S(1)} %dynamic-slice_bitcast_fusion), channel_id=1, source_target_pairs={{0,1},{1,0},{2,3},{3,2},{4,5},{5,4},{6,7},{7,6},{8,9},{9,8},{10,11... | collective-permute-start | bytes 1572872 | tf_op jit(solution)/shard_map/ppermute | solution.py:13
  144.7 8.8 %collective-permute-start.19 = (bf16[128,1024]{1,0:T(8,128)(2,1)S(1)}, bf16[128,1024]{1,0:T(8,128)(2,1)S(1)}, u32[]{:S(2)}, u32[]{:S(2)}) collective-permute-start(bf16[128,1024]{1,0:T(8,128)(2,1)S(1)} %dynamic-slice_bitcast_fusion.1), channel_id=1, source_target_pairs={{0,2},{1,3},{2,0},{3,1},{4,6},{5,7},{6,4},{7,5},{8,10},{9,11},{10,... | collective-permute-start | bytes 786440 | tf_op jit(solution)/shard_map/ppermute | solution.py:13
  153.5 5.3 %collective-permute-start.20 = (bf16[64,1024]{1,0:T(8,128)(2,1)S(1)}, bf16[64,1024]{1,0:T(8,128)(2,1)S(1)}, u32[]{:S(2)}, u32[]{:S(2)}) collective-permute-start(bf16[64,1024]{1,0:T(8,128)(2,1)S(1)} %dynamic-slice_bitcast_fusion.3), channel_id=1, source_target_pairs={{0,4},{4,0},{8,12},{12,8},{16,20},{20,16},{24,28},{28,24},{1,5},{5... | collective-permute-start | bytes 393224 | tf_op jit(solution)/shard_map/ppermute | solution.py:13
  155.5 29.8 %collective-permute-start.27 = (f32[20,512]{1,0:T(8,128)S(1)}, f32[20,512]{1,0:T(8,128)S(1)}, u32[]{:S(2)}, u32[]{:S(2)}) collective-permute-start(f32[20,512]{1,0:T(8,128)S(1)} %slice_add_fusion.2), channel_id=1, source_target_pairs={{0,2},{1,3},{2,0},{3,1},{4,6},{5,7},{6,4},{7,5},{8,10},{9,11},{10,... | collective-permute-start | bytes 122888 | tf_op jit(solution)/shard_map/ppermute | solution.py:13
  158.9 4.3 %collective-permute-start.21 = (bf16[32,1024]{1,0:T(8,128)(2,1)S(1)}, bf16[32,1024]{1,0:T(8,128)(2,1)S(1)}, u32[]{:S(2)}, u32[]{:S(2)}) collective-permute-start(bf16[32,1024]{1,0:T(8,128)(2,1)S(1)} %dynamic-slice_bitcast_fusion.5), channel_id=1, source_target_pairs={{0,8},{4,12},{8,0},{12,4},{16,24},{20,28},{24,16},{28,20},{1,9},{5... | collective-permute-start | bytes 196616 | tf_op jit(solution)/shard_map/ppermute | solution.py:13
  159.4 7.0 %collective-permute-start.11 = (bf16[128,1024]{1,0:T(8,128)(2,1)S(1)}, bf16[128,1024]{1,0:T(8,128)(2,1)S(1)}, u32[]{:S(2)}, u32[]{:S(2)}) collective-permute-start(bf16[128,1024]{1,0:T(8,128)(2,1)S(1)} %dynamic-slice_bitcast_fusion.2), channel_id=1, source_target_pairs={{0,2},{1,3},{2,0},{3,1},{4,6},{5,7},{6,4},{7,5},{8,10},{9,11},{10,... | collective-permute-start | bytes 786440 | tf_op jit(solution)/shard_map/ppermute | solution.py:13
  163.2 5.2 %collective-permute-start.22 = (bf16[16,1024]{1,0:T(8,128)(2,1)S(1)}, bf16[16,1024]{1,0:T(8,128)(2,1)S(1)}, u32[]{:S(2)}, u32[]{:S(2)}) collective-permute-start(bf16[16,1024]{1,0:T(8,128)(2,1)S(1)} %dynamic-slice_bitcast_fusion.7), channel_id=1, source_target_pairs={{0,16},{4,20},{8,24},{12,28},{16,0},{20,4},{24,8},{28,12},{1,17},{... | collective-permute-start | bytes 98312 | tf_op jit(solution)/shard_map/ppermute | solution.py:13
  166.5 5.0 %collective-permute-start.12 = (bf16[64,1024]{1,0:T(8,128)(2,1)S(1)}, bf16[64,1024]{1,0:T(8,128)(2,1)S(1)}, u32[]{:S(2)}, u32[]{:S(2)}) collective-permute-start(bf16[64,1024]{1,0:T(8,128)(2,1)S(1)} %dynamic-slice_bitcast_fusion.4), channel_id=1, source_target_pairs={{0,4},{4,0},{8,12},{12,8},{16,20},{20,16},{24,28},{28,24},{1,5},{5... | collective-permute-start | bytes 393224 | tf_op jit(solution)/shard_map/ppermute | solution.py:13
  168.5 5.0 %collective-permute-start.23 = (bf16[16,1024]{1,0:T(8,128)(2,1)S(1)}, bf16[16,1024]{1,0:T(8,128)(2,1)S(1)}, u32[]{:S(2)}, u32[]{:S(2)}) collective-permute-start(bf16[16,1024]{1,0:T(8,128)(2,1)S(1)} %fusion.101), channel_id=1, source_target_pairs={{0,16},{4,20},{8,24},{12,28},{16,0},{20,4},{24,8},{28,12},{1,17},{... | collective-permute-start | bytes 98312 | tf_op jit(solution)/shard_map/ppermute | solution.py:13
  171.6 4.7 %collective-permute-start.13 = (bf16[32,1024]{1,0:T(8,128)(2,1)S(1)}, bf16[32,1024]{1,0:T(8,128)(2,1)S(1)}, u32[]{:S(2)}, u32[]{:S(2)}) collective-permute-start(bf16[32,1024]{1,0:T(8,128)(2,1)S(1)} %dynamic-slice_bitcast_fusion.6), channel_id=1, source_target_pairs={{0,8},{4,12},{8,0},{12,4},{16,24},{20,28},{24,16},{28,20},{1,9},{5... | collective-permute-start | bytes 196616 | tf_op jit(solution)/shard_map/ppermute | solution.py:13
  173.5 5.7 %collective-permute-start.24 = (bf16[32,1024]{1,0:T(8,128)(2,1)S(1)}, bf16[32,1024]{1,0:T(8,128)(2,1)S(1)}, u32[]{:S(2)}, u32[]{:S(2)}) collective-permute-start(bf16[32,1024]{1,0:T(8,128)(2,1)S(1)} %maximum_select_fusion.5), channel_id=1, source_target_pairs={{0,8},{4,12},{8,0},{12,4},{16,24},{20,28},{24,16},{28,20},{1,9},{5... | collective-permute-start | bytes 196616 | tf_op jit(solution)/shard_map/ppermute | solution.py:13
  176.3 4.9 %collective-permute-start.14 = (bf16[16,1024]{1,0:T(8,128)(2,1)S(1)}, bf16[16,1024]{1,0:T(8,128)(2,1)S(1)}, u32[]{:S(2)}, u32[]{:S(2)}) collective-permute-start(bf16[16,1024]{1,0:T(8,128)(2,1)S(1)} %dynamic-slice_bitcast_fusion.8), channel_id=1, source_target_pairs={{0,16},{4,20},{8,24},{12,28},{16,0},{20,4},{24,8},{28,12},{1,17},{... | collective-permute-start | bytes 98312 | tf_op jit(solution)/shard_map/ppermute | solution.py:13
  179.2 8.5 %collective-permute-start.25 = (bf16[64,1024]{1,0:T(8,128)(2,1)S(1)}, bf16[64,1024]{1,0:T(8,128)(2,1)S(1)}, u32[]{:S(2)}, u32[]{:S(2)}) collective-permute-start(bf16[64,1024]{1,0:T(8,128)(2,1)S(1)} %maximum_select_fusion.3), channel_id=1, source_target_pairs={{0,4},{4,0},{8,12},{12,8},{16,20},{20,16},{24,28},{28,24},{1,5},{5... | collective-permute-start | bytes 393224 | tf_op jit(solution)/shard_map/ppermute | solution.py:13
  181.2 5.3 %collective-permute-start.15 = (bf16[16,1024]{1,0:T(8,128)(2,1)S(1)}, bf16[16,1024]{1,0:T(8,128)(2,1)S(1)}, u32[]{:S(2)}, u32[]{:S(2)}) collective-permute-start(bf16[16,1024]{1,0:T(8,128)(2,1)S(1)} %fusion.102), channel_id=1, source_target_pairs={{0,16},{4,20},{8,24},{12,28},{16,0},{20,4},{24,8},{28,12},{1,17},{... | collective-permute-start | bytes 98312 | tf_op jit(solution)/shard_map/ppermute | solution.py:13
  186.5 4.3 %collective-permute-start.16 = (bf16[32,1024]{1,0:T(8,128)(2,1)S(1)}, bf16[32,1024]{1,0:T(8,128)(2,1)S(1)}, u32[]{:S(2)}, u32[]{:S(2)}) collective-permute-start(bf16[32,1024]{1,0:T(8,128)(2,1)S(1)} %maximum_select_fusion.4), channel_id=1, source_target_pairs={{0,8},{4,12},{8,0},{12,4},{16,24},{20,28},{24,16},{28,20},{1,9},{5... | collective-permute-start | bytes 196616 | tf_op jit(solution)/shard_map/ppermute | solution.py:13
  190.9 5.0 %collective-permute-start.17 = (bf16[64,1024]{1,0:T(8,128)(2,1)S(1)}, bf16[64,1024]{1,0:T(8,128)(2,1)S(1)}, u32[]{:S(2)}, u32[]{:S(2)}) collective-permute-start(bf16[64,1024]{1,0:T(8,128)(2,1)S(1)} %maximum_select_fusion.2), channel_id=1, source_target_pairs={{0,4},{4,0},{8,12},{12,8},{16,20},{20,16},{24,28},{28,24},{1,5},{5... | collective-permute-start | bytes 393224 | tf_op jit(solution)/shard_map/ppermute | solution.py:13
  (28 other events, 32.1 us)

commit v2 on v1

v2 whole, which is shorter than its diff:
```python
import functools

import jax
import jax.numpy as jnp
from jax import lax
from jax.experimental import pallas as pl
from jax.experimental.pallas import tpu as pltpu
from jax.sharding import PartitionSpec as P

EPS = 1e-06
F32 = jnp.float32
BF16 = jnp.bfloat16
LANES = 128
PAD = 8
COLS = 64
EDGE = 2


def swap_bit(value, axis, bit):
    count = lax.axis_size(axis)
    return lax.ppermute(value, axis, [(i, i ^ bit) for i in range(count)])


def bits_of(axis):
    count = lax.axis_size(axis)
    bits = []
    bit = 1
    while bit < count:
        bits.append(bit)
        bit *= 2
    return bits


def all_sum(value, axis):
    for bit in bits_of(axis):
        value = value + swap_bit(value, axis, bit)
    return value


def own_bit(axis, bit):
    return (lax.axis_index(axis) // bit) % 2


def halve(value, axis, bit, dim):
    mine = own_bit(axis, bit)
    keep = lax.dynamic_index_in_dim(value, mine, dim, False)
    give = lax.dynamic_index_in_dim(value, 1 - mine, dim, False)
    got = swap_bit(give, axis, bit)
    return (keep.astype(F32) + got.astype(F32)).astype(BF16)


def reduce_rows(part):
    rows, cols = part.shape
    rep_bits = bits_of("rep")
    value = part.reshape((2,) * len(rep_bits) + (-1, cols))
    for bit in rep_bits:
        depth = value.ndim - 3
        value = halve(value, "rep", bit, depth)
    for bit in bits_of("sp"):
        value = halve(value.reshape(2, -1, cols), "sp", bit, 0)
    for bit in reversed(bits_of("sp")):
        other = swap_bit(value, "sp", bit)
        mine = own_bit("sp", bit)
        value = jnp.where(
            mine == 0, jnp.concatenate([value, other]), jnp.concatenate([other, value])
        )
    return value.astype(F32)


def dot32(a, b, left, right):
    return lax.dot_general(a, b, (((left,), (right,)), ((), ())), preferred_element_type=F32)


def norm_stats(values):
    centred = values - jnp.mean(values, -1, keepdims=True)
    inverse = lax.rsqrt(jnp.mean(centred * centred, -1, keepdims=True) + EPS)
    return centred * inverse, inverse


def norm_back(upstream, gain_vec, normed, inverse):
    scaled = upstream * gain_vec
    return inverse * (
        scaled
        - jnp.mean(scaled, -1, keepdims=True)
        - normed * jnp.mean(scaled * normed, -1, keepdims=True)
    )


def masks(head_dim):
    lane = lax.broadcasted_iota(jnp.int32, (head_dim, LANES), 1)
    row = lax.broadcasted_iota(jnp.int32, (head_dim, LANES), 0)
    return lane // head_dim, lane % head_dim == row


def by_head(block_id, parts):
    out = parts[-1]
    for index in range(len(parts) - 2, -1, -1):
        out = jnp.where(block_id == index, parts[index], out)
    return out


def seg_reduce(block_id, value, fill, func):
    count = LANES // value.shape[0]
    parts = [
        func(jnp.where(block_id == index, value, fill), -1, keepdims=True) for index in range(count)
    ]
    return by_head(block_id, parts)


def seg_sum(block_id, value):
    return seg_reduce(block_id, value, 0.0, jnp.sum)


def block_diag(block_id, value):
    count = LANES // value.shape[0]
    return jnp.concatenate(
        [jnp.where(block_id == index, value, 0.0) for index in range(count)], 0
    ).astype(BF16)


def compact(block_id, full):
    head_dim = block_id.shape[0]
    count = LANES // head_dim
    return by_head(block_id, [full[i * head_dim : (i + 1) * head_dim] for i in range(count)])


def softmax_block(pack_ref, sharp_ref, block, head_dim):
    block_id, diag = masks(head_dim)
    lanes = slice(block * LANES, (block + 1) * LANES)
    count = LANES // head_dim
    gram = pack_ref[:head_dim, lanes]
    query_row = jnp.sqrt(pack_ref[head_dim : head_dim + 1, lanes] + EPS)
    key_row = jnp.sqrt(pack_ref[head_dim + 1 : head_dim + 2, lanes] + EPS)
    query_col = seg_sum(block_id, jnp.where(diag, query_row, 0.0))
    sharp = by_head(block_id, [sharp_ref[block * count + i] for i in range(count)])
    divisor = query_col * key_row
    scores = sharp * gram / divisor
    shifted = scores - seg_reduce(block_id, scores, -jnp.inf, jnp.max)
    exponent = jnp.exp(shifted)
    prob = exponent / seg_sum(block_id, exponent)
    return prob, scores, sharp, divisor, query_col, key_row, block_id, diag


def first_kernel(x_ref, gain_ref, w_ref, mixed_ref, act_ref, pack_ref, *, head_dim):
    tokens, dim = x_ref.shape
    step = 64

    @pl.loop(0, tokens // step)
    def _(index):
        rows = pl.ds(pl.multiple_of(index * step, step), step)
        normed, _ = norm_stats(x_ref[rows, :].astype(F32))
        act_ref[rows, :] = (normed * gain_ref[...]).astype(BF16)

    act = act_ref[...]
    for part in range(w_ref.shape[1] // 256):
        cols = slice(part * 256, part * 256 + 256)
        mixed_ref[:, cols] = dot32(act, w_ref[:, cols], 1, 0).astype(BF16)
    block_id, _ = masks(head_dim)
    pack_ref[head_dim:, :] = jnp.zeros_like(pack_ref[head_dim:, :])
    for block in range(dim // LANES):
        lanes = slice(block * LANES, (block + 1) * LANES)
        query = mixed_ref[:, lanes]
        key = mixed_ref[:, dim + block * LANES : dim + (block + 1) * LANES]
        pack_ref[:head_dim, lanes] = compact(block_id, dot32(query, key, 0, 0))
        for row, value in enumerate((query, key)):
            value = value.astype(F32)
            pack_ref[head_dim + row : head_dim + row + 1, lanes] = jnp.sum(
                value * value, 0, keepdims=True
            )


def shift_sum(parts):
    size = parts[1].shape[0]
    return pltpu.roll(parts[0], 1, 0) + parts[1] + pltpu.roll(parts[2], size - 1, 0)


def inner(value):
    return value[PAD:-PAD]


def row_taps(ref, rows, window, lanes, kernel, flip):
    loaded = [ref[row, window, lanes] for row in rows]
    parts = []
    for j in range(3):
        total = None
        for i in range(3):
            tap = kernel[3 * i + j]
            term = loaded[2 - i if flip else i] * tap
            total = term if total is None else total + term
        parts.append(total)
    return shift_sum(parts[::-1] if flip else parts)


def for_tiles(width, dim, body):
    @pl.loop(0, dim // LANES)
    def _(block):
        lanes = pl.ds(pl.multiple_of(block * LANES, LANES), LANES)

        @pl.loop(0, width // COLS)
        def _(part):
            start = pl.multiple_of(part * COLS, COLS)
            body(start, lanes)


def attend_kernel(
    edge_ref, sharp_ref, pack_ref, x_ref, near_ref, far_ref, value_ref, gain_one_ref, gain_two_ref,
    factor_ref, w_value_ref, w_out_ref, kernel_ref,
    attended_ref, projected_ref, residual_ref, act_mid_ref, hidden_ref, slope_ref, act_ext, diag_ref,
):
    rows, width, dim = x_ref.shape
    head_dim = dim // sharp_ref.shape[0]
    blocks = dim // LANES
    for block in range(blocks):
        prob, *_, block_id, _ = softmax_block(pack_ref, sharp_ref, block, head_dim)
        diag_ref[block] = block_diag(block_id, prob)
    act_ext[:, :PAD] = jnp.zeros_like(act_ext[:, :PAD])
    act_ext[:, PAD + width :] = jnp.zeros_like(act_ext[:, PAD + width :])

    def token_part(x_rows, value, place, own):
        parts = []
        for block in range(blocks):
            lanes = slice(block * LANES, (block + 1) * LANES)
            parts.append(dot32(value[:, lanes], diag_ref[block], 1, 1).astype(BF16))
        attended = jnp.concatenate(parts, 1)
        projected = dot32(attended, w_out_ref[...], 1, 0)
        residual = (x_rows + factor_ref[0:1, :] * projected).astype(BF16)
        normed, _ = norm_stats(residual.astype(F32))
        act = (normed * gain_two_ref[...]).astype(BF16)
        act_ext[place, PAD : PAD + width, :] = act.astype(F32)
        if own is not None:
            span = slice(own * width, (own + 1) * width)
            attended_ref[span, :] = attended
            projected_ref[span, :] = projected
            residual_ref[span, :] = residual

    for row in range(rows):
        value = value_ref[row * width : (row + 1) * width, :]
        token_part(x_ref[row].astype(F32), value, EDGE + row, row)
    even = edge_ref[0]
    for ref, place, source in (
        (near_ref, even * (rows + EDGE), (1 - even) * (rows - EDGE)),
        (far_ref, (1 - even) * (rows + EDGE), even * (rows - EDGE)),
    ):
        for row in range(EDGE):
            x_rows = ref[source + row].astype(F32)
            normed, _ = norm_stats(x_rows)
            act = (normed * gain_one_ref[...]).astype(BF16)
            value = dot32(act, w_value_ref[...], 1, 0).astype(BF16)
            token_part(x_rows, value, place + row, None)
    for row in range(rows + 2):
        act_mid_ref[row] = act_ext[row + 1, PAD : PAD + width, :].astype(BF16)

    def tile(start, lanes):
        window = pl.ds(start, COLS + 2 * PAD)
        cols = pl.ds(start, COLS)
        kernel = [kernel_ref[tap : tap + 1, lanes] for tap in range(9)]
        for row in range(rows + 2):
            h_one = inner(row_taps(act_ext, (row, row + 1, row + 2), window, lanes, kernel, False))
            cumul = 0.5 * (1.0 + lax.erf(h_one * 0.7071067811865476))
            density = jnp.exp(-0.5 * h_one * h_one) * 0.3989422804014327
            slope_ref[row, cols, lanes] = cumul + h_one * density
            if 1 <= row <= rows:
                hidden_ref[row - 1, cols, lanes] = (h_one * cumul).astype(BF16)

    for_tiles(width, dim, tile)


def back_kernel(
    edge_ref, sharp_ref, pack_ref, up_ref, near_ref, far_ref, act_mid_ref, hidden_ref, slope_ref,
    attended_ref, projected_ref, residual_ref, value_ref, act_one_ref, gain_two_ref, factor_ref,
    w_out_ref, kernel_ref,
    pack_out_ref, d_res_ref, d_value_ref, grad_ref,
    up_ext, d_ext, hid_ext, d_act, sums, d_proj_ref, d_att_ref,
):
    rows, width, dim = up_ref.shape
    head_dim = dim // sharp_ref.shape[0]
    blocks = dim // LANES
    for ref in (up_ext, d_ext, hid_ext):
        ref[:, :PAD] = jnp.zeros_like(ref[:, :PAD])
        ref[:, PAD + width :] = jnp.zeros_like(ref[:, PAD + width :])
    sums[...] = jnp.zeros_like(sums)
    main = slice(PAD, PAD + width)
    even = edge_ref[0]
    for row in range(rows):
        up_ext[EDGE + row, main, :] = up_ref[row].astype(F32)
        hid_ext[row, main, :] = hidden_ref[row].astype(F32)
    for ref, place, source in (
        (near_ref, even * (rows + EDGE), (1 - even) * (rows - EDGE)),
        (far_ref, (1 - even) * (rows + EDGE), even * (rows - EDGE)),
    ):
        for row in range(EDGE):
            up_ext[place + row, main, :] = ref[source + row].astype(F32)

    def d_hidden_tile(start, lanes):
        window = pl.ds(start, COLS + 2 * PAD)
        cols = pl.ds(start, COLS)
        factor = factor_ref[1:2, lanes]
        kernel = [kernel_ref[9 + tap : 10 + tap, lanes] * factor for tap in range(9)]
        for row in range(rows + 2):
            d_hidden = inner(row_taps(up_ext, (row, row + 1, row + 2), window, lanes, kernel, True))
            d_h = d_hidden * slope_ref[row, cols, lanes]
            if row == 0:
                d_h = jnp.where(edge_ref[1] > 0, d_h, 0.0)
            if row == rows + 1:
                d_h = jnp.where(edge_ref[2] > 0, d_h, 0.0)
            d_ext[row, pl.ds(start + PAD, COLS), lanes] = d_h

    for_tiles(width, dim, d_hidden_tile)

    def fold(value):
        return jnp.sum(value.reshape(-1, 8, LANES), 0)

    def d_act_tile(start, lanes):
        window = pl.ds(start, COLS + 2 * PAD)
        cols = pl.ds(start, COLS)
        kernel = [kernel_ref[tap : tap + 1, lanes] for tap in range(9)]
        size = COLS + 2 * PAD
        shifts = (1, 0, size - 1)
        for row in range(rows):
            d_act[row, cols, lanes] = inner(
                row_taps(d_ext, (row, row + 1, row + 2), window, lanes, kernel, True)
            )
        act = [act_mid_ref[row, cols, lanes].astype(F32) for row in range(rows + 2)]
        moved = [
            [inner(pltpu.roll(d_ext[1 + row, window, lanes], shifts[2 - j], 0)) if j != 1
             else inner(d_ext[1 + row, window, lanes]) for j in range(3)]
            for row in range(rows)
        ]
        for i in range(3):
            for j in range(3):
                total = moved[0][j] * act[i]
                for row in range(1, rows):
                    total = total + moved[row][j] * act[i + row]
                sums[3 * i + j, :, lanes] += fold(total)
        up = [up_ext[1 + row, pl.ds(start + PAD, COLS), lanes] for row in range(rows + 2)]
        moved = [
            [inner(pltpu.roll(hid_ext[row, window, lanes], shifts[j], 0)) if j != 1
             else inner(hid_ext[row, window, lanes]) for j in range(3)]
            for row in range(rows)
        ]
        for i in range(3):
            for j in range(3):
                total = moved[0][j] * up[2 - i]
                for row in range(1, rows):
                    total = total + moved[row][j] * up[2 - i + row]
                sums[9 + 3 * i + j, :, lanes] += fold(total)

    for_tiles(width, dim, d_act_tile)

    factor_one, factor_two = factor_ref[0:1, :], factor_ref[1:2, :]
    scale_one = jnp.zeros((1, dim), F32)
    step = 64
    for row in range(rows):
        for part in range(width // step):
            span = slice(row * width + part * step, row * width + (part + 1) * step)
            cols = slice(part * step, (part + 1) * step)
            normed, inverse = norm_stats(residual_ref[span, :].astype(F32))
            d_res = up_ref[row, cols, :].astype(F32) + norm_back(
                d_act[row, cols, :], gain_two_ref[...], normed, inverse
            )
            d_res_ref[span, :] = d_res
            scale_one = scale_one + jnp.sum(projected_ref[span, :] * d_res, 0, keepdims=True)
            d_proj_ref[span, :] = (factor_one * d_res).astype(BF16)
    scale_two = jnp.zeros((1, dim), F32)
    for tap in range(9):
        pack_out_ref[head_dim + tap : head_dim + tap + 1, :] = jnp.sum(sums[tap], 0, keepdims=True)
        raw = jnp.sum(sums[9 + tap], 0, keepdims=True)
        pack_out_ref[head_dim + 9 + tap : head_dim + 10 + tap, :] = raw * factor_two
        scale_two = scale_two + raw * kernel_ref[9 + tap : 10 + tap, :]
    pack_out_ref[head_dim + 18 : head_dim + 19, :] = scale_one
    pack_out_ref[head_dim + 19 : head_dim + 20, :] = scale_two
    pack_out_ref[head_dim + 20 :, :] = jnp.zeros_like(pack_out_ref[head_dim + 20 :, :])
    d_att_ref[...] = dot32(d_proj_ref[...], w_out_ref[...], 1, 1).astype(BF16)
    for block in range(blocks):
        lanes = slice(block * LANES, (block + 1) * LANES)
        prob, *_, block_id, _ = softmax_block(pack_ref, sharp_ref, block, head_dim)
        d_att = d_att_ref[:, lanes]
        pack_out_ref[:head_dim, lanes] = compact(block_id, dot32(d_att, value_ref[:, lanes], 0, 0))
        d_value_ref[:, lanes] = dot32(d_att, block_diag(block_id, prob), 1, 0).astype(BF16)
    grad_ref[:, :dim] = dot32(act_one_ref[...], d_value_ref[...], 0, 0).astype(BF16)
    grad_ref[:, dim:] = dot32(attended_ref[...], d_proj_ref[...], 0, 0).astype(BF16)


def gram_kernel(
    sharp_ref, pack_ref, prob_ref, mixed_ref, act_ref, d_qk_ref, grad_ref,
):
    tokens, dim = act_ref.shape
    head_dim = dim // sharp_ref.shape[0]
    for block in range(dim // LANES):
        lanes = slice(block * LANES, (block + 1) * LANES)
        key_lanes = slice(dim + block * LANES, dim + (block + 1) * LANES)
        prob, scores, sharp, divisor, query_col, key_row, block_id, diag = softmax_block(
            pack_ref, sharp_ref, block, head_dim
        )
        prob_grad = prob_ref[:head_dim, lanes]
        d_scores = prob * (prob_grad - seg_sum(block_id, prob * prob_grad))
        d_gram = block_diag(block_id, d_scores * sharp / divisor)
        weighted = d_scores * scores
        d_qsq_col = -seg_sum(block_id, weighted) / (2.0 * query_col * query_col)
        d_qsq = jnp.sum(jnp.where(diag, d_qsq_col, 0.0), 0, keepdims=True)
        d_ksq = -jnp.sum(weighted, 0, keepdims=True) / (2.0 * key_row * key_row)
        query, key = mixed_ref[:, lanes], mixed_ref[:, key_lanes]
        d_query = dot32(key, d_gram, 1, 1) + 2.0 * d_qsq * query.astype(F32)
        d_key = dot32(query, d_gram, 1, 0) + 2.0 * d_ksq * key.astype(F32)
        d_qk_ref[:, lanes] = d_query.astype(BF16)
        d_qk_ref[:, key_lanes] = d_key.astype(BF16)
    act = act_ref[...]
    for part in range(2 * dim // 256):
        cols = slice(part * 256, part * 256 + 256)
        grad_ref[:, cols] = dot32(act, d_qk_ref[:, cols], 0, 0).astype(BF16)


def input_kernel(x_ref, gain_ref, w_ref, d_qk_ref, d_value_ref, d_res_ref, out_ref):
    tokens, dim = x_ref.shape
    step = 128
    for part in range(tokens // step):
        rows = slice(part * step, (part + 1) * step)
        d_act = dot32(d_qk_ref[rows, :], w_ref[:, : 2 * dim], 1, 1) + dot32(
            d_value_ref[rows, :], w_ref[:, 2 * dim :], 1, 1
        )
        normed, inverse = norm_stats(x_ref[rows, :].astype(F32))
        out_ref[rows, :] = (
            d_res_ref[rows, :] + norm_back(d_act, gain_ref[...], normed, inverse)
        ).astype(BF16)


def call(body, name, outs, args, scalars=0, scratch=()):
    specs = [
        pl.BlockSpec(memory_space=pltpu.SMEM if i < scalars else pltpu.VMEM)
        for i in range(len(args))
    ]
    return pl.pallas_call(
        body,
        name=name,
        out_shape=[jax.ShapeDtypeStruct(shape, dtype) for shape, dtype in outs],
        in_specs=specs,
        out_specs=[pl.BlockSpec(memory_space=pltpu.VMEM)] * len(outs),
        scratch_shapes=[pltpu.VMEM(shape, dtype) for shape, dtype in scratch],
    )(*args)


def beside(value):
    return swap_bit(value, "sp", 1)


def beyond(value):
    count = lax.axis_size("sp")
    hops = [(i, i - 2) for i in range(count) if i % 2 == 1 and i >= 2]
    hops += [(i, i + 2) for i in range(count) if i % 2 == 0 and i + 2 < count]
    return lax.ppermute(value, "sp", hops)


def shards(x4, up4, gain_one, w_qkv, sharp, w_out, factors, gain_two, kernels):
    rows, width, dim = x4.shape[1:]
    heads = sharp.shape[0]
    head_dim = dim // heads
    tokens = rows * width
    x_own, up_own = x4[0], up4[0]
    flat = x_own.reshape(tokens, dim)
    gain_one, gain_two = gain_one[None], gain_two[None]
    taps = kernels.reshape(-1, dim)
    index = lax.axis_index("sp")
    last = lax.axis_size("sp") - 1
    edges = jnp.stack([1 - index % 2, (index > 0).astype(jnp.int32), (index < last).astype(jnp.int32)])
    pack_rows = head_dim + 8

    x_near = beside(x_own)
    mixed, act_one, pack = call(
        functools.partial(first_kernel, head_dim=head_dim), "first",
        [((tokens, 3 * dim), BF16), ((tokens, dim), BF16), ((pack_rows, dim), F32)],
        (flat, gain_one, w_qkv),
    )
    x_far = beyond(x_near)
    up_near = beside(up_own)
    up_far = beyond(up_near)
    pack = all_sum(pack, "sp")
    value = mixed[:, 2 * dim :]
    attended, projected, residual, act_mid, hidden, slope = call(
        attend_kernel, "attend",
        [((tokens, dim), BF16), ((tokens, dim), F32), ((tokens, dim), BF16),
         ((rows + 2, width, dim), BF16), ((rows, width, dim), BF16), ((rows + 2, width, dim), F32)],
        (edges, sharp, pack, x_own, x_near, x_far, value, gain_one, gain_two, factors,
         w_qkv[:, 2 * dim :], w_out, taps),
        scalars=2,
        scratch=[((rows + 2 * EDGE, width + 2 * PAD, dim), F32), ((dim // LANES, LANES, LANES), BF16)],
    )
    small_rows = head_dim + 24
    pack_two, d_res, d_value, grad_early = call(
        back_kernel, "back",
        [((small_rows, dim), F32), ((tokens, dim), F32), ((tokens, dim), BF16), ((dim, 2 * dim), BF16)],
        (edges, sharp, pack, up_own, up_near, up_far, act_mid, hidden, slope, attended, projected,
         residual, value, act_one, gain_two, factors, w_out, taps),
        scalars=2,
        scratch=[((rows + 2 * EDGE, width + 2 * PAD, dim), F32),
                 ((rows + 2, width + 2 * PAD, dim), F32), ((rows, width + 2 * PAD, dim), F32),
                 ((rows, width, dim), F32), ((18, 8, dim), F32), ((tokens, dim), BF16),
                 ((tokens, dim), BF16)],
    )
    pack_two = all_sum(pack_two, "sp")
    d_qk, grad_late = call(
        gram_kernel, "gram",
        [((tokens, 2 * dim), BF16), ((dim, 2 * dim), BF16)],
        (sharp, pack, pack_two, mixed, act_one), scalars=1,
    )
    early = reduce_rows(grad_early)
    late = reduce_rows(grad_late)
    small = all_sum(pack_two[head_dim:], "rep")
    (grad_input,) = call(
        input_kernel, "input", [((tokens, dim), BF16)],
        (flat, gain_one, w_qkv, d_qk, d_value, d_res),
    )
    return (
        grad_input.reshape(1, rows, width, dim),
        jnp.concatenate([late, early[:, :dim]], 1),
        early[:, dim:],
        small[:18].reshape(kernels.shape),
        small[18:20],
    )


def solution(mesh):
    rows = P("rep", "sp", None, None)
    return jax.shard_map(
        shards,
        mesh=mesh,
        in_specs=(rows, rows) + (P(),) * 7,
        out_specs=(rows, P("rep", None), P("rep", None), P(), P()),
        check_vma=False,
    )
```

time: 198 us -> 159 us (0.80)
  Pallas kernels: 0 us -> 37.8 us
  other arithmetic: 40.5 us -> 5.83 us
  local copies, waits for them, and re-layouts: 36.7 us -> 11.1 us
  matrix products: 19.4 us -> 0 us
  waiting for transfers between devices: 51.8 us -> 68.5 us
  starting transfers between devices: 46.4 us -> 34.2 us
    pallas_call x0 -> x5, Pallas kernels: none -> 37.8 us  [call(): pl.pallas_call(body, name=name, out_shape=[jax.ShapeDtypeStruct(shape, dt...]
    dot_general x20 -> x0, matrix products: 19.4 us -> none  [the longest x12 9.84 us: dot32(): return lax.dot_general(a, b, (dims, ((), ())), preferred_element_type=F32)]
    ppermute x26, waiting for transfers between devices: 51.8 us -> 68.5 us  [swap_bit(): return lax.ppermute(value, axis, [(i, i ^ bit) for i in range(count)])]
    ppermute x26, starting transfers between devices: 37.8 us -> 26.4 us  [swap_bit(): return lax.ppermute(value, axis, [(i, i ^ bit) for i in range(count)])]
    slice x16 -> x3, local copies, waits for them, and re-layouts: 14.2 us -> 3.8 us  [the longest x1 1.92 us: shards(): value = mixed[:, 2 * dim:]]
    reduce_sum x13 -> x0, other arithmetic: 8.92 us -> none  [the longest x5 2.77 us: norm_stats(): inverse = lax.rsqrt(jnp.mean(centred * centred, -1, keepdims=True) + EPS)]
    convert_element_type x7 -> x0, other arithmetic: 6.78 us -> none  [the longest x1 1.94 us: shards(): up_ext = jnp.concatenate([up_above[-2:], up_own, up_below[:2]]).astype(F32)]
    add x3 -> x0, other arithmetic: 6.72 us -> none  [conv(): column = column + field[row:row + field.shape[0] - 2] * kernel[i, j]]
  transfers between devices with their start and end apart: 28 -> 28, of which waited for: 18 -> 16; matrix products, arithmetic and copies ran while one was open for 28% -> 8% of each run, Pallas kernels for 0% -> 16%
where the time goes in v2:
time: 159 us; the launch traced here: 158 us
  waiting for transfers between devices  68.5 us (43%)
  Pallas kernels  37.8 us (24%)
  starting transfers between devices  34.2 us (22%)
  local copies, waits for them, and re-layouts  11.1 us (7%)
  other arithmetic  5.83 us (4%)
    ppermute x26, waiting for transfers between devices, swap_bit(): return lax.ppermute(value, axis, [(i, i ^ bit) for i in range(count)])  68.5 us
    pallas_call x5, Pallas kernels, call(): pl.pallas_call(body, name=name, out_shape=[jax.ShapeDtypeStruct(shape, dt...  37.8 us
    ppermute x26, starting transfers between devices, swap_bit(): return lax.ppermute(value, axis, [(i, i ^ bit) for i in range(count)])  26.4 us
    ppermute x2, starting transfers between devices, beyond(): return lax.ppermute(value, 'sp', hops)  7.78 us
    add x8, other arithmetic, all_sum(): value = value + swap_bit(value, axis, bit)  3.45 us
  transfers between devices with their start and end apart: 28, of which 16 were waited for; matrix products, arithmetic and copies ran while one was open for 8% of the time, Pallas kernels for 16%

profile of v2, /device:TPU:0, one launch (start us, length us, event | category | flops | bytes accessed | tf_op | source)
XLA Modules:
  0.0 158.4 jit_solution(6508327957001856714)
XLA Ops:
  0.6 3.0 %collective-permute-start.5 = (bf16[2,256,512]{2,1,0:T(8,128)(2,1)}, bf16[2,256,512]{2,1,0:T(8,128)(2,1)S(1)}, u32[]{:S(2)}, u32[]{:S(2)}) collective-permute-start(bf16[2,256,512]{2,1,0:T(8,128)(2,1)} %bitcast.68), channel_id=1, source_target_pairs={{0,4},{4,0},{8,12},{12,8},{16,20},{20,16},{24,28},{28,24},{1,5},{5... | collective-permute-start | bytes 1572872 | tf_op jit(solution)/shard_map/ppermute | solution.py:21
  3.7 0.1 collective-permute-start.3
  3.7 12.9 %collective-permute-done.5.near_ref = bf16[2,256,512]{2,1,0:T(8,128)(2,1)S(1)} collective-permute-done((bf16[2,256,512]{2,1,0:T(8,128)(2,1)}, bf16[2,256,512]{2,1,0:T(8,128)(2,1)S(1)}, u32[]{:S(2)}, u32[]{:S(2)}) %collective-permute-start.5) | collective-permute-done | bytes 524320 | tf_op jit(solution)/shard_map/ppermute | solution.py:21
  16.7 4.0 %collective-permute-start.6 = (bf16[2,256,512]{2,1,0:T(8,128)(2,1)S(1)}, bf16[2,256,512]{2,1,0:T(8,128)(2,1)S(1)}, u32[]{:S(2)}, u32[]{:S(2)}) collective-permute-start(bf16[2,256,512]{2,1,0:T(8,128)(2,1)S(1)} %collective-permute-done.5.near_ref), channel_id=1, source_target_pairs={{12,4},{20,12},{28,20},{0,8},{8,16},{16,24},{13,5},{21,13},{29,21}... | collective-permute-start | bytes 1572872 | tf_op jit(solution)/shard_map/ppermute | solution.py:450
  20.7 6.3 %collective-permute-done.3.near_ref = bf16[2,256,512]{2,1,0:T(8,128)(2,1)S(1)} collective-permute-done((bf16[2,256,512]{2,1,0:T(8,128)(2,1)}, bf16[2,256,512]{2,1,0:T(8,128)(2,1)S(1)}, u32[]{:S(2)}, u32[]{:S(2)}) %collective-permute-start.3) | collective-permute-done | bytes 524320 | tf_op jit(solution)/shard_map/ppermute | solution.py:21
  27.0 3.7 %collective-permute-start.4 = (bf16[2,256,512]{2,1,0:T(8,128)(2,1)S(1)}, bf16[2,256,512]{2,1,0:T(8,128)(2,1)S(1)}, u32[]{:S(2)}, u32[]{:S(2)}) collective-permute-start(bf16[2,256,512]{2,1,0:T(8,128)(2,1)S(1)} %collective-permute-done.3.near_ref), channel_id=1, source_target_pairs={{12,4},{20,12},{28,20},{0,8},{8,16},{16,24},{13,5},{21,13},{29,21}... | collective-permute-start | bytes 1572872 | tf_op jit(solution)/shard_map/ppermute | solution.py:450
  30.8 5.3 %first.1 = (bf16[512,1536]{1,0:T(8,128)(2,1)}, bf16[512,512]{1,0:T(8,128)(2,1)}, f32[72,512]{1,0:T(8,128)}) custom-call(bf16[512,512]{1,0:T(8,128)(2,1)} %bitcast.69, f32[1,512]{1,0:T(1,128)} %bitcast.92, bf16[512,1536]{1,0:T(8,128)(2,1)} %w_ref.3), custom_call_target="tpu_custom_call" | custom-call | tf_op jit(solution)/shard_map/first/pallas_call | solution.py:432
  36.1 5.4 %collective-permute-done = f32[72,512]{1,0:T(8,128)S(1)} collective-permute-done((f32[72,512]{1,0:T(8,128)}, f32[72,512]{1,0:T(8,128)S(1)}, u32[]{:S(2)}, u32[]{:S(2)}) %collective-permute-start) | collective-permute-done | bytes 147488 | tf_op jit(solution)/shard_map/ppermute | solution.py:21
  41.5 0.9 add.137
  42.4 1.6 %collective-permute-start.1 = (f32[72,512]{1,0:T(8,128)S(1)}, f32[72,512]{1,0:T(8,128)S(1)}, u32[]{:S(2)}, u32[]{:S(2)}) collective-permute-start(f32[72,512]{1,0:T(8,128)S(1)} %add.137), channel_id=1, source_target_pairs={{0,8},{4,12},{8,0},{12,4},{16,24},{20,28},{24,16},{28,20},{1,9},{5... | collective-permute-start | bytes 442376 | tf_op jit(solution)/shard_map/ppermute | solution.py:21
  44.0 3.6 %collective-permute-done.1 = f32[72,512]{1,0:T(8,128)S(1)} collective-permute-done((f32[72,512]{1,0:T(8,128)S(1)}, f32[72,512]{1,0:T(8,128)S(1)}, u32[]{:S(2)}, u32[]{:S(2)}) %collective-permute-start.1) | collective-permute-done | bytes 147488 | tf_op jit(solution)/shard_map/ppermute | solution.py:21
  47.7 3.4 %collective-permute-start.2 = (f32[72,512]{1,0:T(8,128)S(1)}, f32[72,512]{1,0:T(8,128)S(1)}, u32[]{:S(2)}, u32[]{:S(2)}) collective-permute-start(f32[72,512]{1,0:T(8,128)S(1)} %add.138), channel_id=1, source_target_pairs={{0,16},{4,20},{8,24},{12,28},{16,0},{20,4},{24,8},{28,12},{1,17},{... | collective-permute-start | bytes 442376 | tf_op jit(solution)/shard_map/ppermute | solution.py:21
  51.0 1.9 %slice.22.w_value_ref = bf16[512,512]{1,0:T(8,128)(2,1)} slice(bf16[512,1536]{1,0:T(8,128)(2,1)} %w_ref.3), slice={[0:512], [1024:1536]} | slice | bytes 1048576 | tf_op jit(solution)/shard_map/slice | solution.py:483
  52.9 1.9 %slice.21.value_ref = bf16[512,512]{1,0:T(8,128)(2,1)} slice(bf16[512,1536]{1,0:T(8,128)(2,1)} %get-tuple-element.21.mixed_ref), slice={[0:512], [1024:1536]} | slice | bytes 1048576 | tf_op jit(solution)/shard_map/slice | solution.py:477
  54.8 0.6 reshape.63.kernel_ref
  55.5 0.6 pad_add_fusion.edge_ref
  56.1 0.7 add.139.pack_ref
  56.8 0.8 copy-done.6
  57.5 10.5 %attend.1 = (bf16[512,512]{1,0:T(8,128)(2,1)}, f32[512,512]{1,0:T(8,128)}, bf16[512,512]{1,0:T(8,128)(2,1)}, bf16[4,256,512]{2,1,0:T(8,128)(2,1)}, bf16[2,256,512]{2,1,0:T(8,128)(2,1)}, /*index=5*/f32[4,256,512]{2,1,0:T(8,128)}) custom-call(s32[3]{0:T(128)} %pad_add_fusion.edge_ref, f32[8]{0:T(128)} %sharp_ref.5, f32[72,512]{1,0:T(8,128)} %add.139.pack_ref, ...), custom_call_target="tpu_custom_call" | custom-call | tf_op jit(solution)/shard_map/attend/pallas_call | solution.py:432
  68.1 0.8 copy-done.4
  68.9 11.9 %back.1 = (f32[88,512]{1,0:T(8,128)}, f32[512,512]{1,0:T(8,128)}, bf16[512,512]{1,0:T(8,128)(2,1)}, bf16[512,1024]{1,0:T(8,128)(2,1)}) custom-call(s32[3]{0:T(128)} %pad_add_fusion.edge_ref, f32[8]{0:T(128)} %sharp_ref.5, f32[72,512]{1,0:T(8,128)} %add.139.pack_ref, bf16[2,256,512]{2,1,0:T(8,128)(2,1)} %bitcast.81, bf16[2,256,512]{2,1,0:T(8,128)(2,1)} %copy-done.3, ...), custom_call_target="tpu_custom_call" | custom-call | tf_op jit(solution)/shard_map/back/pallas_call | solution.py:432
  80.8 1.2 dynamic-slice_bitcast_fusion
  82.0 0.1 collective-permute-start.18
  82.1 0.4 collective-permute-start.7
  82.5 6.7 %collective-permute-done.7 = f32[88,512]{1,0:T(8,128)S(1)} collective-permute-done((f32[88,512]{1,0:T(8,128)}, f32[88,512]{1,0:T(8,128)S(1)}, u32[]{:S(2)}, u32[]{:S(2)}) %collective-permute-start.7) | collective-permute-done | bytes 180256 | tf_op jit(solution)/shard_map/ppermute | solution.py:21
  89.2 0.9 add.141
  90.2 0.1 collective-permute-start.8
  90.4 5.9 %collective-permute-done.8 = f32[88,512]{1,0:T(8,128)S(1)} collective-permute-done((f32[88,512]{1,0:T(8,128)S(1)}, f32[88,512]{1,0:T(8,128)S(1)}, u32[]{:S(2)}, u32[]{:S(2)}) %collective-permute-start.8) | collective-permute-done | bytes 180256 | tf_op jit(solution)/shard_map/ppermute | solution.py:21
  96.3 1.0 collective-permute-start.9
  97.4 0.2 fusion
  97.6 1.6 %collective-permute-start.19 = (bf16[128,1024]{1,0:T(8,128)(2,1)S(1)}, bf16[128,1024]{1,0:T(8,128)(2,1)S(1)}, u32[]{:S(2)}, u32[]{:S(2)}) collective-permute-start(bf16[128,1024]{1,0:T(8,128)(2,1)S(1)} %dynamic-slice_bitcast_fusion.2), channel_id=1, source_target_pairs={{0,2},{1,3},{2,0},{3,1},{4,6},{5,7},{6,4},{7,5},{8,10},{9,11},{10,... | collective-permute-start | bytes 786440 | tf_op jit(solution)/shard_map/ppermute | solution.py:21
  99.2 7.1 %collective-permute-done.9 = f32[88,512]{1,0:T(8,128)S(1)} collective-permute-done((f32[88,512]{1,0:T(8,128)S(1)}, f32[88,512]{1,0:T(8,128)S(1)}, u32[]{:S(2)}, u32[]{:S(2)}) %collective-permute-start.9) | collective-permute-done | bytes 180256 | tf_op jit(solution)/shard_map/ppermute | solution.py:21
  106.4 0.6 copy-done
  107.0 4.5 %gram.1 = (bf16[512,1024]{1,0:T(8,128)(2,1)}, bf16[512,1024]{1,0:T(8,128)(2,1)}) custom-call(f32[8]{0:T(128)} %sharp_ref.5, f32[72,512]{1,0:T(8,128)} %add.139.pack_ref, f32[88,512]{1,0:T(8,128)} %copy-done, bf16[512,1536]{1,0:T(8,128)(2,1)} %get-tuple-element.21.mixed_ref, bf16[512,512]{1,0:T(8,128)(2,1)} %get-tuple-element.28.act_one_ref.act_ref), custom_call_target="tpu_custom_call" | custom-call | tf_op jit(solution)/shard_map/gram/pallas_call | solution.py:432
  111.5 1.2 dynamic-slice_bitcast_fusion.1
  112.7 0.5 collective-permute-start.10
  113.2 0.8 slice_add_fusion
  114.0 1.5 collective-permute-start.27
  115.6 0.4 collective-permute-start.20
  116.1 0.2 fusion.1
  116.3 0.6 collective-permute-start.11
  116.9 4.0 %collective-permute-done.20 = bf16[64,1024]{1,0:T(8,128)(2,1)S(1)} collective-permute-done((bf16[64,1024]{1,0:T(8,128)(2,1)S(1)}, bf16[64,1024]{1,0:T(8,128)(2,1)S(1)}, u32[]{:S(2)}, u32[]{:S(2)}) %collective-permute-start.20) | collective-permute-done | bytes 131104 | tf_op jit(solution)/shard_map/ppermute | solution.py:21
  121.1 3.1 %collective-permute-done.11 = bf16[128,1024]{1,0:T(8,128)(2,1)S(1)} collective-permute-done((bf16[128,1024]{1,0:T(8,128)(2,1)S(1)}, bf16[128,1024]{1,0:T(8,128)(2,1)S(1)}, u32[]{:S(2)}, u32[]{:S(2)}) %collective-permute-start.11) | collective-permute-done | bytes 262176 | tf_op jit(solution)/shard_map/ppermute | solution.py:21
  124.2 1.7 %collective-permute-start.12 = (bf16[64,1024]{1,0:T(8,128)(2,1)S(1)}, bf16[64,1024]{1,0:T(8,128)(2,1)S(1)}, u32[]{:S(2)}, u32[]{:S(2)}) collective-permute-start(bf16[64,1024]{1,0:T(8,128)(2,1)S(1)} %dynamic-slice_bitcast_fusion.5), channel_id=1, source_target_pairs={{0,4},{4,0},{8,12},{12,8},{16,20},{20,16},{24,28},{28,24},{1,5},{5... | collective-permute-start | bytes 393224 | tf_op jit(solution)/shard_map/ppermute | solution.py:21
  126.1 3.2 %collective-permute-done.12 = bf16[64,1024]{1,0:T(8,128)(2,1)S(1)} collective-permute-done((bf16[64,1024]{1,0:T(8,128)(2,1)S(1)}, bf16[64,1024]{1,0:T(8,128)(2,1)S(1)}, u32[]{:S(2)}, u32[]{:S(2)}) %collective-permute-start.12) | collective-permute-done | bytes 131104 | tf_op jit(solution)/shard_map/ppermute | solution.py:21
  129.3 0.1 collective-permute-start.13
  129.4 1.4 collective-permute-done.22
  130.9 2.0 %collective-permute-start.23 = (bf16[16,1024]{1,0:T(8,128)(2,1)S(1)}, bf16[16,1024]{1,0:T(8,128)(2,1)S(1)}, u32[]{:S(2)}, u32[]{:S(2)}) collective-permute-start(bf16[16,1024]{1,0:T(8,128)(2,1)S(1)} %fusion.10), channel_id=1, source_target_pairs={{0,16},{4,20},{8,24},{12,28},{16,0},{20,4},{24,8},{28,12},{1,17},{... | collective-permute-start | bytes 98312 | tf_op jit(solution)/shard_map/ppermute | solution.py:21
  132.9 0.8 collective-permute-done.13
  133.7 1.8 %collective-permute-start.14 = (bf16[16,1024]{1,0:T(8,128)(2,1)S(1)}, bf16[16,1024]{1,0:T(8,128)(2,1)S(1)}, u32[]{:S(2)}, u32[]{:S(2)}) collective-permute-start(bf16[16,1024]{1,0:T(8,128)(2,1)S(1)} %dynamic-slice_bitcast_fusion.9), channel_id=1, source_target_pairs={{0,16},{4,20},{8,24},{12,28},{16,0},{20,4},{24,8},{28,12},{1,17},{... | collective-permute-start | bytes 98312 | tf_op jit(solution)/shard_map/ppermute | solution.py:21
  135.4 0.6 collective-permute-done.23
  136.1 1.3 collective-permute-start.24
  137.4 1.9 %collective-permute-done.14 = bf16[16,1024]{1,0:T(8,128)(2,1)S(1)} collective-permute-done((bf16[16,1024]{1,0:T(8,128)(2,1)S(1)}, bf16[16,1024]{1,0:T(8,128)(2,1)S(1)}, u32[]{:S(2)}, u32[]{:S(2)}) %collective-permute-start.14) | collective-permute-done | bytes 32800 | tf_op jit(solution)/shard_map/ppermute | solution.py:21
  139.3 1.2 collective-permute-start.15
  140.5 0.8 collective-permute-start.25
  141.3 5.4 %input.1 = bf16[512,512]{1,0:T(8,128)(2,1)} custom-call(bf16[512,512]{1,0:T(8,128)(2,1)} %bitcast.71, f32[1,512]{1,0:T(1,128)} %bitcast.94, bf16[512,1536]{1,0:T(8,128)(2,1)} %w_ref.3, bf16[512,1024]{1,0:T(8,128)(2,1)} %get-tuple-element.30.d_qk_ref, bf16[512,512]{1,0:T(8,128)(2,1)} %get-tuple-element.31.d_value_ref, f32[512,512]{1,0:T(8,128)} %get-tuple-element.32.d_res_ref), custom_call_target="tpu_custom_call" | custom-call | tf_op jit(solution)/shard_map/input/pallas_call | solution.py:432
  146.8 0.6 slice.32
  147.4 0.6 copy.17
  148.1 1.7 %collective-permute-start.16 = (bf16[32,1024]{1,0:T(8,128)(2,1)S(1)}, bf16[32,1024]{1,0:T(8,128)(2,1)S(1)}, u32[]{:S(2)}, u32[]{:S(2)}) collective-permute-start(bf16[32,1024]{1,0:T(8,128)(2,1)S(1)} %maximum_select_fusion.4), channel_id=1, source_target_pairs={{0,8},{4,12},{8,0},{12,4},{16,24},{20,28},{24,16},{28,20},{1,9},{5... | collective-permute-start | bytes 196616 | tf_op jit(solution)/shard_map/ppermute | solution.py:21
  149.9 2.5 %collective-permute-done.16 = bf16[32,1024]{1,0:T(8,128)(2,1)S(1)} collective-permute-done((bf16[32,1024]{1,0:T(8,128)(2,1)S(1)}, bf16[32,1024]{1,0:T(8,128)(2,1)S(1)}, u32[]{:S(2)}, u32[]{:S(2)}) %collective-permute-start.16) | collective-permute-done | bytes 65568 | tf_op jit(solution)/shard_map/ppermute | solution.py:21
  152.4 1.3 collective-permute-start.17
  153.7 0.7 fusion.12
  154.5 3.0 %collective-permute-done.17 = bf16[64,1024]{1,0:T(8,128)(2,1)S(1)} collective-permute-done((bf16[64,1024]{1,0:T(8,128)(2,1)S(1)}, bf16[64,1024]{1,0:T(8,128)(2,1)S(1)}, u32[]{:S(2)}, u32[]{:S(2)}) %collective-permute-start.17) | collective-permute-done | bytes 131104 | tf_op jit(solution)/shard_map/ppermute | solution.py:21
  157.5 0.9 pad_maximum_fusion
  (58 shorter events, 0.9 us)
Async XLA Ops:
  0.6 16.0 %collective-permute-start.5 = (bf16[2,256,512]{2,1,0:T(8,128)(2,1)}, bf16[2,256,512]{2,1,0:T(8,128)(2,1)S(1)}, u32[]{:S(2)}, u32[]{:S(2)}) collective-permute-start(bf16[2,256,512]{2,1,0:T(8,128)(2,1)} %bitcast.68), channel_id=1, source_target_pairs={{0,4},{4,0},{8,12},{12,8},{16,20},{20,16},{24,28},{28,24},{1,5},{5... | collective-permute-start | bytes 1572872 | tf_op jit(solution)/shard_map/ppermute | solution.py:21
  3.7 23.4 %collective-permute-start.3 = (bf16[2,256,512]{2,1,0:T(8,128)(2,1)}, bf16[2,256,512]{2,1,0:T(8,128)(2,1)S(1)}, u32[]{:S(2)}, u32[]{:S(2)}) collective-permute-start(bf16[2,256,512]{2,1,0:T(8,128)(2,1)} %bitcast.80), channel_id=1, source_target_pairs={{0,4},{4,0},{8,12},{12,8},{16,20},{20,16},{24,28},{28,24},{1,5},{5... | collective-permute-start | bytes 1572872 | tf_op jit(solution)/shard_map/ppermute | solution.py:21
  16.6 36.2 %copy-start.5 = (bf16[2,256,512]{2,1,0:T(8,128)(2,1)}, bf16[2,256,512]{2,1,0:T(8,128)(2,1)S(1)}, u32[]{:S(2)}) copy-start(bf16[2,256,512]{2,1,0:T(8,128)(2,1)S(1)} %collective-permute-done.5.near_ref) | copy-start | bytes 1572868
  16.7 40.1 %collective-permute-start.6 = (bf16[2,256,512]{2,1,0:T(8,128)(2,1)S(1)}, bf16[2,256,512]{2,1,0:T(8,128)(2,1)S(1)}, u32[]{:S(2)}, u32[]{:S(2)}) collective-permute-start(bf16[2,256,512]{2,1,0:T(8,128)(2,1)S(1)} %collective-permute-done.5.near_ref), channel_id=1, source_target_pairs={{12,4},{20,12},{28,20},{0,8},{8,16},{16,24},{13,5},{21,13},{29,21}... | collective-permute-start | bytes 1572872 | tf_op jit(solution)/shard_map/ppermute | solution.py:450
  27.0 25.9 %copy-start.3 = (bf16[2,256,512]{2,1,0:T(8,128)(2,1)}, bf16[2,256,512]{2,1,0:T(8,128)(2,1)S(1)}, u32[]{:S(2)}) copy-start(bf16[2,256,512]{2,1,0:T(8,128)(2,1)S(1)} %collective-permute-done.3.near_ref) | copy-start | bytes 1572868
  27.0 41.1 %collective-permute-start.4 = (bf16[2,256,512]{2,1,0:T(8,128)(2,1)S(1)}, bf16[2,256,512]{2,1,0:T(8,128)(2,1)S(1)}, u32[]{:S(2)}, u32[]{:S(2)}) collective-permute-start(bf16[2,256,512]{2,1,0:T(8,128)(2,1)S(1)} %collective-permute-done.3.near_ref), channel_id=1, source_target_pairs={{12,4},{20,12},{28,20},{0,8},{8,16},{16,24},{13,5},{21,13},{29,21}... | collective-permute-start | bytes 1572872 | tf_op jit(solution)/shard_map/ppermute | solution.py:450
  36.1 18.7 %copy-start.7 = (f32[2,3,3,512]{3,0,2,1:T(2,128)S(1)}, f32[2,3,3,512]{3,0,2,1:T(2,128)}, u32[]{:S(2)}) copy-start(f32[2,3,3,512]{3,0,2,1:T(2,128)} %param.17) | copy-start | bytes 110596
  36.1 5.4 %collective-permute-start = (f32[72,512]{1,0:T(8,128)}, f32[72,512]{1,0:T(8,128)S(1)}, u32[]{:S(2)}, u32[]{:S(2)}) collective-permute-start(f32[72,512]{1,0:T(8,128)} %get-tuple-element.20), channel_id=1, source_target_pairs={{0,4},{4,0},{8,12},{12,8},{16,20},{20,16},{24,28},{28,24},{1,5},{5... | collective-permute-start | bytes 442376 | tf_op jit(solution)/shard_map/ppermute | solution.py:21
  42.4 5.2 %collective-permute-start.1 = (f32[72,512]{1,0:T(8,128)S(1)}, f32[72,512]{1,0:T(8,128)S(1)}, u32[]{:S(2)}, u32[]{:S(2)}) collective-permute-start(f32[72,512]{1,0:T(8,128)S(1)} %add.137), channel_id=1, source_target_pairs={{0,8},{4,12},{8,0},{12,4},{16,24},{20,28},{24,16},{28,20},{1,9},{5... | collective-permute-start | bytes 442376 | tf_op jit(solution)/shard_map/ppermute | solution.py:21
  47.7 8.4 %collective-permute-start.2 = (f32[72,512]{1,0:T(8,128)S(1)}, f32[72,512]{1,0:T(8,128)S(1)}, u32[]{:S(2)}, u32[]{:S(2)}) collective-permute-start(f32[72,512]{1,0:T(8,128)S(1)} %add.138), channel_id=1, source_target_pairs={{0,16},{4,20},{8,24},{12,28},{16,0},{20,4},{24,8},{28,12},{1,17},{... | collective-permute-start | bytes 442376 | tf_op jit(solution)/shard_map/ppermute | solution.py:21
  56.8 0.8 copy-start.6
  68.1 0.8 copy-start.4
  80.8 16.5 %copy-start.1 = (bf16[512,1024]{1,0:T(8,128)(2,1)S(1)}, bf16[512,1024]{1,0:T(8,128)(2,1)}, u32[]{:S(2)}) copy-start(bf16[512,1024]{1,0:T(8,128)(2,1)} %get-tuple-element.34) | copy-start | bytes 3145732
  82.0 15.4 %collective-permute-start.18 = (bf16[2,128,1024]{2,1,0:T(8,128)(2,1)S(1)}, bf16[2,128,1024]{2,1,0:T(8,128)(2,1)S(1)}, u32[]{:S(2)}, u32[]{:S(2)}) collective-permute-start(bf16[2,128,1024]{2,1,0:T(8,128)(2,1)S(1)} %dynamic-slice_bitcast_fusion), channel_id=1, source_target_pairs={{0,1},{1,0},{2,3},{3,2},{4,5},{5,4},{6,7},{7,6},{8,9},{9,8},{10,11... | collective-permute-start | bytes 1572872 | tf_op jit(solution)/shard_map/ppermute | solution.py:21
  82.1 7.2 %collective-permute-start.7 = (f32[88,512]{1,0:T(8,128)}, f32[88,512]{1,0:T(8,128)S(1)}, u32[]{:S(2)}, u32[]{:S(2)}) collective-permute-start(f32[88,512]{1,0:T(8,128)} %get-tuple-element.29), channel_id=1, source_target_pairs={{0,4},{4,0},{8,12},{12,8},{16,20},{20,16},{24,28},{28,24},{1,5},{5... | collective-permute-start | bytes 540680 | tf_op jit(solution)/shard_map/ppermute | solution.py:21
  90.2 6.1 %collective-permute-start.8 = (f32[88,512]{1,0:T(8,128)S(1)}, f32[88,512]{1,0:T(8,128)S(1)}, u32[]{:S(2)}, u32[]{:S(2)}) collective-permute-start(f32[88,512]{1,0:T(8,128)S(1)} %add.141), channel_id=1, source_target_pairs={{0,8},{4,12},{8,0},{12,4},{16,24},{20,28},{24,16},{28,20},{1,9},{5... | collective-permute-start | bytes 540680 | tf_op jit(solution)/shard_map/ppermute | solution.py:21
  96.3 10.0 %collective-permute-start.9 = (f32[88,512]{1,0:T(8,128)S(1)}, f32[88,512]{1,0:T(8,128)S(1)}, u32[]{:S(2)}, u32[]{:S(2)}) collective-permute-start(f32[88,512]{1,0:T(8,128)S(1)} %add.142), channel_id=1, source_target_pairs={{0,16},{4,20},{8,24},{12,28},{16,0},{20,4},{24,8},{28,12},{1,17},{... | collective-permute-start | bytes 540680 | tf_op jit(solution)/shard_map/ppermute | solution.py:21
  97.6 17.9 %collective-permute-start.19 = (bf16[128,1024]{1,0:T(8,128)(2,1)S(1)}, bf16[128,1024]{1,0:T(8,128)(2,1)S(1)}, u32[]{:S(2)}, u32[]{:S(2)}) collective-permute-start(bf16[128,1024]{1,0:T(8,128)(2,1)S(1)} %dynamic-slice_bitcast_fusion.2), channel_id=1, source_target_pairs={{0,2},{1,3},{2,0},{3,1},{4,6},{5,7},{6,4},{7,5},{8,10},{9,11},{10,... | collective-permute-start | bytes 786440 | tf_op jit(solution)/shard_map/ppermute | solution.py:21
  106.3 0.7 copy-start
  111.5 4.5 %copy-start.2 = (bf16[512,1024]{1,0:T(8,128)(2,1)S(1)}, bf16[512,1024]{1,0:T(8,128)(2,1)}, u32[]{:S(2)}) copy-start(bf16[512,1024]{1,0:T(8,128)(2,1)} %get-tuple-element.33) | copy-start | bytes 3145732
  111.5 1.7 %collective-permute-start.26 = (f32[24,512]{1,0:T(8,128)S(1)}, f32[24,512]{1,0:T(8,128)S(1)}, u32[]{:S(2)}, u32[]{:S(2)}) collective-permute-start(f32[24,512]{1,0:T(8,128)S(1)} %slice.30), channel_id=1, source_target_pairs={{0,1},{1,0},{2,3},{3,2},{4,5},{5,4},{6,7},{7,6},{8,9},{9,8},{10,11... | collective-permute-start | bytes 147464 | tf_op jit(solution)/shard_map/ppermute | solution.py:21
  112.7 3.3 %collective-permute-start.10 = (bf16[2,128,1024]{2,1,0:T(8,128)(2,1)S(1)}, bf16[2,128,1024]{2,1,0:T(8,128)(2,1)S(1)}, u32[]{:S(2)}, u32[]{:S(2)}) collective-permute-start(bf16[2,128,1024]{2,1,0:T(8,128)(2,1)S(1)} %dynamic-slice_bitcast_fusion.1), channel_id=1, source_target_pairs={{0,1},{1,0},{2,3},{3,2},{4,5},{5,4},{6,7},{7,6},{8,9},{9,8},{10,11... | collective-permute-start | bytes 1572872 | tf_op jit(solution)/shard_map/ppermute | solution.py:21
  114.0 32.8 %collective-permute-start.27 = (f32[24,512]{1,0:T(8,128)S(1)}, f32[24,512]{1,0:T(8,128)S(1)}, u32[]{:S(2)}, u32[]{:S(2)}) collective-permute-start(f32[24,512]{1,0:T(8,128)S(1)} %slice_add_fusion), channel_id=1, source_target_pairs={{0,2},{1,3},{2,0},{3,1},{4,6},{5,7},{6,4},{7,5},{8,10},{9,11},{10,... | collective-permute-start | bytes 147464 | tf_op jit(solution)/shard_map/ppermute | solution.py:21
  115.6 5.3 %collective-permute-start.20 = (bf16[64,1024]{1,0:T(8,128)(2,1)S(1)}, bf16[64,1024]{1,0:T(8,128)(2,1)S(1)}, u32[]{:S(2)}, u32[]{:S(2)}) collective-permute-start(bf16[64,1024]{1,0:T(8,128)(2,1)S(1)} %dynamic-slice_bitcast_fusion.4), channel_id=1, source_target_pairs={{0,4},{4,0},{8,12},{12,8},{16,20},{20,16},{24,28},{28,24},{1,5},{5... | collective-permute-start | bytes 393224 | tf_op jit(solution)/shard_map/ppermute | solution.py:21
  116.3 7.8 %collective-permute-start.11 = (bf16[128,1024]{1,0:T(8,128)(2,1)S(1)}, bf16[128,1024]{1,0:T(8,128)(2,1)S(1)}, u32[]{:S(2)}, u32[]{:S(2)}) collective-permute-start(bf16[128,1024]{1,0:T(8,128)(2,1)S(1)} %dynamic-slice_bitcast_fusion.3), channel_id=1, source_target_pairs={{0,2},{1,3},{2,0},{3,1},{4,6},{5,7},{6,4},{7,5},{8,10},{9,11},{10,... | collective-permute-start | bytes 786440 | tf_op jit(solution)/shard_map/ppermute | solution.py:21
  121.0 5.0 %collective-permute-start.21 = (bf16[32,1024]{1,0:T(8,128)(2,1)S(1)}, bf16[32,1024]{1,0:T(8,128)(2,1)S(1)}, u32[]{:S(2)}, u32[]{:S(2)}) collective-permute-start(bf16[32,1024]{1,0:T(8,128)(2,1)S(1)} %dynamic-slice_bitcast_fusion.6), channel_id=1, source_target_pairs={{0,8},{4,12},{8,0},{12,4},{16,24},{20,28},{24,16},{28,20},{1,9},{5... | collective-permute-start | bytes 196616 | tf_op jit(solution)/shard_map/ppermute | solution.py:21
  124.2 5.0 %collective-permute-start.12 = (bf16[64,1024]{1,0:T(8,128)(2,1)S(1)}, bf16[64,1024]{1,0:T(8,128)(2,1)S(1)}, u32[]{:S(2)}, u32[]{:S(2)}) collective-permute-start(bf16[64,1024]{1,0:T(8,128)(2,1)S(1)} %dynamic-slice_bitcast_fusion.5), channel_id=1, source_target_pairs={{0,4},{4,0},{8,12},{12,8},{16,20},{20,16},{24,28},{28,24},{1,5},{5... | collective-permute-start | bytes 393224 | tf_op jit(solution)/shard_map/ppermute | solution.py:21
  126.0 4.9 %collective-permute-start.22 = (bf16[16,1024]{1,0:T(8,128)(2,1)S(1)}, bf16[16,1024]{1,0:T(8,128)(2,1)S(1)}, u32[]{:S(2)}, u32[]{:S(2)}) collective-permute-start(bf16[16,1024]{1,0:T(8,128)(2,1)S(1)} %dynamic-slice_bitcast_fusion.8), channel_id=1, source_target_pairs={{0,16},{4,20},{8,24},{12,28},{16,0},{20,4},{24,8},{28,12},{1,17},{... | collective-permute-start | bytes 98312 | tf_op jit(solution)/shard_map/ppermute | solution.py:21
  129.3 4.3 %collective-permute-start.13 = (bf16[32,1024]{1,0:T(8,128)(2,1)S(1)}, bf16[32,1024]{1,0:T(8,128)(2,1)S(1)}, u32[]{:S(2)}, u32[]{:S(2)}) collective-permute-start(bf16[32,1024]{1,0:T(8,128)(2,1)S(1)} %dynamic-slice_bitcast_fusion.7), channel_id=1, source_target_pairs={{0,8},{4,12},{8,0},{12,4},{16,24},{20,28},{24,16},{28,20},{1,9},{5... | collective-permute-start | bytes 196616 | tf_op jit(solution)/shard_map/ppermute | solution.py:21
  130.9 5.2 %collective-permute-start.23 = (bf16[16,1024]{1,0:T(8,128)(2,1)S(1)}, bf16[16,1024]{1,0:T(8,128)(2,1)S(1)}, u32[]{:S(2)}, u32[]{:S(2)}) collective-permute-start(bf16[16,1024]{1,0:T(8,128)(2,1)S(1)} %fusion.10), channel_id=1, source_target_pairs={{0,16},{4,20},{8,24},{12,28},{16,0},{20,4},{24,8},{28,12},{1,17},{... | collective-permute-start | bytes 98312 | tf_op jit(solution)/shard_map/ppermute | solution.py:21
  133.7 5.6 %collective-permute-start.14 = (bf16[16,1024]{1,0:T(8,128)(2,1)S(1)}, bf16[16,1024]{1,0:T(8,128)(2,1)S(1)}, u32[]{:S(2)}, u32[]{:S(2)}) collective-permute-start(bf16[16,1024]{1,0:T(8,128)(2,1)S(1)} %dynamic-slice_bitcast_fusion.9), channel_id=1, source_target_pairs={{0,16},{4,20},{8,24},{12,28},{16,0},{20,4},{24,8},{28,12},{1,17},{... | collective-permute-start | bytes 98312 | tf_op jit(solution)/shard_map/ppermute | solution.py:21
  136.1 4.3 %collective-permute-start.24 = (bf16[32,1024]{1,0:T(8,128)(2,1)S(1)}, bf16[32,1024]{1,0:T(8,128)(2,1)S(1)}, u32[]{:S(2)}, u32[]{:S(2)}) collective-permute-start(bf16[32,1024]{1,0:T(8,128)(2,1)S(1)} %maximum_select_fusion.5), channel_id=1, source_target_pairs={{0,8},{4,12},{8,0},{12,4},{16,24},{20,28},{24,16},{28,20},{1,9},{5... | collective-permute-start | bytes 196616 | tf_op jit(solution)/shard_map/ppermute | solution.py:21
  139.3 8.8 %collective-permute-start.15 = (bf16[16,1024]{1,0:T(8,128)(2,1)S(1)}, bf16[16,1024]{1,0:T(8,128)(2,1)S(1)}, u32[]{:S(2)}, u32[]{:S(2)}) collective-permute-start(bf16[16,1024]{1,0:T(8,128)(2,1)S(1)} %fusion.11), channel_id=1, source_target_pairs={{0,16},{4,20},{8,24},{12,28},{16,0},{20,4},{24,8},{28,12},{1,17},{... | collective-permute-start | bytes 98312 | tf_op jit(solution)/shard_map/ppermute | solution.py:21
  140.5 9.3 %collective-permute-start.25 = (bf16[64,1024]{1,0:T(8,128)(2,1)S(1)}, bf16[64,1024]{1,0:T(8,128)(2,1)S(1)}, u32[]{:S(2)}, u32[]{:S(2)}) collective-permute-start(bf16[64,1024]{1,0:T(8,128)(2,1)S(1)} %maximum_select_fusion.3), channel_id=1, source_target_pairs={{0,4},{4,0},{8,12},{12,8},{16,20},{20,16},{24,28},{28,24},{1,5},{5... | collective-permute-start | bytes 393224 | tf_op jit(solution)/shard_map/ppermute | solution.py:21
  148.1 4.3 %collective-permute-start.16 = (bf16[32,1024]{1,0:T(8,128)(2,1)S(1)}, bf16[32,1024]{1,0:T(8,128)(2,1)S(1)}, u32[]{:S(2)}, u32[]{:S(2)}) collective-permute-start(bf16[32,1024]{1,0:T(8,128)(2,1)S(1)} %maximum_select_fusion.4), channel_id=1, source_target_pairs={{0,8},{4,12},{8,0},{12,4},{16,24},{20,28},{24,16},{28,20},{1,9},{5... | collective-permute-start | bytes 196616 | tf_op jit(solution)/shard_map/ppermute | solution.py:21
  152.4 5.0 %collective-permute-start.17 = (bf16[64,1024]{1,0:T(8,128)(2,1)S(1)}, bf16[64,1024]{1,0:T(8,128)(2,1)S(1)}, u32[]{:S(2)}, u32[]{:S(2)}) collective-permute-start(bf16[64,1024]{1,0:T(8,128)(2,1)S(1)} %maximum_select_fusion.2), channel_id=1, source_target_pairs={{0,4},{4,0},{8,12},{12,8},{16,20},{20,16},{24,28},{28,24},{1,5},{5... | collective-permute-start | bytes 393224 | tf_op jit(solution)/shard_map/ppermute | solution.py:21

commit v3 on v2

--- a/solution.py
+++ b/solution.py
@@ -41,29 +41,61 @@
     return (lax.axis_index(axis) // bit) % 2
 
 
-def halve(value, axis, bit, dim):
-    mine = own_bit(axis, bit)
-    keep = lax.dynamic_index_in_dim(value, mine, dim, False)
-    give = lax.dynamic_index_in_dim(value, 1 - mine, dim, False)
-    got = swap_bit(give, axis, bit)
-    return (keep.astype(F32) + got.astype(F32)).astype(BF16)
-
-
-def reduce_rows(part):
-    rows, cols = part.shape
-    rep_bits = bits_of("rep")
-    value = part.reshape((2,) * len(rep_bits) + (-1, cols))
-    for bit in rep_bits:
-        depth = value.ndim - 3
-        value = halve(value, "rep", bit, depth)
-    for bit in bits_of("sp"):
-        value = halve(value.reshape(2, -1, cols), "sp", bit, 0)
-    for bit in reversed(bits_of("sp")):
-        other = swap_bit(value, "sp", bit)
-        mine = own_bit("sp", bit)
-        value = jnp.where(
-            mine == 0, jnp.concatenate([value, other]), jnp.concatenate([other, value])
-        )
+def add_low(parts):
+    total = parts[0].astype(F32)
+    for part in parts[1:]:
+        total = total + part.astype(F32)
+    return total.astype(BF16)
+
+
+def member(axis, bits):
+    return sum(own_bit(axis, bit) << place for place, bit in enumerate(bits))
+
+
+def spread(bits, offset):
+    return sum(bit for place, bit in enumerate(bits) if (offset >> place) & 1)
+
+
+def scatter_stage(value, axis, bits, dim):
+    mine = member(axis, bits)
+    parts = [lax.dynamic_index_in_dim(value, mine, dim, False)]
+    for offset in range(1, 1 << len(bits)):
+        give = lax.dynamic_index_in_dim(value, mine ^ offset, dim, False)
+        parts.append(swap_bit(give, axis, spread(bits, offset)))
+    return add_low(parts)
+
+
+def gather_stage(value, axis, bits):
+    mine = member(axis, bits)
+    parts = [value]
+    for offset in range(1, 1 << len(bits)):
+        parts.append(swap_bit(value, axis, spread(bits, offset)))
+    out = []
+    for piece in range(len(parts)):
+        chosen = parts[0]
+        for offset in range(1, len(parts)):
+            chosen = jnp.where(mine == piece ^ offset, parts[offset], chosen)
+        out.append(chosen)
+    return jnp.concatenate(out)
+
+
+def stages_of(axis):
+    bits = bits_of(axis)
+    return [bits[:1]] + [bits[i : i + 2] for i in range(1, len(bits), 2)]
+
+
+def reduce_rows(keep, give):
+    cols = keep.shape[-1]
+    bits = bits_of("rep")
+    value = add_low([keep, swap_bit(give, "rep", bits[0])])
+    for bit in bits[1:]:
+        value = value.reshape(-1, 2, value.shape[-2], cols)
+        value = scatter_stage(value, "rep", [bit], 1)
+    value = value.reshape(-1, cols)
+    for bits in stages_of("sp"):
+        value = scatter_stage(value.reshape(1 << len(bits), -1, cols), "sp", bits, 0)
+    for bits in reversed(stages_of("sp")):
+        value = gather_stage(value, "sp", bits)
     return value.astype(F32)
 
 
@@ -269,8 +301,8 @@
     edge_ref, sharp_ref, pack_ref, up_ref, near_ref, far_ref, act_mid_ref, hidden_ref, slope_ref,
     attended_ref, projected_ref, residual_ref, value_ref, act_one_ref, gain_two_ref, factor_ref,
     w_out_ref, kernel_ref,
-    pack_out_ref, d_res_ref, d_value_ref, grad_ref,
-    up_ext, d_ext, hid_ext, d_act, sums, d_proj_ref, d_att_ref,
+    prob_out_ref, small_ref, d_res_ref, d_value_ref, keep_ref, give_ref,
+    up_ext, d_ext, hid_ext, d_act, sums, d_proj_ref, d_att_ref, grad_ref,
 ):
     rows, width, dim = up_ref.shape
     head_dim = dim // sharp_ref.shape[0]
@@ -362,27 +394,37 @@
             scale_one = scale_one + jnp.sum(projected_ref[span, :] * d_res, 0, keepdims=True)
             d_proj_ref[span, :] = (factor_one * d_res).astype(BF16)
     scale_two = jnp.zeros((1, dim), F32)
+    small_ref[20:, :] = jnp.zeros_like(small_ref[20:, :])
     for tap in range(9):
-        pack_out_ref[head_dim + tap : head_dim + tap + 1, :] = jnp.sum(sums[tap], 0, keepdims=True)
+        small_ref[tap : tap + 1, :] = jnp.sum(sums[tap], 0, keepdims=True)
         raw = jnp.sum(sums[9 + tap], 0, keepdims=True)
-        pack_out_ref[head_dim + 9 + tap : head_dim + 10 + tap, :] = raw * factor_two
+        small_ref[9 + tap : 10 + tap, :] = raw * factor_two
         scale_two = scale_two + raw * kernel_ref[9 + tap : 10 + tap, :]
-    pack_out_ref[head_dim + 18 : head_dim + 19, :] = scale_one
-    pack_out_ref[head_dim + 19 : head_dim + 20, :] = scale_two
-    pack_out_ref[head_dim + 20 :, :] = jnp.zeros_like(pack_out_ref[head_dim + 20 :, :])
+    small_ref[18:19, :] = scale_one
+    small_ref[19:20, :] = scale_two
     d_att_ref[...] = dot32(d_proj_ref[...], w_out_ref[...], 1, 1).astype(BF16)
     for block in range(blocks):
         lanes = slice(block * LANES, (block + 1) * LANES)
         prob, *_, block_id, _ = softmax_block(pack_ref, sharp_ref, block, head_dim)
         d_att = d_att_ref[:, lanes]
-        pack_out_ref[:head_dim, lanes] = compact(block_id, dot32(d_att, value_ref[:, lanes], 0, 0))
+        prob_out_ref[:, lanes] = compact(block_id, dot32(d_att, value_ref[:, lanes], 0, 0))
         d_value_ref[:, lanes] = dot32(d_att, block_diag(block_id, prob), 1, 0).astype(BF16)
     grad_ref[:, :dim] = dot32(act_one_ref[...], d_value_ref[...], 0, 0).astype(BF16)
     grad_ref[:, dim:] = dot32(attended_ref[...], d_proj_ref[...], 0, 0).astype(BF16)
+    split_rows(grad_ref, keep_ref, give_ref, edge_ref[3])
+
+
+def split_rows(full_ref, keep_ref, give_ref, bit):
+    count = keep_ref.shape[0]
+    size = keep_ref.shape[1]
+    for index in range(count):
+        for ref, side in ((keep_ref, bit), (give_ref, 1 - bit)):
+            start = pl.multiple_of((2 * index + side) * size, size)
+            ref[index] = full_ref[pl.ds(start, size), :]
 
 
 def gram_kernel(
-    sharp_ref, pack_ref, prob_ref, mixed_ref, act_ref, d_qk_ref, grad_ref,
+    edge_ref, sharp_ref, pack_ref, prob_ref, mixed_ref, act_ref, d_qk_ref, keep_ref, give_ref, grad_ref,
 ):
     tokens, dim = act_ref.shape
     head_dim = dim // sharp_ref.shape[0]
@@ -392,7 +434,7 @@
         prob, scores, sharp, divisor, query_col, key_row, block_id, diag = softmax_block(
             pack_ref, sharp_ref, block, head_dim
         )
-        prob_grad = prob_ref[:head_dim, lanes]
+        prob_grad = prob_ref[:, lanes]
         d_scores = prob * (prob_grad - seg_sum(block_id, prob * prob_grad))
         d_gram = block_diag(block_id, d_scores * sharp / divisor)
         weighted = d_scores * scores
@@ -408,6 +450,7 @@
     for part in range(2 * dim // 256):
         cols = slice(part * 256, part * 256 + 256)
         grad_ref[:, cols] = dot32(act, d_qk_ref[:, cols], 0, 0).astype(BF16)
+    split_rows(grad_ref, keep_ref, give_ref, edge_ref[3])
 
 
 def input_kernel(x_ref, gain_ref, w_ref, d_qk_ref, d_value_ref, d_res_ref, out_ref):
@@ -424,17 +467,22 @@
         ).astype(BF16)
 
 
-def call(body, name, outs, args, scalars=0, scratch=()):
-    specs = [
-        pl.BlockSpec(memory_space=pltpu.SMEM if i < scalars else pltpu.VMEM)
-        for i in range(len(args))
-    ]
+def call(body, name, outs, args, scalars=0, scratch=(), thirds=()):
+    specs = []
+    for i, arg in enumerate(args):
+        if i < scalars:
+            specs.append(pl.BlockSpec(memory_space=pltpu.SMEM))
+        elif i in thirds:
+            specs.append(pl.BlockSpec((arg.shape[0], arg.shape[1] // 3), lambda i: (0, 2)))
+        else:
+            specs.append(pl.BlockSpec(arg.shape, lambda i, n=arg.ndim: (0,) * n))
     return pl.pallas_call(
         body,
         name=name,
+        grid=(1,),
         out_shape=[jax.ShapeDtypeStruct(shape, dtype) for shape, dtype in outs],
         in_specs=specs,
-        out_specs=[pl.BlockSpec(memory_space=pltpu.VMEM)] * len(outs),
+        out_specs=[pl.BlockSpec(o[0], lambda i, n=len(o[0]): (0,) * n) for o in outs],
         scratch_shapes=[pltpu.VMEM(shape, dtype) for shape, dtype in scratch],
     )(*args)
 
@@ -448,6 +496,10 @@
     hops = [(i, i - 2) for i in range(count) if i % 2 == 1 and i >= 2]
     hops += [(i, i + 2) for i in range(count) if i % 2 == 0 and i + 2 < count]
     return lax.ppermute(value, "sp", hops)
+
+
+def after(value, earlier):
+    return lax.optimization_barrier((value, earlier))
 
 
 def shards(x4, up4, gain_one, w_qkv, sharp, w_out, factors, gain_two, kernels):
@@ -461,7 +513,9 @@
     taps = kernels.reshape(-1, dim)
     index = lax.axis_index("sp")
     last = lax.axis_size("sp") - 1
-    edges = jnp.stack([1 - index % 2, (index > 0).astype(jnp.int32), (index < last).astype(jnp.int32)])
+    edges = jnp.stack(
+        [1 - index % 2, jnp.minimum(index, 1), jnp.minimum(last - index, 1), own_bit("rep", 1)]
+    )
     pack_rows = head_dim + 8
 
     x_near = beside(x_own)
@@ -470,41 +524,51 @@
         [((tokens, 3 * dim), BF16), ((tokens, dim), BF16), ((pack_rows, dim), F32)],
         (flat, gain_one, w_qkv),
     )
-    x_far = beyond(x_near)
-    up_near = beside(up_own)
+    sp_bits = bits_of("sp")
+    for step, bit in enumerate(sp_bits):
+        pack = pack + swap_bit(pack, "sp", bit)
+        if step == 0:
+            x_near, pack = after(x_near, pack)
+            x_far = beyond(x_near)
+            up_far_in, pack = after(up_own, pack)
+            up_near = beside(up_far_in)
+    up_near, pack = after(up_near, pack)
     up_far = beyond(up_near)
-    pack = all_sum(pack, "sp")
-    value = mixed[:, 2 * dim :]
     attended, projected, residual, act_mid, hidden, slope = call(
         attend_kernel, "attend",
         [((tokens, dim), BF16), ((tokens, dim), F32), ((tokens, dim), BF16),
          ((rows + 2, width, dim), BF16), ((rows, width, dim), BF16), ((rows + 2, width, dim), F32)],
-        (edges, sharp, pack, x_own, x_near, x_far, value, gain_one, gain_two, factors,
-         w_qkv[:, 2 * dim :], w_out, taps),
+        (edges, sharp, pack, x_own, x_near, x_far, mixed, gain_one, gain_two, factors,
+         w_qkv, w_out, taps),
         scalars=2,
+        thirds=(6, 10),
         scratch=[((rows + 2 * EDGE, width + 2 * PAD, dim), F32), ((dim // LANES, LANES, LANES), BF16)],
     )
-    small_rows = head_dim + 24
-    pack_two, d_res, d_value, grad_early = call(
+    blocks = lax.axis_size("rep")
+    split = ((blocks // 2, dim // blocks, 2 * dim), BF16)
+    prob_part, small, d_res, d_value, keep, give = call(
         back_kernel, "back",
-        [((small_rows, dim), F32), ((tokens, dim), F32), ((tokens, dim), BF16), ((dim, 2 * dim), BF16)],
+        [((head_dim, dim), F32), ((24, dim), F32), ((tokens, dim), F32), ((tokens, dim), BF16),
+         split, split],
         (edges, sharp, pack, up_own, up_near, up_far, act_mid, hidden, slope, attended, projected,
-         residual, value, act_one, gain_two, factors, w_out, taps),
+         residual, mixed, act_one, gain_two, factors, w_out, taps),
         scalars=2,
+        thirds=(12,),
         scratch=[((rows + 2 * EDGE, width + 2 * PAD, dim), F32),
                  ((rows + 2, width + 2 * PAD, dim), F32), ((rows, width + 2 * PAD, dim), F32),
                  ((rows, width, dim), F32), ((18, 8, dim), F32), ((tokens, dim), BF16),
-                 ((tokens, dim), BF16)],
-    )
-    pack_two = all_sum(pack_two, "sp")
-    d_qk, grad_late = call(
+                 ((tokens, dim), BF16), ((dim, 2 * dim), BF16)],
+    )
+    prob_part = all_sum(prob_part, "sp")
+    early = reduce_rows(keep, give)
+    d_qk, keep, give = call(
         gram_kernel, "gram",
-        [((tokens, 2 * dim), BF16), ((dim, 2 * dim), BF16)],
-        (sharp, pack, pack_two, mixed, act_one), scalars=1,
-    )
-    early = reduce_rows(grad_early)
-    late = reduce_rows(grad_late)
-    small = all_sum(pack_two[head_dim:], "rep")
+        [((tokens, 2 * dim), BF16), split, split],
+        (edges, sharp, pack, prob_part, mixed, act_one), scalars=2,
+        scratch=[((dim, 2 * dim), BF16)],
+    )
+    late = reduce_rows(keep, give)
+    small = all_sum(all_sum(small, "rep"), "sp")
     (grad_input,) = call(
         input_kernel, "input", [((tokens, dim), BF16)],
         (flat, gain_one, w_qkv, d_qk, d_value, d_res),

time: 159 us -> 154 us (0.969)
  starting transfers between devices: 34.2 us -> 53.9 us
  waiting for transfers between devices: 68.5 us -> 49.7 us
  local copies, waits for them, and re-layouts: 11.1 us -> 4.35 us
    ppermute x26 -> x33, waiting for transfers between devices: 68.5 us -> 45.2 us  [swap_bit(): return lax.ppermute(value, axis, [(i, i ^ bit) for i in range(count)])]
    ppermute x26 -> x33, starting transfers between devices: 26.4 us -> 46.2 us  [swap_bit(): return lax.ppermute(value, axis, [(i, i ^ bit) for i in range(count)])]
    ppermute x2, waiting for transfers between devices: 0.01 us -> 4.49 us  [beyond(): return lax.ppermute(value, 'sp', hops)]
    slice x3 -> x0, local copies, waits for them, and re-layouts: 3.8 us -> none  [the longest x1 1.92 us: shards(): value = mixed[:, 2 * dim:]]
    squeeze x10 -> x6, local copies, waits for them, and re-layouts: 2.47 us -> 0.11 us  [scatter_stage(): give = lax.dynamic_index_in_dim(value, mine ^ offset, dim, False)]
    add x8, other arithmetic: 3.45 us -> 1.65 us  [all_sum(): value = value + swap_bit(value, axis, bit)]
    add x0 -> x3, other arithmetic: none -> 1.63 us  [shards(): pack = pack + swap_bit(pack, 'sp', bit)]
  transfers between devices with their start and end apart: 28 -> 35, of which waited for: 16 -> 19; matrix products, arithmetic and copies ran while one was open for 8% -> 5% of each run, Pallas kernels for 16% -> 17%
where the time goes in v3:
time: 154 us
  starting transfers between devices  53.9 us (35%)
  waiting for transfers between devices  49.7 us (32%)
  Pallas kernels  38.1 us (25%)
  other arithmetic  6.74 us (4%)
  local copies, waits for them, and re-layouts  4.35 us (3%)
    ppermute x33, starting transfers between devices, swap_bit(): return lax.ppermute(value, axis, [(i, i ^ bit) for i in range(count)])  46.2 us
    ppermute x33, waiting for transfers between devices, swap_bit(): return lax.ppermute(value, axis, [(i, i ^ bit) for i in range(count)])  45.2 us
    pallas_call x5, Pallas kernels, call(): pl.pallas_call(body, name=name, grid=(1,), out_shape=[jax.ShapeDtypeStruc...  38.1 us
    ppermute x2, starting transfers between devices, beyond(): return lax.ppermute(value, 'sp', hops)  7.74 us
    ppermute x2, waiting for transfers between devices, beyond(): return lax.ppermute(value, 'sp', hops)  4.49 us
  transfers between devices with their start and end apart: 35, of which 19 were waited for; matrix products, arithmetic and copies ran while one was open for 5% of the time, Pallas kernels for 17%

profile of v3, /device:TPU:0, one launch (start us, length us, event | category | flops | bytes accessed | tf_op | source)
XLA Modules:
  0.0 153.8 jit_solution(14286675755065893929)
XLA Ops:
  0.6 3.0 %collective-permute-start = (bf16[2,256,512]{2,1,0:T(8,128)(2,1)}, bf16[2,256,512]{2,1,0:T(8,128)(2,1)S(1)}, u32[]{:S(2)}, u32[]{:S(2)}) collective-permute-start(bf16[2,256,512]{2,1,0:T(8,128)(2,1)} %bitcast.43), channel_id=1, source_target_pairs={{0,4},{4,0},{8,12},{12,8},{16,20},{20,16},{24,28},{28,24},{1,5},{5... | collective-permute-start | bytes 1572872 | tf_op jit(solution)/shard_map/ppermute | solution.py:21
  3.7 5.3 %first.1 = (bf16[512,1536]{1,0:T(8,128)(2,1)}, bf16[512,512]{1,0:T(8,128)(2,1)}, f32[72,512]{1,0:T(8,128)}) custom-call(bf16[512,512]{1,0:T(8,128)(2,1)} %bitcast.44, f32[1,512]{1,0:T(1,128)} %bitcast.59, bf16[512,1536]{1,0:T(8,128)(2,1)} %w_ref.3), custom_call_target="tpu_custom_call" | custom-call | tf_op jit(solution)/shard_map/first/pallas_call | solution.py:479
  9.1 9.9 %collective-permute-done.1 = f32[72,512]{1,0:T(8,128)S(1)} collective-permute-done((f32[72,512]{1,0:T(8,128)}, f32[72,512]{1,0:T(8,128)S(1)}, u32[]{:S(2)}, u32[]{:S(2)}) %collective-permute-start.1) | collective-permute-done | bytes 147488 | tf_op jit(solution)/shard_map/ppermute | solution.py:21
  19.0 0.9 add.144
  19.9 1.8 %collective-permute-start.2 = (bf16[2,256,512]{2,1,0:T(8,128)(2,1)S(1)}, bf16[2,256,512]{2,1,0:T(8,128)(2,1)S(1)}, u32[]{:S(2)}, u32[]{:S(2)}) collective-permute-start(bf16[2,256,512]{2,1,0:T(8,128)(2,1)S(1)} %bitcast.57), channel_id=1, source_target_pairs={{0,4},{4,0},{8,12},{12,8},{16,20},{20,16},{24,28},{28,24},{1,5},{5... | collective-permute-start | bytes 1572872 | tf_op jit(solution)/shard_map/ppermute | solution.py:21
  21.7 1.6 %collective-permute-start.3 = (f32[72,512]{1,0:T(8,128)S(1)}, f32[72,512]{1,0:T(8,128)S(1)}, u32[]{:S(2)}, u32[]{:S(2)}) collective-permute-start(f32[72,512]{1,0:T(8,128)S(1)} %add.144), channel_id=1, source_target_pairs={{0,8},{4,12},{8,0},{12,4},{16,24},{20,28},{24,16},{28,20},{1,9},{5... | collective-permute-start | bytes 442376 | tf_op jit(solution)/shard_map/ppermute | solution.py:21
  23.3 3.6 %collective-permute-done.3 = f32[72,512]{1,0:T(8,128)S(1)} collective-permute-done((f32[72,512]{1,0:T(8,128)S(1)}, f32[72,512]{1,0:T(8,128)S(1)}, u32[]{:S(2)}, u32[]{:S(2)}) %collective-permute-start.3) | collective-permute-done | bytes 147488 | tf_op jit(solution)/shard_map/ppermute | solution.py:21
  26.9 2.7 %collective-permute-start.4 = (f32[72,512]{1,0:T(8,128)S(1)}, f32[72,512]{1,0:T(8,128)S(1)}, u32[]{:S(2)}, u32[]{:S(2)}) collective-permute-start(f32[72,512]{1,0:T(8,128)S(1)} %add.145), channel_id=1, source_target_pairs={{0,16},{4,20},{8,24},{12,28},{16,0},{20,4},{24,8},{28,12},{1,17},{... | collective-permute-start | bytes 442376 | tf_op jit(solution)/shard_map/ppermute | solution.py:21
  29.6 3.5 %collective-permute-start.6 = (bf16[2,256,512]{2,1,0:T(8,128)(2,1)S(1)}, bf16[2,256,512]{2,1,0:T(8,128)(2,1)S(1)}, u32[]{:S(2)}, u32[]{:S(2)}) collective-permute-start(bf16[2,256,512]{2,1,0:T(8,128)(2,1)S(1)} %collective-permute-done.near_ref), channel_id=1, source_target_pairs={{12,4},{20,12},{28,20},{0,8},{8,16},{16,24},{13,5},{21,13},{29,21}... | collective-permute-start | bytes 1572872 | tf_op jit(solution)/shard_map/ppermute | solution.py:498
  33.1 1.6 %collective-permute-done.4 = f32[72,512]{1,0:T(8,128)S(1)} collective-permute-done((f32[72,512]{1,0:T(8,128)S(1)}, f32[72,512]{1,0:T(8,128)S(1)}, u32[]{:S(2)}, u32[]{:S(2)}) %collective-permute-start.4) | collective-permute-done | bytes 147488 | tf_op jit(solution)/shard_map/ppermute | solution.py:21
  34.6 0.7 add.146.pack_ref
  35.3 4.2 %collective-permute-start.5 = (bf16[2,256,512]{2,1,0:T(8,128)(2,1)S(1)}, bf16[2,256,512]{2,1,0:T(8,128)(2,1)S(1)}, u32[]{:S(2)}, u32[]{:S(2)}) collective-permute-start(bf16[2,256,512]{2,1,0:T(8,128)(2,1)S(1)} %collective-permute-done.2.near_ref), channel_id=1, source_target_pairs={{12,4},{20,12},{28,20},{0,8},{8,16},{16,24},{13,5},{21,13},{29,21}... | collective-permute-start | bytes 1572872 | tf_op jit(solution)/shard_map/ppermute | solution.py:498
  39.6 0.6 reshape.47.kernel_ref
  40.3 0.6 pad_add_fusion.edge_ref
  40.9 4.5 %collective-permute-done.6.far_ref = bf16[2,256,512]{2,1,0:T(8,128)(2,1)S(1)} collective-permute-done((bf16[2,256,512]{2,1,0:T(8,128)(2,1)S(1)}, bf16[2,256,512]{2,1,0:T(8,128)(2,1)S(1)}, u32[]{:S(2)}, u32[]{:S(2)}) %collective-permute-start.6) | collective-permute-done | bytes 524320 | tf_op jit(solution)/shard_map/ppermute | solution.py:498
  45.3 0.8 copy-done.2
  46.1 10.7 %attend.1 = (bf16[512,512]{1,0:T(8,128)(2,1)}, f32[512,512]{1,0:T(8,128)}, bf16[512,512]{1,0:T(8,128)(2,1)}, bf16[4,256,512]{2,1,0:T(8,128)(2,1)}, bf16[2,256,512]{2,1,0:T(8,128)(2,1)}, /*index=5*/f32[4,256,512]{2,1,0:T(8,128)}) custom-call(s32[4]{0:T(128)} %pad_add_fusion.edge_ref, f32[8]{0:T(128)} %sharp_ref.5, f32[72,512]{1,0:T(8,128)} %add.146.pack_ref, ...), custom_call_target="tpu_custom_call" | custom-call | tf_op jit(solution)/shard_map/attend/pallas_call | solution.py:479
  56.9 0.8 copy-done.5
  57.7 12.0 %back.1 = (f32[64,512]{1,0:T(8,128)}, f32[24,512]{1,0:T(8,128)}, f32[512,512]{1,0:T(8,128)}, bf16[512,512]{1,0:T(8,128)(2,1)}, bf16[2,128,1024]{2,1,0:T(8,128)(2,1)}, /*index=5*/bf16[2,128,1024]{2,1,0:T(8,128)(2,1)}) custom-call(s32[4]{0:T(128)} %pad_add_fusion.edge_ref, f32[8]{0:T(128)} %sharp_ref.5, f32[72,512]{1,0:T(8,128)} %add.146.pack_ref, ...), custom_call_target="tpu_custom_call" | custom-call | tf_op jit(solution)/shard_map/back/pallas_call | solution.py:479
  69.8 1.5 collective-permute-start.7
  71.3 4.6 %collective-permute-done.7 = f32[64,512]{1,0:T(8,128)S(1)} collective-permute-done((f32[64,512]{1,0:T(8,128)}, f32[64,512]{1,0:T(8,128)S(1)}, u32[]{:S(2)}, u32[]{:S(2)}) %collective-permute-start.7) | collective-permute-done | bytes 131104 | tf_op jit(solution)/shard_map/ppermute | solution.py:21
  75.9 0.9 add.147
  76.8 2.9 %collective-permute-start.8 = (f32[64,512]{1,0:T(8,128)S(1)}, f32[64,512]{1,0:T(8,128)S(1)}, u32[]{:S(2)}, u32[]{:S(2)}) collective-permute-start(f32[64,512]{1,0:T(8,128)S(1)} %add.147), channel_id=1, source_target_pairs={{0,8},{4,12},{8,0},{12,4},{16,24},{20,28},{24,16},{28,20},{1,9},{5... | collective-permute-start | bytes 393224 | tf_op jit(solution)/shard_map/ppermute | solution.py:21
  79.7 1.2 add_convert_fusion
  81.0 1.6 %collective-permute-start.21 = (bf16[1,128,1024]{2,1,0:T(8,128)(2,1)S(1)}, bf16[1,128,1024]{2,1,0:T(8,128)(2,1)S(1)}, u32[]{:S(2)}, u32[]{:S(2)}) collective-permute-start(bf16[1,128,1024]{2,1,0:T(8,128)(2,1)S(1)} %constant_dynamic-slice_fusion), channel_id=1, source_target_pairs={{0,2},{1,3},{2,0},{3,1},{4,6},{5,7},{6,4},{7,5},{8,10},{9,11},{10,... | collective-permute-start | bytes 786440 | tf_op jit(solution)/shard_map/ppermute | solution.py:21
  82.6 0.4 collective-permute-done.8
  83.0 3.7 %collective-permute-start.9 = (f32[64,512]{1,0:T(8,128)S(1)}, f32[64,512]{1,0:T(8,128)S(1)}, u32[]{:S(2)}, u32[]{:S(2)}) collective-permute-start(f32[64,512]{1,0:T(8,128)S(1)} %add.148), channel_id=1, source_target_pairs={{0,16},{4,20},{8,24},{12,28},{16,0},{20,4},{24,8},{28,12},{1,17},{... | collective-permute-start | bytes 393224 | tf_op jit(solution)/shard_map/ppermute | solution.py:21
  86.7 1.2 collective-permute-done.30
  87.9 1.6 %collective-permute-start.31 = (f32[24,512]{1,0:T(8,128)S(1)}, f32[24,512]{1,0:T(8,128)S(1)}, u32[]{:S(2)}, u32[]{:S(2)}) collective-permute-start(f32[24,512]{1,0:T(8,128)S(1)} %add.174), channel_id=1, source_target_pairs={{0,2},{1,3},{2,0},{3,1},{4,6},{5,7},{6,4},{7,5},{8,10},{9,11},{10,... | collective-permute-start | bytes 147464 | tf_op jit(solution)/shard_map/ppermute | solution.py:21
  89.5 2.4 %collective-permute-done.9 = f32[64,512]{1,0:T(8,128)S(1)} collective-permute-done((f32[64,512]{1,0:T(8,128)S(1)}, f32[64,512]{1,0:T(8,128)S(1)}, u32[]{:S(2)}, u32[]{:S(2)}) %collective-permute-start.9) | collective-permute-done | bytes 131104 | tf_op jit(solution)/shard_map/ppermute | solution.py:21
  91.9 0.7 add.149.prob_ref
  92.5 4.5 %gram.1 = (bf16[512,1024]{1,0:T(8,128)(2,1)}, bf16[2,128,1024]{2,1,0:T(8,128)(2,1)}, bf16[2,128,1024]{2,1,0:T(8,128)(2,1)}) custom-call(s32[4]{0:T(128)} %pad_add_fusion.edge_ref, f32[8]{0:T(128)} %sharp_ref.5, f32[72,512]{1,0:T(8,128)} %add.146.pack_ref, f32[64,512]{1,0:T(8,128)} %add.149.prob_ref, bf16[512,1536]{1,0:T(8,128)(2,1)} %get-tuple-element.36.value_ref.mixed_ref, ...), custom_call_target="tpu_custom_call" | custom-call | tf_op jit(solution)/shard_map/gram/pallas_call | solution.py:479
  97.2 0.9 collective-permute-start.22
  98.1 1.3 collective-permute-start.32
  99.4 4.8 %collective-permute-done.32 = f32[24,512]{1,0:T(8,128)S(1)} collective-permute-done((f32[24,512]{1,0:T(8,128)S(1)}, f32[24,512]{1,0:T(8,128)S(1)}, u32[]{:S(2)}, u32[]{:S(2)}) %collective-permute-start.32) | collective-permute-done | bytes 49184 | tf_op jit(solution)/shard_map/ppermute | solution.py:21
  104.4 4.0 %collective-permute-done.33 = f32[24,512]{1,0:T(8,128)S(1)} collective-permute-done((f32[24,512]{1,0:T(8,128)S(1)}, f32[24,512]{1,0:T(8,128)S(1)}, u32[]{:S(2)}, u32[]{:S(2)}) %collective-permute-start.33) | collective-permute-done | bytes 49184 | tf_op jit(solution)/shard_map/ppermute | solution.py:21
  108.4 1.3 collective-permute-start.34
  110.0 1.6 %collective-permute-start.11 = (bf16[1,128,1024]{2,1,0:T(8,128)(2,1)S(1)}, bf16[1,128,1024]{2,1,0:T(8,128)(2,1)S(1)}, u32[]{:S(2)}, u32[]{:S(2)}) collective-permute-start(bf16[1,128,1024]{2,1,0:T(8,128)(2,1)S(1)} %constant_dynamic-slice_fusion.1), channel_id=1, source_target_pairs={{0,2},{1,3},{2,0},{3,1},{4,6},{5,7},{6,4},{7,5},{8,10},{9,11},{10,... | collective-permute-start | bytes 786440 | tf_op jit(solution)/shard_map/ppermute | solution.py:21
  111.5 2.1 %collective-permute-start.23 = (bf16[16,1024]{1,0:T(8,128)(2,1)S(1)}, bf16[16,1024]{1,0:T(8,128)(2,1)S(1)}, u32[]{:S(2)}, u32[]{:S(2)}) collective-permute-start(bf16[16,1024]{1,0:T(8,128)(2,1)S(1)} %get-tuple-element.80), channel_id=1, source_target_pairs={{0,8},{4,12},{8,0},{12,4},{16,24},{20,28},{24,16},{28,20},{1,9},{5... | collective-permute-start | bytes 98312 | tf_op jit(solution)/shard_map/ppermute | solution.py:21
  113.7 2.4 %collective-permute-start.25 = (bf16[16,1024]{1,0:T(8,128)(2,1)S(1)}, bf16[16,1024]{1,0:T(8,128)(2,1)S(1)}, u32[]{:S(2)}, u32[]{:S(2)}) collective-permute-start(bf16[16,1024]{1,0:T(8,128)(2,1)S(1)} %get-tuple-element.81), channel_id=1, source_target_pairs={{0,24},{4,28},{8,16},{12,20},{16,8},{20,12},{24,0},{28,4},{1,25},{... | collective-permute-start | bytes 98312 | tf_op jit(solution)/shard_map/ppermute | solution.py:21
  116.1 0.6 slice.19
  116.7 0.6 copy.17
  117.3 5.4 %input.1 = bf16[512,512]{1,0:T(8,128)(2,1)} custom-call(bf16[512,512]{1,0:T(8,128)(2,1)} %bitcast.46, f32[1,512]{1,0:T(1,128)} %bitcast.61, bf16[512,1536]{1,0:T(8,128)(2,1)} %w_ref.3, bf16[512,1024]{1,0:T(8,128)(2,1)} %get-tuple-element.45.d_qk_ref, bf16[512,512]{1,0:T(8,128)(2,1)} %get-tuple-element.46.d_value_ref, f32[512,512]{1,0:T(8,128)} %get-tuple-element.47.d_res_ref), custom_call_target="tpu_custom_call" | custom-call | tf_op jit(solution)/shard_map/input/pallas_call | solution.py:479
  122.8 1.5 collective-permute-start.26
  124.3 1.1 collective-permute-start.27
  125.4 1.9 %collective-permute-start.28 = (bf16[16,1024]{1,0:T(8,128)(2,1)S(1)}, bf16[16,1024]{1,0:T(8,128)(2,1)S(1)}, u32[]{:S(2)}, u32[]{:S(2)}) collective-permute-start(bf16[16,1024]{1,0:T(8,128)(2,1)S(1)} %fusion.4), channel_id=1, source_target_pairs={{0,8},{4,12},{8,0},{12,4},{16,24},{20,28},{24,16},{28,20},{1,9},{5... | collective-permute-start | bytes 98312 | tf_op jit(solution)/shard_map/ppermute | solution.py:21
  127.4 0.9 collective-permute-start.12
  128.3 0.3 collective-permute-done.26
  128.6 0.8 collective-permute-done.27
  129.4 0.2 collective-permute-done.28
  129.7 0.9 collective-permute-start.29
  130.6 1.8 %collective-permute-done.12 = bf16[64,1024]{1,0:T(8,128)(2,1)S(1)} collective-permute-done((bf16[64,1024]{1,0:T(8,128)(2,1)S(1)}, bf16[64,1024]{1,0:T(8,128)(2,1)S(1)}, u32[]{:S(2)}, u32[]{:S(2)}) %collective-permute-start.12) | collective-permute-done | bytes 131104 | tf_op jit(solution)/shard_map/ppermute | solution.py:21
  132.7 1.8 %collective-permute-start.14 = (bf16[16,1024]{1,0:T(8,128)(2,1)S(1)}, bf16[16,1024]{1,0:T(8,128)(2,1)S(1)}, u32[]{:S(2)}, u32[]{:S(2)}) collective-permute-start(bf16[16,1024]{1,0:T(8,128)(2,1)S(1)} %get-tuple-element.75), channel_id=1, source_target_pairs={{0,16},{4,20},{8,24},{12,28},{16,0},{20,4},{24,8},{28,12},{1,17},{... | collective-permute-start | bytes 98312 | tf_op jit(solution)/shard_map/ppermute | solution.py:21
  134.5 2.4 %collective-permute-start.15 = (bf16[16,1024]{1,0:T(8,128)(2,1)S(1)}, bf16[16,1024]{1,0:T(8,128)(2,1)S(1)}, u32[]{:S(2)}, u32[]{:S(2)}) collective-permute-start(bf16[16,1024]{1,0:T(8,128)(2,1)S(1)} %get-tuple-element.74), channel_id=1, source_target_pairs={{0,24},{4,28},{8,16},{12,20},{16,8},{20,12},{24,0},{28,4},{1,25},{... | collective-permute-start | bytes 98312 | tf_op jit(solution)/shard_map/ppermute | solution.py:21
  137.0 0.5 collective-permute-done.14
  137.5 2.8 %collective-permute-done.15 = bf16[16,1024]{1,0:T(8,128)(2,1)S(1)} collective-permute-done((bf16[16,1024]{1,0:T(8,128)(2,1)S(1)}, bf16[16,1024]{1,0:T(8,128)(2,1)S(1)}, u32[]{:S(2)}, u32[]{:S(2)}) %collective-permute-start.15) | collective-permute-done | bytes 32800 | tf_op jit(solution)/shard_map/ppermute | solution.py:21
  140.3 2.6 %collective-permute-start.16 = (bf16[16,1024]{1,0:T(8,128)(2,1)S(1)}, bf16[16,1024]{1,0:T(8,128)(2,1)S(1)}, u32[]{:S(2)}, u32[]{:S(2)}) collective-permute-start(bf16[16,1024]{1,0:T(8,128)(2,1)S(1)} %fusion.7), channel_id=1, source_target_pairs={{0,24},{4,28},{8,16},{12,20},{16,8},{20,12},{24,0},{28,4},{1,25},{... | collective-permute-start | bytes 98312 | tf_op jit(solution)/shard_map/ppermute | solution.py:21
  142.9 1.9 %collective-permute-start.18 = (bf16[16,1024]{1,0:T(8,128)(2,1)S(1)}, bf16[16,1024]{1,0:T(8,128)(2,1)S(1)}, u32[]{:S(2)}, u32[]{:S(2)}) collective-permute-start(bf16[16,1024]{1,0:T(8,128)(2,1)S(1)} %fusion.7), channel_id=1, source_target_pairs={{0,8},{4,12},{8,0},{12,4},{16,24},{20,28},{24,16},{28,20},{1,9},{5... | collective-permute-start | bytes 98312 | tf_op jit(solution)/shard_map/ppermute | solution.py:21
  144.8 1.3 collective-permute-done.16
  146.1 1.6 %collective-permute-done.17 = bf16[16,1024]{1,0:T(8,128)(2,1)S(1)} collective-permute-done((bf16[16,1024]{1,0:T(8,128)(2,1)S(1)}, bf16[16,1024]{1,0:T(8,128)(2,1)S(1)}, u32[]{:S(2)}, u32[]{:S(2)}) %collective-permute-start.17) | collective-permute-done | bytes 32800 | tf_op jit(solution)/shard_map/ppermute | solution.py:21
  147.8 0.9 collective-permute-start.19
  148.7 0.7 fusion.8
  149.4 3.4 %collective-permute-done.19 = bf16[64,1024]{1,0:T(8,128)(2,1)S(1)} collective-permute-done((bf16[64,1024]{1,0:T(8,128)(2,1)S(1)}, bf16[64,1024]{1,0:T(8,128)(2,1)S(1)}, u32[]{:S(2)}, u32[]{:S(2)}) %collective-permute-start.19) | collective-permute-done | bytes 131104 | tf_op jit(solution)/shard_map/ppermute | solution.py:21
  152.9 0.9 pad_maximum_fusion
  (68 shorter events, 1.4 us)
Async XLA Ops:
  0.6 19.3 %copy-start.3 = (bf16[1,2,256,512]{3,2,1,0:T(8,128)(2,1)S(1)}, bf16[1,2,256,512]{3,2,1,0:T(8,128)(2,1)}, u32[]{:S(2)}) copy-start(bf16[1,2,256,512]{3,2,1,0:T(8,128)(2,1)} %param.10) | copy-start | bytes 1572868
  0.6 19.3 %collective-permute-start = (bf16[2,256,512]{2,1,0:T(8,128)(2,1)}, bf16[2,256,512]{2,1,0:T(8,128)(2,1)S(1)}, u32[]{:S(2)}, u32[]{:S(2)}) collective-permute-start(bf16[2,256,512]{2,1,0:T(8,128)(2,1)} %bitcast.43), channel_id=1, source_target_pairs={{0,4},{4,0},{8,12},{12,8},{16,20},{20,16},{24,28},{28,24},{1,5},{5... | collective-permute-start | bytes 1572872 | tf_op jit(solution)/shard_map/ppermute | solution.py:21
  3.7 35.9 %copy-start.7 = (f32[2,3,3,512]{3,0,2,1:T(2,128)S(1)}, f32[2,3,3,512]{3,0,2,1:T(2,128)}, u32[]{:S(2)}) copy-start(f32[2,3,3,512]{3,0,2,1:T(2,128)} %param.17) | copy-start | bytes 110596
  9.0 10.0 %collective-permute-start.1 = (f32[72,512]{1,0:T(8,128)}, f32[72,512]{1,0:T(8,128)S(1)}, u32[]{:S(2)}, u32[]{:S(2)}) collective-permute-start(f32[72,512]{1,0:T(8,128)} %get-tuple-element.29), channel_id=1, source_target_pairs={{0,4},{4,0},{8,12},{12,8},{16,20},{20,16},{24,28},{28,24},{1,5},{5... | collective-permute-start | bytes 442376 | tf_op jit(solution)/shard_map/ppermute | solution.py:21
  19.9 25.4 %copy-start.1 = (bf16[2,256,512]{2,1,0:T(8,128)(2,1)}, bf16[2,256,512]{2,1,0:T(8,128)(2,1)S(1)}, u32[]{:S(2)}) copy-start(bf16[2,256,512]{2,1,0:T(8,128)(2,1)S(1)} %collective-permute-done.near_ref) | copy-start | bytes 1572868
  19.9 15.4 %collective-permute-start.2 = (bf16[2,256,512]{2,1,0:T(8,128)(2,1)S(1)}, bf16[2,256,512]{2,1,0:T(8,128)(2,1)S(1)}, u32[]{:S(2)}, u32[]{:S(2)}) collective-permute-start(bf16[2,256,512]{2,1,0:T(8,128)(2,1)S(1)} %bitcast.57), channel_id=1, source_target_pairs={{0,4},{4,0},{8,12},{12,8},{16,20},{20,16},{24,28},{28,24},{1,5},{5... | collective-permute-start | bytes 1572872 | tf_op jit(solution)/shard_map/ppermute | solution.py:21
  21.7 5.1 %collective-permute-start.3 = (f32[72,512]{1,0:T(8,128)S(1)}, f32[72,512]{1,0:T(8,128)S(1)}, u32[]{:S(2)}, u32[]{:S(2)}) collective-permute-start(f32[72,512]{1,0:T(8,128)S(1)} %add.144), channel_id=1, source_target_pairs={{0,8},{4,12},{8,0},{12,4},{16,24},{20,28},{24,16},{28,20},{1,9},{5... | collective-permute-start | bytes 442376 | tf_op jit(solution)/shard_map/ppermute | solution.py:21
  26.9 7.7 %collective-permute-start.4 = (f32[72,512]{1,0:T(8,128)S(1)}, f32[72,512]{1,0:T(8,128)S(1)}, u32[]{:S(2)}, u32[]{:S(2)}) collective-permute-start(f32[72,512]{1,0:T(8,128)S(1)} %add.145), channel_id=1, source_target_pairs={{0,16},{4,20},{8,24},{12,28},{16,0},{20,4},{24,8},{28,12},{1,17},{... | collective-permute-start | bytes 442376 | tf_op jit(solution)/shard_map/ppermute | solution.py:21
  29.6 15.8 %collective-permute-start.6 = (bf16[2,256,512]{2,1,0:T(8,128)(2,1)S(1)}, bf16[2,256,512]{2,1,0:T(8,128)(2,1)S(1)}, u32[]{:S(2)}, u32[]{:S(2)}) collective-permute-start(bf16[2,256,512]{2,1,0:T(8,128)(2,1)S(1)} %collective-permute-done.near_ref), channel_id=1, source_target_pairs={{12,4},{20,12},{28,20},{0,8},{8,16},{16,24},{13,5},{21,13},{29,21}... | collective-permute-start | bytes 1572872 | tf_op jit(solution)/shard_map/ppermute | solution.py:498
  35.3 21.6 %copy-start.4 = (bf16[2,256,512]{2,1,0:T(8,128)(2,1)}, bf16[2,256,512]{2,1,0:T(8,128)(2,1)S(1)}, u32[]{:S(2)}) copy-start(bf16[2,256,512]{2,1,0:T(8,128)(2,1)S(1)} %collective-permute-done.2.near_ref) | copy-start | bytes 1572868
  35.3 21.5 %collective-permute-start.5 = (bf16[2,256,512]{2,1,0:T(8,128)(2,1)S(1)}, bf16[2,256,512]{2,1,0:T(8,128)(2,1)S(1)}, u32[]{:S(2)}, u32[]{:S(2)}) collective-permute-start(bf16[2,256,512]{2,1,0:T(8,128)(2,1)S(1)} %collective-permute-done.2.near_ref), channel_id=1, source_target_pairs={{12,4},{20,12},{28,20},{0,8},{8,16},{16,24},{13,5},{21,13},{29,21}... | collective-permute-start | bytes 1572872 | tf_op jit(solution)/shard_map/ppermute | solution.py:498
  45.3 0.8 copy-start.2
  56.9 0.8 copy-start.5
  69.7 17.0 %copy-start.6 = (f32[24,512]{1,0:T(8,128)S(1)}, f32[24,512]{1,0:T(8,128)}, u32[]{:S(2)}) copy-start(f32[24,512]{1,0:T(8,128)} %get-tuple-element.52) | copy-start | bytes 147460
  69.7 10.0 %collective-permute-start.20 = (bf16[2,128,1024]{2,1,0:T(8,128)(2,1)}, bf16[2,128,1024]{2,1,0:T(8,128)(2,1)S(1)}, u32[]{:S(2)}, u32[]{:S(2)}) collective-permute-start(bf16[2,128,1024]{2,1,0:T(8,128)(2,1)} %get-tuple-element.51), channel_id=1, source_target_pairs={{0,1},{1,0},{2,3},{3,2},{4,5},{5,4},{6,7},{7,6},{8,9},{9,8},{10,11... | collective-permute-start | bytes 1572872 | tf_op jit(solution)/shard_map/ppermute | solution.py:21
  69.8 6.1 %collective-permute-start.7 = (f32[64,512]{1,0:T(8,128)}, f32[64,512]{1,0:T(8,128)S(1)}, u32[]{:S(2)}, u32[]{:S(2)}) collective-permute-start(f32[64,512]{1,0:T(8,128)} %get-tuple-element.44), channel_id=1, source_target_pairs={{0,4},{4,0},{8,12},{12,8},{16,20},{20,16},{24,28},{28,24},{1,5},{5... | collective-permute-start | bytes 393224 | tf_op jit(solution)/shard_map/ppermute | solution.py:21
  76.8 6.2 %collective-permute-start.8 = (f32[64,512]{1,0:T(8,128)S(1)}, f32[64,512]{1,0:T(8,128)S(1)}, u32[]{:S(2)}, u32[]{:S(2)}) collective-permute-start(f32[64,512]{1,0:T(8,128)S(1)} %add.147), channel_id=1, source_target_pairs={{0,8},{4,12},{8,0},{12,4},{16,24},{20,28},{24,16},{28,20},{1,9},{5... | collective-permute-start | bytes 393224 | tf_op jit(solution)/shard_map/ppermute | solution.py:21
  81.0 16.1 %collective-permute-start.21 = (bf16[1,128,1024]{2,1,0:T(8,128)(2,1)S(1)}, bf16[1,128,1024]{2,1,0:T(8,128)(2,1)S(1)}, u32[]{:S(2)}, u32[]{:S(2)}) collective-permute-start(bf16[1,128,1024]{2,1,0:T(8,128)(2,1)S(1)} %constant_dynamic-slice_fusion), channel_id=1, source_target_pairs={{0,2},{1,3},{2,0},{3,1},{4,6},{5,7},{6,4},{7,5},{8,10},{9,11},{10,... | collective-permute-start | bytes 786440 | tf_op jit(solution)/shard_map/ppermute | solution.py:21
  83.0 8.9 %collective-permute-start.9 = (f32[64,512]{1,0:T(8,128)S(1)}, f32[64,512]{1,0:T(8,128)S(1)}, u32[]{:S(2)}, u32[]{:S(2)}) collective-permute-start(f32[64,512]{1,0:T(8,128)S(1)} %add.148), channel_id=1, source_target_pairs={{0,16},{4,20},{8,24},{12,28},{16,0},{20,4},{24,8},{28,12},{1,17},{... | collective-permute-start | bytes 393224 | tf_op jit(solution)/shard_map/ppermute | solution.py:21
  86.7 1.2 collective-permute-start.30
  87.9 10.2 %collective-permute-start.31 = (f32[24,512]{1,0:T(8,128)S(1)}, f32[24,512]{1,0:T(8,128)S(1)}, u32[]{:S(2)}, u32[]{:S(2)}) collective-permute-start(f32[24,512]{1,0:T(8,128)S(1)} %add.174), channel_id=1, source_target_pairs={{0,2},{1,3},{2,0},{3,1},{4,6},{5,7},{6,4},{7,5},{8,10},{9,11},{10,... | collective-permute-start | bytes 147464 | tf_op jit(solution)/shard_map/ppermute | solution.py:21
  97.1 12.6 %copy-start = (bf16[2,128,1024]{2,1,0:T(8,128)(2,1)S(1)}, bf16[2,128,1024]{2,1,0:T(8,128)(2,1)}, u32[]{:S(2)}) copy-start(bf16[2,128,1024]{2,1,0:T(8,128)(2,1)} %get-tuple-element.48) | copy-start | bytes 1572868
  97.1 12.6 %collective-permute-start.10 = (bf16[2,128,1024]{2,1,0:T(8,128)(2,1)}, bf16[2,128,1024]{2,1,0:T(8,128)(2,1)S(1)}, u32[]{:S(2)}, u32[]{:S(2)}) collective-permute-start(bf16[2,128,1024]{2,1,0:T(8,128)(2,1)} %get-tuple-element.49), channel_id=1, source_target_pairs={{0,1},{1,0},{2,3},{3,2},{4,5},{5,4},{6,7},{7,6},{8,9},{9,8},{10,11... | collective-permute-start | bytes 1572872 | tf_op jit(solution)/shard_map/ppermute | solution.py:21
  97.2 12.4 %collective-permute-start.22 = (bf16[64,1024]{1,0:T(8,128)(2,1)S(1)}, bf16[64,1024]{1,0:T(8,128)(2,1)S(1)}, u32[]{:S(2)}, u32[]{:S(2)}) collective-permute-start(bf16[64,1024]{1,0:T(8,128)(2,1)S(1)} %dynamic-slice_bitcast_fusion), channel_id=1, source_target_pairs={{0,4},{4,0},{8,12},{12,8},{16,20},{20,16},{24,28},{28,24},{1,5},{5... | collective-permute-start | bytes 393224 | tf_op jit(solution)/shard_map/ppermute | solution.py:21
  98.1 6.1 %collective-permute-start.32 = (f32[24,512]{1,0:T(8,128)S(1)}, f32[24,512]{1,0:T(8,128)S(1)}, u32[]{:S(2)}, u32[]{:S(2)}) collective-permute-start(f32[24,512]{1,0:T(8,128)S(1)} %add.175), channel_id=1, source_target_pairs={{0,4},{4,0},{8,12},{12,8},{16,20},{20,16},{24,28},{28,24},{1,5},{5... | collective-permute-start | bytes 147464 | tf_op jit(solution)/shard_map/ppermute | solution.py:21
  104.2 4.2 %collective-permute-start.33 = (f32[24,512]{1,0:T(8,128)S(1)}, f32[24,512]{1,0:T(8,128)S(1)}, u32[]{:S(2)}, u32[]{:S(2)}) collective-permute-start(f32[24,512]{1,0:T(8,128)S(1)} %add.176), channel_id=1, source_target_pairs={{0,8},{4,12},{8,0},{12,4},{16,24},{20,28},{24,16},{28,20},{1,9},{5... | collective-permute-start | bytes 147464 | tf_op jit(solution)/shard_map/ppermute | solution.py:21
  108.4 7.7 %collective-permute-start.34 = (f32[24,512]{1,0:T(8,128)S(1)}, f32[24,512]{1,0:T(8,128)S(1)}, u32[]{:S(2)}, u32[]{:S(2)}) collective-permute-start(f32[24,512]{1,0:T(8,128)S(1)} %add.177), channel_id=1, source_target_pairs={{0,16},{4,20},{8,24},{12,28},{16,0},{20,4},{24,8},{28,12},{1,17},{... | collective-permute-start | bytes 147464 | tf_op jit(solution)/shard_map/ppermute | solution.py:21
  110.0 17.3 %collective-permute-start.11 = (bf16[1,128,1024]{2,1,0:T(8,128)(2,1)S(1)}, bf16[1,128,1024]{2,1,0:T(8,128)(2,1)S(1)}, u32[]{:S(2)}, u32[]{:S(2)}) collective-permute-start(bf16[1,128,1024]{2,1,0:T(8,128)(2,1)S(1)} %constant_dynamic-slice_fusion.1), channel_id=1, source_target_pairs={{0,2},{1,3},{2,0},{3,1},{4,6},{5,7},{6,4},{7,5},{8,10},{9,11},{10,... | collective-permute-start | bytes 786440 | tf_op jit(solution)/shard_map/ppermute | solution.py:21
  111.5 11.2 %collective-permute-start.23 = (bf16[16,1024]{1,0:T(8,128)(2,1)S(1)}, bf16[16,1024]{1,0:T(8,128)(2,1)S(1)}, u32[]{:S(2)}, u32[]{:S(2)}) collective-permute-start(bf16[16,1024]{1,0:T(8,128)(2,1)S(1)} %get-tuple-element.80), channel_id=1, source_target_pairs={{0,8},{4,12},{8,0},{12,4},{16,24},{20,28},{24,16},{28,20},{1,9},{5... | collective-permute-start | bytes 98312 | tf_op jit(solution)/shard_map/ppermute | solution.py:21
  113.6 9.2 %collective-permute-start.24 = (bf16[16,1024]{1,0:T(8,128)(2,1)S(1)}, bf16[16,1024]{1,0:T(8,128)(2,1)S(1)}, u32[]{:S(2)}, u32[]{:S(2)}) collective-permute-start(bf16[16,1024]{1,0:T(8,128)(2,1)S(1)} %get-tuple-element.82), channel_id=1, source_target_pairs={{0,16},{4,20},{8,24},{12,28},{16,0},{20,4},{24,8},{28,12},{1,17},{... | collective-permute-start | bytes 98312 | tf_op jit(solution)/shard_map/ppermute | solution.py:21
  113.7 9.1 %collective-permute-start.25 = (bf16[16,1024]{1,0:T(8,128)(2,1)S(1)}, bf16[16,1024]{1,0:T(8,128)(2,1)S(1)}, u32[]{:S(2)}, u32[]{:S(2)}) collective-permute-start(bf16[16,1024]{1,0:T(8,128)(2,1)S(1)} %get-tuple-element.81), channel_id=1, source_target_pairs={{0,24},{4,28},{8,16},{12,20},{16,8},{20,12},{24,0},{28,4},{1,25},{... | collective-permute-start | bytes 98312 | tf_op jit(solution)/shard_map/ppermute | solution.py:21
  122.8 5.8 %collective-permute-start.26 = (bf16[16,1024]{1,0:T(8,128)(2,1)S(1)}, bf16[16,1024]{1,0:T(8,128)(2,1)S(1)}, u32[]{:S(2)}, u32[]{:S(2)}) collective-permute-start(bf16[16,1024]{1,0:T(8,128)(2,1)S(1)} %fusion.4), channel_id=1, source_target_pairs={{0,24},{4,28},{8,16},{12,20},{16,8},{20,12},{24,0},{28,4},{1,25},{... | collective-permute-start | bytes 98312 | tf_op jit(solution)/shard_map/ppermute | solution.py:21
  124.3 5.1 %collective-permute-start.27 = (bf16[16,1024]{1,0:T(8,128)(2,1)S(1)}, bf16[16,1024]{1,0:T(8,128)(2,1)S(1)}, u32[]{:S(2)}, u32[]{:S(2)}) collective-permute-start(bf16[16,1024]{1,0:T(8,128)(2,1)S(1)} %fusion.4), channel_id=1, source_target_pairs={{0,16},{4,20},{8,24},{12,28},{16,0},{20,4},{24,8},{28,12},{1,17},{... | collective-permute-start | bytes 98312 | tf_op jit(solution)/shard_map/ppermute | solution.py:21
  125.4 4.2 %collective-permute-start.28 = (bf16[16,1024]{1,0:T(8,128)(2,1)S(1)}, bf16[16,1024]{1,0:T(8,128)(2,1)S(1)}, u32[]{:S(2)}, u32[]{:S(2)}) collective-permute-start(bf16[16,1024]{1,0:T(8,128)(2,1)S(1)} %fusion.4), channel_id=1, source_target_pairs={{0,8},{4,12},{8,0},{12,4},{16,24},{20,28},{24,16},{28,20},{1,9},{5... | collective-permute-start | bytes 98312 | tf_op jit(solution)/shard_map/ppermute | solution.py:21
  127.4 5.0 %collective-permute-start.12 = (bf16[64,1024]{1,0:T(8,128)(2,1)S(1)}, bf16[64,1024]{1,0:T(8,128)(2,1)S(1)}, u32[]{:S(2)}, u32[]{:S(2)}) collective-permute-start(bf16[64,1024]{1,0:T(8,128)(2,1)S(1)} %dynamic-slice_bitcast_fusion.1), channel_id=1, source_target_pairs={{0,4},{4,0},{8,12},{12,8},{16,20},{20,16},{24,28},{28,24},{1,5},{5... | collective-permute-start | bytes 393224 | tf_op jit(solution)/shard_map/ppermute | solution.py:21
  129.7 7.2 %collective-permute-start.29 = (bf16[64,1024]{1,0:T(8,128)(2,1)S(1)}, bf16[64,1024]{1,0:T(8,128)(2,1)S(1)}, u32[]{:S(2)}, u32[]{:S(2)}) collective-permute-start(bf16[64,1024]{1,0:T(8,128)(2,1)S(1)} %pad_maximum_fusion.2), channel_id=1, source_target_pairs={{0,4},{4,0},{8,12},{12,8},{16,20},{20,16},{24,28},{28,24},{1,5},{5... | collective-permute-start | bytes 393224 | tf_op jit(solution)/shard_map/ppermute | solution.py:21
  132.5 4.5 %collective-permute-start.13 = (bf16[16,1024]{1,0:T(8,128)(2,1)S(1)}, bf16[16,1024]{1,0:T(8,128)(2,1)S(1)}, u32[]{:S(2)}, u32[]{:S(2)}) collective-permute-start(bf16[16,1024]{1,0:T(8,128)(2,1)S(1)} %get-tuple-element.73), channel_id=1, source_target_pairs={{0,8},{4,12},{8,0},{12,4},{16,24},{20,28},{24,16},{28,20},{1,9},{5... | collective-permute-start | bytes 98312 | tf_op jit(solution)/shard_map/ppermute | solution.py:21
  132.7 4.8 %collective-permute-start.14 = (bf16[16,1024]{1,0:T(8,128)(2,1)S(1)}, bf16[16,1024]{1,0:T(8,128)(2,1)S(1)}, u32[]{:S(2)}, u32[]{:S(2)}) collective-permute-start(bf16[16,1024]{1,0:T(8,128)(2,1)S(1)} %get-tuple-element.75), channel_id=1, source_target_pairs={{0,16},{4,20},{8,24},{12,28},{16,0},{20,4},{24,8},{28,12},{1,17},{... | collective-permute-start | bytes 98312 | tf_op jit(solution)/shard_map/ppermute | solution.py:21
  134.5 5.7 %collective-permute-start.15 = (bf16[16,1024]{1,0:T(8,128)(2,1)S(1)}, bf16[16,1024]{1,0:T(8,128)(2,1)S(1)}, u32[]{:S(2)}, u32[]{:S(2)}) collective-permute-start(bf16[16,1024]{1,0:T(8,128)(2,1)S(1)} %get-tuple-element.74), channel_id=1, source_target_pairs={{0,24},{4,28},{8,16},{12,20},{16,8},{20,12},{24,0},{28,4},{1,25},{... | collective-permute-start | bytes 98312 | tf_op jit(solution)/shard_map/ppermute | solution.py:21
  140.3 5.8 %collective-permute-start.16 = (bf16[16,1024]{1,0:T(8,128)(2,1)S(1)}, bf16[16,1024]{1,0:T(8,128)(2,1)S(1)}, u32[]{:S(2)}, u32[]{:S(2)}) collective-permute-start(bf16[16,1024]{1,0:T(8,128)(2,1)S(1)} %fusion.7), channel_id=1, source_target_pairs={{0,24},{4,28},{8,16},{12,20},{16,8},{20,12},{24,0},{28,4},{1,25},{... | collective-permute-start | bytes 98312 | tf_op jit(solution)/shard_map/ppermute | solution.py:21
  142.9 4.8 %collective-permute-start.17 = (bf16[16,1024]{1,0:T(8,128)(2,1)S(1)}, bf16[16,1024]{1,0:T(8,128)(2,1)S(1)}, u32[]{:S(2)}, u32[]{:S(2)}) collective-permute-start(bf16[16,1024]{1,0:T(8,128)(2,1)S(1)} %fusion.7), channel_id=1, source_target_pairs={{0,16},{4,20},{8,24},{12,28},{16,0},{20,4},{24,8},{28,12},{1,17},{... | collective-permute-start | bytes 98312 | tf_op jit(solution)/shard_map/ppermute | solution.py:21
  142.9 4.8 %collective-permute-start.18 = (bf16[16,1024]{1,0:T(8,128)(2,1)S(1)}, bf16[16,1024]{1,0:T(8,128)(2,1)S(1)}, u32[]{:S(2)}, u32[]{:S(2)}) collective-permute-start(bf16[16,1024]{1,0:T(8,128)(2,1)S(1)} %fusion.7), channel_id=1, source_target_pairs={{0,8},{4,12},{8,0},{12,4},{16,24},{20,28},{24,16},{28,20},{1,9},{5... | collective-permute-start | bytes 98312 | tf_op jit(solution)/shard_map/ppermute | solution.py:21
  147.8 5.0 %collective-permute-start.19 = (bf16[64,1024]{1,0:T(8,128)(2,1)S(1)}, bf16[64,1024]{1,0:T(8,128)(2,1)S(1)}, u32[]{:S(2)}, u32[]{:S(2)}) collective-permute-start(bf16[64,1024]{1,0:T(8,128)(2,1)S(1)} %pad_maximum_fusion.1), channel_id=1, source_target_pairs={{0,4},{4,0},{8,12},{12,8},{16,20},{20,16},{24,28},{28,24},{1,5},{5... | collective-permute-start | bytes 393224 | tf_op jit(solution)/shard_map/ppermute | solution.py:21

commit v4 on v3

--- a/solution.py
+++ b/solution.py
@@ -6,6 +6,7 @@
 from jax.experimental import pallas as pl
 from jax.experimental.pallas import tpu as pltpu
 from jax.sharding import PartitionSpec as P
+
 
 EPS = 1e-06
 F32 = jnp.float32
@@ -31,14 +32,8 @@
     return bits
 
 
-def all_sum(value, axis):
-    for bit in bits_of(axis):
-        value = value + swap_bit(value, axis, bit)
-    return value
-
-
 def own_bit(axis, bit):
-    return (lax.axis_index(axis) // bit) % 2
+    return (lax.axis_index(axis) & bit) // bit
 
 
 def add_low(parts):
@@ -84,14 +79,16 @@
     return [bits[:1]] + [bits[i : i + 2] for i in range(1, len(bits), 2)]
 
 
-def reduce_rows(keep, give):
-    cols = keep.shape[-1]
-    bits = bits_of("rep")
-    value = add_low([keep, swap_bit(give, "rep", bits[0])])
-    for bit in bits[1:]:
+def rep_rest(value, bits):
+    cols = value.shape[-1]
+    for bit in bits:
         value = value.reshape(-1, 2, value.shape[-2], cols)
         value = scatter_stage(value, "rep", [bit], 1)
-    value = value.reshape(-1, cols)
+    return value.reshape(-1, cols)
+
+
+def sp_rows(value):
+    cols = value.shape[-1]
     for bits in stages_of("sp"):
         value = scatter_stage(value.reshape(1 << len(bits), -1, cols), "sp", bits, 0)
     for bits in reversed(stages_of("sp")):
@@ -301,7 +298,7 @@
     edge_ref, sharp_ref, pack_ref, up_ref, near_ref, far_ref, act_mid_ref, hidden_ref, slope_ref,
     attended_ref, projected_ref, residual_ref, value_ref, act_one_ref, gain_two_ref, factor_ref,
     w_out_ref, kernel_ref,
-    prob_out_ref, small_ref, d_res_ref, d_value_ref, keep_ref, give_ref,
+    prob_out_ref, d_res_ref, d_value_ref, keep_ref, give_ref,
     up_ext, d_ext, hid_ext, d_act, sums, d_proj_ref, d_att_ref, grad_ref,
 ):
     rows, width, dim = up_ref.shape
@@ -394,7 +391,8 @@
             scale_one = scale_one + jnp.sum(projected_ref[span, :] * d_res, 0, keepdims=True)
             d_proj_ref[span, :] = (factor_one * d_res).astype(BF16)
     scale_two = jnp.zeros((1, dim), F32)
-    small_ref[20:, :] = jnp.zeros_like(small_ref[20:, :])
+    small_ref = prob_out_ref.at[head_dim:]
+    small_ref[20:, :] = jnp.zeros((4, dim), F32)
     for tap in range(9):
         small_ref[tap : tap + 1, :] = jnp.sum(sums[tap], 0, keepdims=True)
         raw = jnp.sum(sums[9 + tap], 0, keepdims=True)
@@ -407,7 +405,7 @@
         lanes = slice(block * LANES, (block + 1) * LANES)
         prob, *_, block_id, _ = softmax_block(pack_ref, sharp_ref, block, head_dim)
         d_att = d_att_ref[:, lanes]
-        prob_out_ref[:, lanes] = compact(block_id, dot32(d_att, value_ref[:, lanes], 0, 0))
+        prob_out_ref[:head_dim, lanes] = compact(block_id, dot32(d_att, value_ref[:, lanes], 0, 0))
         d_value_ref[:, lanes] = dot32(d_att, block_diag(block_id, prob), 1, 0).astype(BF16)
     grad_ref[:, :dim] = dot32(act_one_ref[...], d_value_ref[...], 0, 0).astype(BF16)
     grad_ref[:, dim:] = dot32(attended_ref[...], d_proj_ref[...], 0, 0).astype(BF16)
@@ -426,7 +424,7 @@
 def gram_kernel(
     edge_ref, sharp_ref, pack_ref, prob_ref, mixed_ref, act_ref, d_qk_ref, keep_ref, give_ref, grad_ref,
 ):
-    tokens, dim = act_ref.shape
+    _, dim = act_ref.shape
     head_dim = dim // sharp_ref.shape[0]
     for block in range(dim // LANES):
         lanes = slice(block * LANES, (block + 1) * LANES)
@@ -434,7 +432,7 @@
         prob, scores, sharp, divisor, query_col, key_row, block_id, diag = softmax_block(
             pack_ref, sharp_ref, block, head_dim
         )
-        prob_grad = prob_ref[:, lanes]
+        prob_grad = prob_ref[:head_dim, lanes]
         d_scores = prob * (prob_grad - seg_sum(block_id, prob * prob_grad))
         d_gram = block_diag(block_id, d_scores * sharp / divisor)
         weighted = d_scores * scores
@@ -467,7 +465,7 @@
         ).astype(BF16)
 
 
-def call(body, name, outs, args, scalars=0, scratch=(), thirds=()):
+def call(body, outs, args, scalars=0, scratch=(), thirds=()):
     specs = []
     for i, arg in enumerate(args):
         if i < scalars:
@@ -478,7 +476,6 @@
             specs.append(pl.BlockSpec(arg.shape, lambda i, n=arg.ndim: (0,) * n))
     return pl.pallas_call(
         body,
-        name=name,
         grid=(1,),
         out_shape=[jax.ShapeDtypeStruct(shape, dtype) for shape, dtype in outs],
         in_specs=specs,
@@ -498,8 +495,8 @@
     return lax.ppermute(value, "sp", hops)
 
 
-def after(value, earlier):
-    return lax.optimization_barrier((value, earlier))
+def after(value, *earlier):
+    return lax.optimization_barrier((value, *earlier))[0]
 
 
 def shards(x4, up4, gain_one, w_qkv, sharp, w_out, factors, gain_two, kernels):
@@ -517,25 +514,24 @@
         [1 - index % 2, jnp.minimum(index, 1), jnp.minimum(last - index, 1), own_bit("rep", 1)]
     )
     pack_rows = head_dim + 8
+    sp_bits = bits_of("sp")
+    sp_bits = sp_bits[1:] + sp_bits[:1]
 
     x_near = beside(x_own)
     mixed, act_one, pack = call(
-        functools.partial(first_kernel, head_dim=head_dim), "first",
+        functools.partial(first_kernel, head_dim=head_dim),
         [((tokens, 3 * dim), BF16), ((tokens, dim), BF16), ((pack_rows, dim), F32)],
         (flat, gain_one, w_qkv),
     )
-    sp_bits = bits_of("sp")
-    for step, bit in enumerate(sp_bits):
-        pack = pack + swap_bit(pack, "sp", bit)
-        if step == 0:
-            x_near, pack = after(x_near, pack)
-            x_far = beyond(x_near)
-            up_far_in, pack = after(up_own, pack)
-            up_near = beside(up_far_in)
-    up_near, pack = after(up_near, pack)
-    up_far = beyond(up_near)
+    up_near = beside(after(up_own, pack))
+    packs = [pack]
+    for bit in sp_bits:
+        packs.append(packs[-1] + swap_bit(packs[-1], "sp", bit))
+    x_far = beyond(after(x_near, packs[1]))
+    up_far = beyond(after(up_near, packs[-2]))
+    pack = packs[-1]
     attended, projected, residual, act_mid, hidden, slope = call(
-        attend_kernel, "attend",
+        attend_kernel,
         [((tokens, dim), BF16), ((tokens, dim), F32), ((tokens, dim), BF16),
          ((rows + 2, width, dim), BF16), ((rows, width, dim), BF16), ((rows + 2, width, dim), F32)],
         (edges, sharp, pack, x_own, x_near, x_far, mixed, gain_one, gain_two, factors,
@@ -546,10 +542,9 @@
     )
     blocks = lax.axis_size("rep")
     split = ((blocks // 2, dim // blocks, 2 * dim), BF16)
-    prob_part, small, d_res, d_value, keep, give = call(
-        back_kernel, "back",
-        [((head_dim, dim), F32), ((24, dim), F32), ((tokens, dim), F32), ((tokens, dim), BF16),
-         split, split],
+    prob_part, d_res, d_value, keep, give = call(
+        back_kernel,
+        [((head_dim + 24, dim), F32), ((tokens, dim), F32), ((tokens, dim), BF16), split, split],
         (edges, sharp, pack, up_own, up_near, up_far, act_mid, hidden, slope, attended, projected,
          residual, mixed, act_one, gain_two, factors, w_out, taps),
         scalars=2,
@@ -559,24 +554,38 @@
                  ((rows, width, dim), F32), ((18, 8, dim), F32), ((tokens, dim), BF16),
                  ((tokens, dim), BF16), ((dim, 2 * dim), BF16)],
     )
-    prob_part = all_sum(prob_part, "sp")
-    early = reduce_rows(keep, give)
-    d_qk, keep, give = call(
-        gram_kernel, "gram",
+    probs = [prob_part]
+    for bit in sp_bits:
+        probs.append(probs[-1] + swap_bit(probs[-1], "sp", bit))
+    prob_part = probs[-1]
+    d_qk, late_keep, late_give = call(
+        gram_kernel,
         [((tokens, 2 * dim), BF16), split, split],
         (edges, sharp, pack, prob_part, mixed, act_one), scalars=2,
         scratch=[((dim, 2 * dim), BF16)],
     )
-    late = reduce_rows(keep, give)
-    small = all_sum(all_sum(small, "rep"), "sp")
+    rep_bits = bits_of("rep")
+
+    early = add_low([keep, swap_bit(give, "rep", rep_bits[0])])
+    early = rep_rest(early, rep_bits[1:])
+
+    late = add_low([late_keep, swap_bit(late_give, "rep", rep_bits[0])])
+    late = rep_rest(late, rep_bits[1:])
+    both = jnp.concatenate([late, early], -1)
+    both = sp_rows(both)
+
+    small = prob_part[head_dim:]
+    small = small + swap_bit(after(small, d_qk), "rep", rep_bits[0])
+    for bit in rep_bits[1:]:
+        small = small + swap_bit(small, "rep", bit)
     (grad_input,) = call(
-        input_kernel, "input", [((tokens, dim), BF16)],
+        input_kernel, [((tokens, dim), BF16)],
         (flat, gain_one, w_qkv, d_qk, d_value, d_res),
     )
     return (
         grad_input.reshape(1, rows, width, dim),
-        jnp.concatenate([late, early[:, :dim]], 1),
-        early[:, dim:],
+        both[:, : 3 * dim],
+        both[:, 3 * dim :],
         small[:18].reshape(kernels.shape),
         small[18:20],
     )

time: 154 us -> 138 us (0.90)
  starting transfers between devices: 53.9 us -> 35.7 us
  waiting for transfers between devices: 49.7 us -> 53.2 us
    ppermute x33 -> x22, starting transfers between devices: 46.2 us -> 28.5 us  [swap_bit(): return lax.ppermute(value, axis, [(i, i ^ bit) for i in range(count)])]
    ppermute x33 -> x22, waiting for transfers between devices: 45.2 us -> 53.2 us  [swap_bit(): return lax.ppermute(value, axis, [(i, i ^ bit) for i in range(count)])]
    ppermute x2, waiting for transfers between devices: 4.49 us -> 0.01 us  [beyond(): return lax.ppermute(value, 'sp', hops)]
    add x11 -> x8, other arithmetic: 3.28 us -> 3.33 us  [the longest x3 1.67 us: shards(): probs.append(probs[-1] + swap_bit(probs[-1], 'sp', bit))]
  transfers between devices with their start and end apart: 35 -> 24, of which waited for: 19 -> 15; matrix products, arithmetic and copies ran while one was open for 5% -> 5% of each run, Pallas kernels for 17% -> 19%
where the time goes in v4:
time: 138 us
  waiting for transfers between devices  53.2 us (39%)
  Pallas kernels  37.8 us (27%)
  starting transfers between devices  35.7 us (26%)
  other arithmetic  5.58 us (4%)
  local copies, waits for them, and re-layouts  4.56 us (3%)
    ppermute x22, waiting for transfers between devices, swap_bit(): return lax.ppermute(value, axis, [(i, i ^ bit) for i in range(count)])  53.2 us
    pallas_call x5, Pallas kernels, call(): pl.pallas_call(body, grid=(1,), out_shape=[jax.ShapeDtypeStruct(shape, dt...  37.8 us
    ppermute x22, starting transfers between devices, swap_bit(): return lax.ppermute(value, axis, [(i, i ^ bit) for i in range(count)])  28.5 us
    ppermute x2, starting transfers between devices, beyond(): return lax.ppermute(value, 'sp', hops)  7.25 us
  transfers between devices with their start and end apart: 24, of which 15 were waited for; matrix products, arithmetic and copies ran while one was open for 5% of the time, Pallas kernels for 19%

profile of v4, /device:TPU:0, one launch (start us, length us, event | category | flops | bytes accessed | tf_op | source)
XLA Modules:
  0.0 137.8 jit_solution(7297651875755730342)
XLA Ops:
  0.6 0.0 copy-start.5
  0.7 3.0 %collective-permute-start.5 = (bf16[2,256,512]{2,1,0:T(8,128)(2,1)}, bf16[2,256,512]{2,1,0:T(8,128)(2,1)S(1)}, u32[]{:S(2)}, u32[]{:S(2)}) collective-permute-start(bf16[2,256,512]{2,1,0:T(8,128)(2,1)} %bitcast.30), channel_id=1, source_target_pairs={{0,4},{4,0},{8,12},{12,8},{16,20},{20,16},{24,28},{28,24},{1,5},{5... | collective-permute-start | bytes 1572872 | tf_op jit(solution)/shard_map/ppermute | solution.py:22
  3.7 5.3 %shard_map.128 = (bf16[512,1536]{1,0:T(8,128)(2,1)}, bf16[512,512]{1,0:T(8,128)(2,1)}, f32[72,512]{1,0:T(8,128)}) custom-call(bf16[512,512]{1,0:T(8,128)(2,1)} %bitcast.31, f32[1,512]{1,0:T(1,128)} %bitcast.44, bf16[512,1536]{1,0:T(8,128)(2,1)} %w_ref.3), custom_call_target="tpu_custom_call" | custom-call | tf_op jit(solution)/shard_map/pallas_call | solution.py:477
  9.0 0.1 collective-permute-start.3
  9.1 2.0 %collective-permute-start = (f32[72,512]{1,0:T(8,128)}, f32[72,512]{1,0:T(8,128)S(1)}, u32[]{:S(2)}, u32[]{:S(2)}) collective-permute-start(f32[72,512]{1,0:T(8,128)} %get-tuple-element.26), channel_id=1, source_target_pairs={{0,8},{4,12},{8,0},{12,4},{16,24},{20,28},{24,16},{28,20},{1,9},{5... | collective-permute-start | bytes 442376 | tf_op jit(solution)/shard_map/ppermute | solution.py:22
  11.1 3.5 %collective-permute-done = f32[72,512]{1,0:T(8,128)S(1)} collective-permute-done((f32[72,512]{1,0:T(8,128)}, f32[72,512]{1,0:T(8,128)S(1)}, u32[]{:S(2)}, u32[]{:S(2)}) %collective-permute-start) | collective-permute-done | bytes 147488 | tf_op jit(solution)/shard_map/ppermute | solution.py:22
  14.6 0.9 add.91
  15.6 2.9 %collective-permute-start.1 = (f32[72,512]{1,0:T(8,128)S(1)}, f32[72,512]{1,0:T(8,128)S(1)}, u32[]{:S(2)}, u32[]{:S(2)}) collective-permute-start(f32[72,512]{1,0:T(8,128)S(1)} %add.91), channel_id=1, source_target_pairs={{0,16},{4,20},{8,24},{12,28},{16,0},{20,4},{24,8},{28,12},{1,17},{... | collective-permute-start | bytes 442376 | tf_op jit(solution)/shard_map/ppermute | solution.py:22
  18.5 3.5 %collective-permute-start.6 = (bf16[2,256,512]{2,1,0:T(8,128)(2,1)S(1)}, bf16[2,256,512]{2,1,0:T(8,128)(2,1)S(1)}, u32[]{:S(2)}, u32[]{:S(2)}) collective-permute-start(bf16[2,256,512]{2,1,0:T(8,128)(2,1)S(1)} %collective-permute-done.5.near_ref), channel_id=1, source_target_pairs={{12,4},{20,12},{28,20},{0,8},{8,16},{16,24},{13,5},{21,13},{29,21}... | collective-permute-start | bytes 1572872 | tf_op jit(solution)/shard_map/ppermute | solution.py:495
  22.0 2.1 %collective-permute-done.1 = f32[72,512]{1,0:T(8,128)S(1)} collective-permute-done((f32[72,512]{1,0:T(8,128)S(1)}, f32[72,512]{1,0:T(8,128)S(1)}, u32[]{:S(2)}, u32[]{:S(2)}) %collective-permute-start.1) | collective-permute-done | bytes 147488 | tf_op jit(solution)/shard_map/ppermute | solution.py:22
  24.2 2.9 %collective-permute-done.3.near_ref = bf16[2,256,512]{2,1,0:T(8,128)(2,1)S(1)} collective-permute-done((bf16[2,256,512]{2,1,0:T(8,128)(2,1)S(1)}, bf16[2,256,512]{2,1,0:T(8,128)(2,1)S(1)}, u32[]{:S(2)}, u32[]{:S(2)}) %collective-permute-start.3) | collective-permute-done | bytes 524320 | tf_op jit(solution)/shard_map/ppermute | solution.py:22
  27.1 3.7 %collective-permute-start.4 = (bf16[2,256,512]{2,1,0:T(8,128)(2,1)S(1)}, bf16[2,256,512]{2,1,0:T(8,128)(2,1)S(1)}, u32[]{:S(2)}, u32[]{:S(2)}) collective-permute-start(bf16[2,256,512]{2,1,0:T(8,128)(2,1)S(1)} %collective-permute-done.3.near_ref), channel_id=1, source_target_pairs={{12,4},{20,12},{28,20},{0,8},{8,16},{16,24},{13,5},{21,13},{29,21}... | collective-permute-start | bytes 1572872 | tf_op jit(solution)/shard_map/ppermute | solution.py:495
  30.8 0.1 collective-permute-start.2
  30.9 0.6 reshape.47.kernel_ref
  31.6 0.6 pad_add_fusion.edge_ref
  32.2 3.8 %collective-permute-done.2 = f32[72,512]{1,0:T(8,128)S(1)} collective-permute-done((f32[72,512]{1,0:T(8,128)S(1)}, f32[72,512]{1,0:T(8,128)S(1)}, u32[]{:S(2)}, u32[]{:S(2)}) %collective-permute-start.2) | collective-permute-done | bytes 147488 | tf_op jit(solution)/shard_map/ppermute | solution.py:22
  36.0 0.7 add.93.pack_ref
  36.7 0.0 collective-permute-done.6.far_ref
  36.7 0.8 copy-done.3
  37.5 10.7 %shard_map.129 = (bf16[512,512]{1,0:T(8,128)(2,1)}, f32[512,512]{1,0:T(8,128)}, bf16[512,512]{1,0:T(8,128)(2,1)}, bf16[4,256,512]{2,1,0:T(8,128)(2,1)}, bf16[2,2...) custom-call(s32[4]{0:T(128)} %pad_add_fusion.edge_ref, f32[8]{0:T(128)} %sharp_ref.5, f32[72,512]{1,0:T(8,128)} %add.93.pack_ref, ...), custom_call_target="tpu_custom_call" | custom-call | tf_op jit(solution)/shard_map/pallas_call | solution.py:477
  48.3 0.8 copy-done.7
  49.1 11.8 %shard_map.130 = (f32[88,512]{1,0:T(8,128)}, f32[512,512]{1,0:T(8,128)}, bf16[512,512]{1,0:T(8,128)(2,1)}, bf16[2,128,1024]{2,1,0:T(8,128)(2,1)}, bf16[2,128,1024]{2,1,0:T(8,128)(2,1)}) custom-call(s32[4]{0:T(128)} %pad_add_fusion.edge_ref, f32[8]{0:T(128)} %sharp_ref.5, f32[72,512]{1,0:T(8,128)} %add.93.pack_ref, bf16[2,256,512]{2,1,0:T(8,128)(2,1)} %bitcast.41, ...), custom_call_target="tpu_custom_call" | custom-call | tf_op jit(solution)/shard_map/pallas_call | solution.py:477
  60.9 1.6 %collective-permute-start.7 = (f32[88,512]{1,0:T(8,128)}, f32[88,512]{1,0:T(8,128)S(1)}, u32[]{:S(2)}, u32[]{:S(2)}) collective-permute-start(f32[88,512]{1,0:T(8,128)} %get-tuple-element.38), channel_id=1, source_target_pairs={{0,8},{4,12},{8,0},{12,4},{16,24},{20,28},{24,16},{28,20},{1,9},{5... | collective-permute-start | bytes 540680 | tf_op jit(solution)/shard_map/ppermute | solution.py:22
  62.4 0.0 collective-permute-start.12
  62.4 4.1 %collective-permute-done.7 = f32[88,512]{1,0:T(8,128)S(1)} collective-permute-done((f32[88,512]{1,0:T(8,128)}, f32[88,512]{1,0:T(8,128)S(1)}, u32[]{:S(2)}, u32[]{:S(2)}) %collective-permute-start.7) | collective-permute-done | bytes 180256 | tf_op jit(solution)/shard_map/ppermute | solution.py:22
  66.6 0.9 add.94
  67.5 2.6 %collective-permute-start.8 = (f32[88,512]{1,0:T(8,128)S(1)}, f32[88,512]{1,0:T(8,128)S(1)}, u32[]{:S(2)}, u32[]{:S(2)}) collective-permute-start(f32[88,512]{1,0:T(8,128)S(1)} %add.94), channel_id=1, source_target_pairs={{0,16},{4,20},{8,24},{12,28},{16,0},{20,4},{24,8},{28,12},{1,17},{... | collective-permute-start | bytes 540680 | tf_op jit(solution)/shard_map/ppermute | solution.py:22
  70.2 5.8 %collective-permute-done.8 = f32[88,512]{1,0:T(8,128)S(1)} collective-permute-done((f32[88,512]{1,0:T(8,128)S(1)}, f32[88,512]{1,0:T(8,128)S(1)}, u32[]{:S(2)}, u32[]{:S(2)}) %collective-permute-start.8) | collective-permute-done | bytes 180256 | tf_op jit(solution)/shard_map/ppermute | solution.py:22
  76.0 0.5 collective-permute-start.9
  76.4 5.1 %collective-permute-done.9 = f32[88,512]{1,0:T(8,128)S(1)} collective-permute-done((f32[88,512]{1,0:T(8,128)S(1)}, f32[88,512]{1,0:T(8,128)S(1)}, u32[]{:S(2)}, u32[]{:S(2)}) %collective-permute-start.9) | collective-permute-done | bytes 180256 | tf_op jit(solution)/shard_map/ppermute | solution.py:22
  81.5 0.7 add.96.prob_ref
  82.2 4.5 %shard_map.131 = (bf16[512,1024]{1,0:T(8,128)(2,1)}, bf16[2,128,1024]{2,1,0:T(8,128)(2,1)}, bf16[2,128,1024]{2,1,0:T(8,128)(2,1)}) custom-call(s32[4]{0:T(128)} %pad_add_fusion.edge_ref, f32[8]{0:T(128)} %sharp_ref.5, f32[72,512]{1,0:T(8,128)} %add.93.pack_ref, f32[88,512]{1,0:T(8,128)} %add.96.prob_ref, ...), custom_call_target="tpu_custom_call" | custom-call | tf_op jit(solution)/shard_map/pallas_call | solution.py:477
  86.8 0.0 collective-permute-start.10
  86.8 0.2 add_convert_fusion
  87.0 1.6 %collective-permute-start.13 = (bf16[1,128,1024]{2,1,0:T(8,128)(2,1)S(1)}, bf16[1,128,1024]{2,1,0:T(8,128)(2,1)S(1)}, u32[]{:S(2)}, u32[]{:S(2)}) collective-permute-start(bf16[1,128,1024]{2,1,0:T(8,128)(2,1)S(1)} %constant_dynamic-slice_fusion), channel_id=1, source_target_pairs={{0,2},{1,3},{2,0},{3,1},{4,6},{5,7},{6,4},{7,5},{8,10},{9,11},{10,... | collective-permute-start | bytes 786440 | tf_op jit(solution)/shard_map/ppermute | solution.py:22
  88.6 0.3 collective-permute-done.10
  88.9 0.2 add_convert_fusion.1
  89.1 1.6 %collective-permute-start.11 = (bf16[1,128,1024]{2,1,0:T(8,128)(2,1)S(1)}, bf16[1,128,1024]{2,1,0:T(8,128)(2,1)S(1)}, u32[]{:S(2)}, u32[]{:S(2)}) collective-permute-start(bf16[1,128,1024]{2,1,0:T(8,128)(2,1)S(1)} %constant_dynamic-slice_fusion.1), channel_id=1, source_target_pairs={{0,2},{1,3},{2,0},{3,1},{4,6},{5,7},{6,4},{7,5},{8,10},{9,11},{10,... | collective-permute-start | bytes 786440 | tf_op jit(solution)/shard_map/ppermute | solution.py:22
  90.7 5.6 %collective-permute-done.13 = bf16[1,128,1024]{2,1,0:T(8,128)(2,1)S(1)} collective-permute-done((bf16[1,128,1024]{2,1,0:T(8,128)(2,1)S(1)}, bf16[1,128,1024]{2,1,0:T(8,128)(2,1)S(1)}, u32[]{:S(2)}, u32[]{:S(2)}) %collective-permute-start.13) | collective-permute-done | bytes 262176 | tf_op jit(solution)/shard_map/ppermute | solution.py:22
  96.3 0.1 add_convert_fusion.2
  96.4 0.0 copy-start
  96.4 5.0 %collective-permute-done.11 = bf16[1,128,1024]{2,1,0:T(8,128)(2,1)S(1)} collective-permute-done((bf16[1,128,1024]{2,1,0:T(8,128)(2,1)S(1)}, bf16[1,128,1024]{2,1,0:T(8,128)(2,1)S(1)}, u32[]{:S(2)}, u32[]{:S(2)}) %collective-permute-start.11) | collective-permute-done | bytes 262176 | tf_op jit(solution)/shard_map/ppermute | solution.py:22
  101.4 0.1 add_convert_fusion.3
  101.5 0.5 collective-permute-start.14
  102.0 7.4 %collective-permute-done.14 = bf16[64,2048]{1,0:T(8,128)(2,1)S(1)} collective-permute-done((bf16[64,2048]{1,0:T(8,128)(2,1)S(1)}, bf16[64,2048]{1,0:T(8,128)(2,1)S(1)}, u32[]{:S(2)}, u32[]{:S(2)}) %collective-permute-start.14) | collective-permute-done | bytes 262176 | tf_op jit(solution)/shard_map/ppermute | solution.py:22
  109.4 0.1 fusion
  109.5 0.1 collective-permute-start.15
  109.6 2.6 %collective-permute-start.16 = (bf16[16,2048]{1,0:T(8,128)(2,1)S(1)}, bf16[16,2048]{1,0:T(8,128)(2,1)S(1)}, u32[]{:S(2)}, u32[]{:S(2)}) collective-permute-start(bf16[16,2048]{1,0:T(8,128)(2,1)S(1)} %get-tuple-element.65), channel_id=1, source_target_pairs={{0,16},{4,20},{8,24},{12,28},{16,0},{20,4},{24,8},{28,12},{1,17},{... | collective-permute-start | bytes 196616 | tf_op jit(solution)/shard_map/ppermute | solution.py:22
  112.2 1.7 %collective-permute-start.17 = (bf16[16,2048]{1,0:T(8,128)(2,1)S(1)}, bf16[16,2048]{1,0:T(8,128)(2,1)S(1)}, u32[]{:S(2)}, u32[]{:S(2)}) collective-permute-start(bf16[16,2048]{1,0:T(8,128)(2,1)S(1)} %get-tuple-element.64), channel_id=1, source_target_pairs={{0,24},{4,28},{8,16},{12,20},{16,8},{20,12},{24,0},{28,4},{1,25},{... | collective-permute-start | bytes 196616 | tf_op jit(solution)/shard_map/ppermute | solution.py:22
  114.0 1.0 collective-permute-done.16
  114.9 3.5 %collective-permute-done.17 = bf16[16,2048]{1,0:T(8,128)(2,1)S(1)} collective-permute-done((bf16[16,2048]{1,0:T(8,128)(2,1)S(1)}, bf16[16,2048]{1,0:T(8,128)(2,1)S(1)}, u32[]{:S(2)}, u32[]{:S(2)}) %collective-permute-start.17) | collective-permute-done | bytes 65568 | tf_op jit(solution)/shard_map/ppermute | solution.py:22
  118.4 1.8 %collective-permute-start.18 = (bf16[16,2048]{1,0:T(8,128)(2,1)S(1)}, bf16[16,2048]{1,0:T(8,128)(2,1)S(1)}, u32[]{:S(2)}, u32[]{:S(2)}) collective-permute-start(bf16[16,2048]{1,0:T(8,128)(2,1)S(1)} %fusion.7), channel_id=1, source_target_pairs={{0,24},{4,28},{8,16},{12,20},{16,8},{20,12},{24,0},{28,4},{1,25},{... | collective-permute-start | bytes 196616 | tf_op jit(solution)/shard_map/ppermute | solution.py:22
  120.2 2.7 %collective-permute-start.20 = (bf16[16,2048]{1,0:T(8,128)(2,1)S(1)}, bf16[16,2048]{1,0:T(8,128)(2,1)S(1)}, u32[]{:S(2)}, u32[]{:S(2)}) collective-permute-start(bf16[16,2048]{1,0:T(8,128)(2,1)S(1)} %fusion.7), channel_id=1, source_target_pairs={{0,8},{4,12},{8,0},{12,4},{16,24},{20,28},{24,16},{28,20},{1,9},{5... | collective-permute-start | bytes 196616 | tf_op jit(solution)/shard_map/ppermute | solution.py:22
  122.9 1.7 %collective-permute-done.18 = bf16[16,2048]{1,0:T(8,128)(2,1)S(1)} collective-permute-done((bf16[16,2048]{1,0:T(8,128)(2,1)S(1)}, bf16[16,2048]{1,0:T(8,128)(2,1)S(1)}, u32[]{:S(2)}, u32[]{:S(2)}) %collective-permute-start.18) | collective-permute-done | bytes 65568 | tf_op jit(solution)/shard_map/ppermute | solution.py:22
  124.6 1.4 %collective-permute-done.19 = bf16[16,2048]{1,0:T(8,128)(2,1)S(1)} collective-permute-done((bf16[16,2048]{1,0:T(8,128)(2,1)S(1)}, bf16[16,2048]{1,0:T(8,128)(2,1)S(1)}, u32[]{:S(2)}, u32[]{:S(2)}) %collective-permute-start.19) | collective-permute-done | bytes 65568 | tf_op jit(solution)/shard_map/ppermute | solution.py:22
  126.0 1.6 %collective-permute-start.21 = (bf16[64,2048]{1,0:T(8,128)(2,1)S(1)}, bf16[64,2048]{1,0:T(8,128)(2,1)S(1)}, u32[]{:S(2)}, u32[]{:S(2)}) collective-permute-start(bf16[64,2048]{1,0:T(8,128)(2,1)S(1)} %pad_maximum_fusion), channel_id=1, source_target_pairs={{0,4},{4,0},{8,12},{12,8},{16,20},{20,16},{24,28},{28,24},{1,5},{5... | collective-permute-start | bytes 786440 | tf_op jit(solution)/shard_map/ppermute | solution.py:22
  127.7 1.6 %collective-permute-start.23 = (f32[24,512]{1,0:T(8,128)S(1)}, f32[24,512]{1,0:T(8,128)S(1)}, u32[]{:S(2)}, u32[]{:S(2)}) collective-permute-start(f32[24,512]{1,0:T(8,128)S(1)} %slice_add_fusion), channel_id=1, source_target_pairs={{0,2},{1,3},{2,0},{3,1},{4,6},{5,7},{6,4},{7,5},{8,10},{9,11},{10,... | collective-permute-start | bytes 147464 | tf_op jit(solution)/shard_map/ppermute | solution.py:22
  129.2 5.4 %shard_map.132 = bf16[512,512]{1,0:T(8,128)(2,1)} custom-call(bf16[512,512]{1,0:T(8,128)(2,1)} %bitcast.33, f32[1,512]{1,0:T(1,128)} %bitcast.46, bf16[512,1536]{1,0:T(8,128)(2,1)} %w_ref.3, bf16[512,1024]{1,0:T(8,128)(2,1)} %get-tuple-element.39.d_qk_ref, bf16[512,512]{1,0:T(8,128)(2,1)} %get-tuple-element.40.d_value_ref, ...), custom_call_target="tpu_custom_call" | custom-call | tf_op jit(solution)/shard_map/pallas_call | solution.py:477
  134.7 0.6 slice.23
  135.3 0.6 copy.17
  136.0 0.1 broadcast_select_fusion.1
  136.0 0.7 maximum_convert_fusion.1
  136.8 0.1 maximum_convert_fusion
  136.9 0.9 slice.20
  (38 shorter events, 0.3 us)
Async XLA Ops:
  0.6 8.4 %copy-start.5 = (bf16[1,2,256,512]{3,2,1,0:T(8,128)(2,1)S(1)}, bf16[1,2,256,512]{3,2,1,0:T(8,128)(2,1)}, u32[]{:S(2)}) copy-start(bf16[1,2,256,512]{3,2,1,0:T(8,128)(2,1)} %param.10) | copy-start | bytes 1572868
  0.6 30.3 %copy-start.8 = (f32[2,3,3,512]{3,0,2,1:T(2,128)S(1)}, f32[2,3,3,512]{3,0,2,1:T(2,128)}, u32[]{:S(2)}) copy-start(f32[2,3,3,512]{3,0,2,1:T(2,128)} %param.17) | copy-start | bytes 110596
  0.7 17.8 %collective-permute-start.5 = (bf16[2,256,512]{2,1,0:T(8,128)(2,1)}, bf16[2,256,512]{2,1,0:T(8,128)(2,1)S(1)}, u32[]{:S(2)}, u32[]{:S(2)}) collective-permute-start(bf16[2,256,512]{2,1,0:T(8,128)(2,1)} %bitcast.30), channel_id=1, source_target_pairs={{0,4},{4,0},{8,12},{12,8},{16,20},{20,16},{24,28},{28,24},{1,5},{5... | collective-permute-start | bytes 1572872 | tf_op jit(solution)/shard_map/ppermute | solution.py:22
  9.0 18.0 %collective-permute-start.3 = (bf16[2,256,512]{2,1,0:T(8,128)(2,1)S(1)}, bf16[2,256,512]{2,1,0:T(8,128)(2,1)S(1)}, u32[]{:S(2)}, u32[]{:S(2)}) collective-permute-start(bf16[2,256,512]{2,1,0:T(8,128)(2,1)S(1)} %bitcast.42), channel_id=1, source_target_pairs={{0,4},{4,0},{8,12},{12,8},{16,20},{20,16},{24,28},{28,24},{1,5},{5... | collective-permute-start | bytes 1572872 | tf_op jit(solution)/shard_map/ppermute | solution.py:22
  9.1 5.5 %collective-permute-start = (f32[72,512]{1,0:T(8,128)}, f32[72,512]{1,0:T(8,128)S(1)}, u32[]{:S(2)}, u32[]{:S(2)}) collective-permute-start(f32[72,512]{1,0:T(8,128)} %get-tuple-element.26), channel_id=1, source_target_pairs={{0,8},{4,12},{8,0},{12,4},{16,24},{20,28},{24,16},{28,20},{1,9},{5... | collective-permute-start | bytes 442376 | tf_op jit(solution)/shard_map/ppermute | solution.py:22
  15.6 8.6 %collective-permute-start.1 = (f32[72,512]{1,0:T(8,128)S(1)}, f32[72,512]{1,0:T(8,128)S(1)}, u32[]{:S(2)}, u32[]{:S(2)}) collective-permute-start(f32[72,512]{1,0:T(8,128)S(1)} %add.91), channel_id=1, source_target_pairs={{0,16},{4,20},{8,24},{12,28},{16,0},{20,4},{24,8},{28,12},{1,17},{... | collective-permute-start | bytes 442376 | tf_op jit(solution)/shard_map/ppermute | solution.py:22
  18.5 18.2 %copy-start.1 = (bf16[2,256,512]{2,1,0:T(8,128)(2,1)}, bf16[2,256,512]{2,1,0:T(8,128)(2,1)S(1)}, u32[]{:S(2)}) copy-start(bf16[2,256,512]{2,1,0:T(8,128)(2,1)S(1)} %collective-permute-done.5.near_ref) | copy-start | bytes 1572868
  18.5 18.2 %collective-permute-start.6 = (bf16[2,256,512]{2,1,0:T(8,128)(2,1)S(1)}, bf16[2,256,512]{2,1,0:T(8,128)(2,1)S(1)}, u32[]{:S(2)}, u32[]{:S(2)}) collective-permute-start(bf16[2,256,512]{2,1,0:T(8,128)(2,1)S(1)} %collective-permute-done.5.near_ref), channel_id=1, source_target_pairs={{12,4},{20,12},{28,20},{0,8},{8,16},{16,24},{13,5},{21,13},{29,21}... | collective-permute-start | bytes 1572872 | tf_op jit(solution)/shard_map/ppermute | solution.py:495
  27.1 21.2 %copy-start.6 = (bf16[2,256,512]{2,1,0:T(8,128)(2,1)}, bf16[2,256,512]{2,1,0:T(8,128)(2,1)S(1)}, u32[]{:S(2)}) copy-start(bf16[2,256,512]{2,1,0:T(8,128)(2,1)S(1)} %collective-permute-done.3.near_ref) | copy-start | bytes 1572868
  27.1 21.2 %collective-permute-start.4 = (bf16[2,256,512]{2,1,0:T(8,128)(2,1)S(1)}, bf16[2,256,512]{2,1,0:T(8,128)(2,1)S(1)}, u32[]{:S(2)}, u32[]{:S(2)}) collective-permute-start(bf16[2,256,512]{2,1,0:T(8,128)(2,1)S(1)} %collective-permute-done.3.near_ref), channel_id=1, source_target_pairs={{12,4},{20,12},{28,20},{0,8},{8,16},{16,24},{13,5},{21,13},{29,21}... | collective-permute-start | bytes 1572872 | tf_op jit(solution)/shard_map/ppermute | solution.py:495
  30.8 5.2 %collective-permute-start.2 = (f32[72,512]{1,0:T(8,128)S(1)}, f32[72,512]{1,0:T(8,128)S(1)}, u32[]{:S(2)}, u32[]{:S(2)}) collective-permute-start(f32[72,512]{1,0:T(8,128)S(1)} %add.92), channel_id=1, source_target_pairs={{0,4},{4,0},{8,12},{12,8},{16,20},{20,16},{24,28},{28,24},{1,5},{5... | collective-permute-start | bytes 442376 | tf_op jit(solution)/shard_map/ppermute | solution.py:22
  36.7 0.8 copy-start.3
  48.2 0.8 copy-start.7
  60.9 5.7 %collective-permute-start.7 = (f32[88,512]{1,0:T(8,128)}, f32[88,512]{1,0:T(8,128)S(1)}, u32[]{:S(2)}, u32[]{:S(2)}) collective-permute-start(f32[88,512]{1,0:T(8,128)} %get-tuple-element.38), channel_id=1, source_target_pairs={{0,8},{4,12},{8,0},{12,4},{16,24},{20,28},{24,16},{28,20},{1,9},{5... | collective-permute-start | bytes 540680 | tf_op jit(solution)/shard_map/ppermute | solution.py:22
  62.4 24.4 %collective-permute-start.12 = (bf16[2,128,1024]{2,1,0:T(8,128)(2,1)}, bf16[2,128,1024]{2,1,0:T(8,128)(2,1)S(1)}, u32[]{:S(2)}, u32[]{:S(2)}) collective-permute-start(bf16[2,128,1024]{2,1,0:T(8,128)(2,1)} %get-tuple-element.45), channel_id=1, source_target_pairs={{0,1},{1,0},{2,3},{3,2},{4,5},{5,4},{6,7},{7,6},{8,9},{9,8},{10,11... | collective-permute-start | bytes 1572872 | tf_op jit(solution)/shard_map/ppermute | solution.py:22
  67.5 8.4 %collective-permute-start.8 = (f32[88,512]{1,0:T(8,128)S(1)}, f32[88,512]{1,0:T(8,128)S(1)}, u32[]{:S(2)}, u32[]{:S(2)}) collective-permute-start(f32[88,512]{1,0:T(8,128)S(1)} %add.94), channel_id=1, source_target_pairs={{0,16},{4,20},{8,24},{12,28},{16,0},{20,4},{24,8},{28,12},{1,17},{... | collective-permute-start | bytes 540680 | tf_op jit(solution)/shard_map/ppermute | solution.py:22
  75.9 10.9 %copy-start.2 = (bf16[2,128,1024]{2,1,0:T(8,128)(2,1)S(1)}, bf16[2,128,1024]{2,1,0:T(8,128)(2,1)}, u32[]{:S(2)}) copy-start(bf16[2,128,1024]{2,1,0:T(8,128)(2,1)} %get-tuple-element.44) | copy-start | bytes 1572868
  76.0 5.6 %collective-permute-start.9 = (f32[88,512]{1,0:T(8,128)S(1)}, f32[88,512]{1,0:T(8,128)S(1)}, u32[]{:S(2)}, u32[]{:S(2)}) collective-permute-start(f32[88,512]{1,0:T(8,128)S(1)} %add.95), channel_id=1, source_target_pairs={{0,4},{4,0},{8,12},{12,8},{16,20},{20,16},{24,28},{28,24},{1,5},{5... | collective-permute-start | bytes 540680 | tf_op jit(solution)/shard_map/ppermute | solution.py:22
  86.8 2.1 %copy-start.4 = (bf16[2,128,1024]{2,1,0:T(8,128)(2,1)S(1)}, bf16[2,128,1024]{2,1,0:T(8,128)(2,1)}, u32[]{:S(2)}) copy-start(bf16[2,128,1024]{2,1,0:T(8,128)(2,1)} %get-tuple-element.42) | copy-start | bytes 1572868
  86.8 2.1 %collective-permute-start.10 = (bf16[2,128,1024]{2,1,0:T(8,128)(2,1)}, bf16[2,128,1024]{2,1,0:T(8,128)(2,1)S(1)}, u32[]{:S(2)}, u32[]{:S(2)}) collective-permute-start(bf16[2,128,1024]{2,1,0:T(8,128)(2,1)} %get-tuple-element.43), channel_id=1, source_target_pairs={{0,1},{1,0},{2,3},{3,2},{4,5},{5,4},{6,7},{7,6},{8,9},{9,8},{10,11... | collective-permute-start | bytes 1572872 | tf_op jit(solution)/shard_map/ppermute | solution.py:22
  87.0 9.2 %collective-permute-start.13 = (bf16[1,128,1024]{2,1,0:T(8,128)(2,1)S(1)}, bf16[1,128,1024]{2,1,0:T(8,128)(2,1)S(1)}, u32[]{:S(2)}, u32[]{:S(2)}) collective-permute-start(bf16[1,128,1024]{2,1,0:T(8,128)(2,1)S(1)} %constant_dynamic-slice_fusion), channel_id=1, source_target_pairs={{0,2},{1,3},{2,0},{3,1},{4,6},{5,7},{6,4},{7,5},{8,10},{9,11},{10,... | collective-permute-start | bytes 786440 | tf_op jit(solution)/shard_map/ppermute | solution.py:22
  89.1 12.3 %collective-permute-start.11 = (bf16[1,128,1024]{2,1,0:T(8,128)(2,1)S(1)}, bf16[1,128,1024]{2,1,0:T(8,128)(2,1)S(1)}, u32[]{:S(2)}, u32[]{:S(2)}) collective-permute-start(bf16[1,128,1024]{2,1,0:T(8,128)(2,1)S(1)} %constant_dynamic-slice_fusion.1), channel_id=1, source_target_pairs={{0,2},{1,3},{2,0},{3,1},{4,6},{5,7},{6,4},{7,5},{8,10},{9,11},{10,... | collective-permute-start | bytes 786440 | tf_op jit(solution)/shard_map/ppermute | solution.py:22
  96.4 26.5 %copy-start = (f32[88,512]{1,0:T(8,128)S(1)}, f32[88,512]{1,0:T(8,128)}, u32[]{:S(2)}) copy-start(f32[88,512]{1,0:T(8,128)} %add.96.prob_ref) | copy-start | bytes 540676
  101.5 7.9 %collective-permute-start.14 = (bf16[64,2048]{1,0:T(8,128)(2,1)S(1)}, bf16[64,2048]{1,0:T(8,128)(2,1)S(1)}, u32[]{:S(2)}, u32[]{:S(2)}) collective-permute-start(bf16[64,2048]{1,0:T(8,128)(2,1)S(1)} %fusion.2), channel_id=1, source_target_pairs={{0,4},{4,0},{8,12},{12,8},{16,20},{20,16},{24,28},{28,24},{1,5},{5... | collective-permute-start | bytes 786440 | tf_op jit(solution)/shard_map/ppermute | solution.py:22
  109.5 4.5 %collective-permute-start.15 = (bf16[16,2048]{1,0:T(8,128)(2,1)S(1)}, bf16[16,2048]{1,0:T(8,128)(2,1)S(1)}, u32[]{:S(2)}, u32[]{:S(2)}) collective-permute-start(bf16[16,2048]{1,0:T(8,128)(2,1)S(1)} %get-tuple-element.63), channel_id=1, source_target_pairs={{0,8},{4,12},{8,0},{12,4},{16,24},{20,28},{24,16},{28,20},{1,9},{5... | collective-permute-start | bytes 196616 | tf_op jit(solution)/shard_map/ppermute | solution.py:22
  109.6 5.4 %collective-permute-start.16 = (bf16[16,2048]{1,0:T(8,128)(2,1)S(1)}, bf16[16,2048]{1,0:T(8,128)(2,1)S(1)}, u32[]{:S(2)}, u32[]{:S(2)}) collective-permute-start(bf16[16,2048]{1,0:T(8,128)(2,1)S(1)} %get-tuple-element.65), channel_id=1, source_target_pairs={{0,16},{4,20},{8,24},{12,28},{16,0},{20,4},{24,8},{28,12},{1,17},{... | collective-permute-start | bytes 196616 | tf_op jit(solution)/shard_map/ppermute | solution.py:22
  112.2 6.2 %collective-permute-start.17 = (bf16[16,2048]{1,0:T(8,128)(2,1)S(1)}, bf16[16,2048]{1,0:T(8,128)(2,1)S(1)}, u32[]{:S(2)}, u32[]{:S(2)}) collective-permute-start(bf16[16,2048]{1,0:T(8,128)(2,1)S(1)} %get-tuple-element.64), channel_id=1, source_target_pairs={{0,24},{4,28},{8,16},{12,20},{16,8},{20,12},{24,0},{28,4},{1,25},{... | collective-permute-start | bytes 196616 | tf_op jit(solution)/shard_map/ppermute | solution.py:22
  118.4 6.1 %collective-permute-start.18 = (bf16[16,2048]{1,0:T(8,128)(2,1)S(1)}, bf16[16,2048]{1,0:T(8,128)(2,1)S(1)}, u32[]{:S(2)}, u32[]{:S(2)}) collective-permute-start(bf16[16,2048]{1,0:T(8,128)(2,1)S(1)} %fusion.7), channel_id=1, source_target_pairs={{0,24},{4,28},{8,16},{12,20},{16,8},{20,12},{24,0},{28,4},{1,25},{... | collective-permute-start | bytes 196616 | tf_op jit(solution)/shard_map/ppermute | solution.py:22
  120.2 5.7 %collective-permute-start.19 = (bf16[16,2048]{1,0:T(8,128)(2,1)S(1)}, bf16[16,2048]{1,0:T(8,128)(2,1)S(1)}, u32[]{:S(2)}, u32[]{:S(2)}) collective-permute-start(bf16[16,2048]{1,0:T(8,128)(2,1)S(1)} %fusion.7), channel_id=1, source_target_pairs={{0,16},{4,20},{8,24},{12,28},{16,0},{20,4},{24,8},{28,12},{1,17},{... | collective-permute-start | bytes 196616 | tf_op jit(solution)/shard_map/ppermute | solution.py:22
  120.2 5.7 %collective-permute-start.20 = (bf16[16,2048]{1,0:T(8,128)(2,1)S(1)}, bf16[16,2048]{1,0:T(8,128)(2,1)S(1)}, u32[]{:S(2)}, u32[]{:S(2)}) collective-permute-start(bf16[16,2048]{1,0:T(8,128)(2,1)S(1)} %fusion.7), channel_id=1, source_target_pairs={{0,8},{4,12},{8,0},{12,4},{16,24},{20,28},{24,16},{28,20},{1,9},{5... | collective-permute-start | bytes 196616 | tf_op jit(solution)/shard_map/ppermute | solution.py:22
  122.9 4.8 %collective-permute-start.22 = (f32[24,512]{1,0:T(8,128)S(1)}, f32[24,512]{1,0:T(8,128)S(1)}, u32[]{:S(2)}, u32[]{:S(2)}) collective-permute-start(f32[24,512]{1,0:T(8,128)S(1)} %slice.21), channel_id=1, source_target_pairs={{0,1},{1,0},{2,3},{3,2},{4,5},{5,4},{6,7},{7,6},{8,9},{9,8},{10,11... | collective-permute-start | bytes 147464 | tf_op jit(solution)/shard_map/ppermute | solution.py:22
  126.0 9.9 %collective-permute-start.21 = (bf16[64,2048]{1,0:T(8,128)(2,1)S(1)}, bf16[64,2048]{1,0:T(8,128)(2,1)S(1)}, u32[]{:S(2)}, u32[]{:S(2)}) collective-permute-start(bf16[64,2048]{1,0:T(8,128)(2,1)S(1)} %pad_maximum_fusion), channel_id=1, source_target_pairs={{0,4},{4,0},{8,12},{12,8},{16,20},{20,16},{24,28},{28,24},{1,5},{5... | collective-permute-start | bytes 786440 | tf_op jit(solution)/shard_map/ppermute | solution.py:22
  127.7 7.0 %collective-permute-start.23 = (f32[24,512]{1,0:T(8,128)S(1)}, f32[24,512]{1,0:T(8,128)S(1)}, u32[]{:S(2)}, u32[]{:S(2)}) collective-permute-start(f32[24,512]{1,0:T(8,128)S(1)} %slice_add_fusion), channel_id=1, source_target_pairs={{0,2},{1,3},{2,0},{3,1},{4,6},{5,7},{6,4},{7,5},{8,10},{9,11},{10,... | collective-permute-start | bytes 147464 | tf_op jit(solution)/shard_map/ppermute | solution.py:22

commit v5 on v4

--- a/solution.py
+++ b/solution.py
@@ -232,8 +232,8 @@
 
 
 def attend_kernel(
-    edge_ref, sharp_ref, pack_ref, x_ref, near_ref, far_ref, value_ref, gain_one_ref, gain_two_ref,
-    factor_ref, w_value_ref, w_out_ref, kernel_ref,
+    edge_ref, sharp_ref, pack_ref, x_ref, near_ref, far_ref, mixed_ref, gain_one_ref, gain_two_ref,
+    factor_ref, w_qkv_ref, w_out_ref, kernel_ref,
     attended_ref, projected_ref, residual_ref, act_mid_ref, hidden_ref, slope_ref, act_ext, diag_ref,
 ):
     rows, width, dim = x_ref.shape
@@ -263,7 +263,7 @@
             residual_ref[span, :] = residual
 
     for row in range(rows):
-        value = value_ref[row * width : (row + 1) * width, :]
+        value = mixed_ref[row * width : (row + 1) * width, 2 * dim :]
         token_part(x_ref[row].astype(F32), value, EDGE + row, row)
     even = edge_ref[0]
     for ref, place, source in (
@@ -274,7 +274,7 @@
             x_rows = ref[source + row].astype(F32)
             normed, _ = norm_stats(x_rows)
             act = (normed * gain_one_ref[...]).astype(BF16)
-            value = dot32(act, w_value_ref[...], 1, 0).astype(BF16)
+            value = dot32(act, w_qkv_ref[:, 2 * dim :], 1, 0).astype(BF16)
             token_part(x_rows, value, place + row, None)
     for row in range(rows + 2):
         act_mid_ref[row] = act_ext[row + 1, PAD : PAD + width, :].astype(BF16)
@@ -296,7 +296,7 @@
 
 def back_kernel(
     edge_ref, sharp_ref, pack_ref, up_ref, near_ref, far_ref, act_mid_ref, hidden_ref, slope_ref,
-    attended_ref, projected_ref, residual_ref, value_ref, act_one_ref, gain_two_ref, factor_ref,
+    attended_ref, projected_ref, residual_ref, mixed_ref, act_one_ref, gain_two_ref, factor_ref,
     w_out_ref, kernel_ref,
     prob_out_ref, d_res_ref, d_value_ref, keep_ref, give_ref,
     up_ext, d_ext, hid_ext, d_act, sums, d_proj_ref, d_att_ref, grad_ref,
@@ -405,7 +405,7 @@
         lanes = slice(block * LANES, (block + 1) * LANES)
         prob, *_, block_id, _ = softmax_block(pack_ref, sharp_ref, block, head_dim)
         d_att = d_att_ref[:, lanes]
-        prob_out_ref[:head_dim, lanes] = compact(block_id, dot32(d_att, value_ref[:, lanes], 0, 0))
+        prob_out_ref[:head_dim, lanes] = compact(block_id, dot32(d_att, mixed_ref[:, 2 * dim + block * LANES : 2 * dim + (block + 1) * LANES], 0, 0))
         d_value_ref[:, lanes] = dot32(d_att, block_diag(block_id, prob), 1, 0).astype(BF16)
     grad_ref[:, :dim] = dot32(act_one_ref[...], d_value_ref[...], 0, 0).astype(BF16)
     grad_ref[:, dim:] = dot32(attended_ref[...], d_proj_ref[...], 0, 0).astype(BF16)
@@ -465,22 +465,22 @@
         ).astype(BF16)
 
 
-def call(body, outs, args, scalars=0, scratch=(), thirds=()):
-    specs = []
-    for i, arg in enumerate(args):
-        if i < scalars:
-            specs.append(pl.BlockSpec(memory_space=pltpu.SMEM))
-        elif i in thirds:
-            specs.append(pl.BlockSpec((arg.shape[0], arg.shape[1] // 3), lambda i: (0, 2)))
-        else:
-            specs.append(pl.BlockSpec(arg.shape, lambda i, n=arg.ndim: (0,) * n))
+def call(body, outs, args, scalars=0, scratch=(), limit=16):
+    args = [
+        arg if i < scalars else pltpu.with_memory_space_constraint(arg, pltpu.VMEM)
+        for i, arg in enumerate(args)
+    ]
+    specs = [
+        pl.BlockSpec(memory_space=pltpu.SMEM if i < scalars else pltpu.VMEM)
+        for i in range(len(args))
+    ]
     return pl.pallas_call(
         body,
-        grid=(1,),
-        out_shape=[jax.ShapeDtypeStruct(shape, dtype) for shape, dtype in outs],
+        out_shape=[pltpu.VMEM(shape, dtype) for shape, dtype in outs],
         in_specs=specs,
-        out_specs=[pl.BlockSpec(o[0], lambda i, n=len(o[0]): (0,) * n) for o in outs],
+        out_specs=[pl.BlockSpec(memory_space=pltpu.VMEM)] * len(outs),
         scratch_shapes=[pltpu.VMEM(shape, dtype) for shape, dtype in scratch],
+        compiler_params=pltpu.CompilerParams(vmem_limit_bytes=limit << 20),
     )(*args)
 
 
@@ -537,7 +537,6 @@
         (edges, sharp, pack, x_own, x_near, x_far, mixed, gain_one, gain_two, factors,
          w_qkv, w_out, taps),
         scalars=2,
-        thirds=(6, 10),
         scratch=[((rows + 2 * EDGE, width + 2 * PAD, dim), F32), ((dim // LANES, LANES, LANES), BF16)],
     )
     blocks = lax.axis_size("rep")
@@ -548,7 +547,6 @@
         (edges, sharp, pack, up_own, up_near, up_far, act_mid, hidden, slope, attended, projected,
          residual, mixed, act_one, gain_two, factors, w_out, taps),
         scalars=2,
-        thirds=(12,),
         scratch=[((rows + 2 * EDGE, width + 2 * PAD, dim), F32),
                  ((rows + 2, width + 2 * PAD, dim), F32), ((rows, width + 2 * PAD, dim), F32),
                  ((rows, width, dim), F32), ((18, 8, dim), F32), ((tokens, dim), BF16),

time: 138 us -> 144 us (1.043)
  Pallas kernels: 37.8 us -> 25.4 us
  local copies, waits for them, and re-layouts: 4.56 us -> 16.7 us
  other arithmetic: 5.58 us -> 12.7 us
  starting transfers between devices: 35.7 us -> 34 us
    pallas_call x5, Pallas kernels: 37.8 us -> 25.4 us  [call(): pl.pallas_call(body, out_shape=[pltpu.VMEM(shape, dtype) for shape, dtype...]
    unnamed x20 -> x73, local copies, waits for them, and re-layouts: 2.29 us -> 13.7 us
    convert_element_type x6, other arithmetic: 0.62 us -> 5.81 us  [add_low(): return total.astype(BF16)]
    ppermute x22, starting transfers between devices: 28.5 us -> 25.2 us  [swap_bit(): return lax.ppermute(value, axis, [(i, i ^ bit) for i in range(count)])]
    select_n x2, other arithmetic: 0.13 us -> 2.04 us  [gather_stage(): chosen = jnp.where(mine == piece ^ offset, parts[offset], chosen)]
    add x3, other arithmetic: 1.67 us -> 0.08 us  [shards(): probs.append(probs[-1] + swap_bit(probs[-1], 'sp', bit))]
    ppermute x2, starting transfers between devices: 7.25 us -> 8.81 us  [beyond(): return lax.ppermute(value, 'sp', hops)]
  transfers between devices with their start and end apart: 24 -> 24, of which waited for: 15 -> 15; matrix products, arithmetic and copies ran while one was open for 5% -> 8% of each run, Pallas kernels for 19% -> 11%
where the time goes in v5:
time: 144 us; the launch traced here: 143 us
  waiting for transfers between devices  53.6 us (37%)
  starting transfers between devices  34 us (24%)
  Pallas kernels  25.4 us (18%)
  local copies, waits for them, and re-layouts  16.7 us (12%)
  other arithmetic  12.7 us (9%)
    ppermute x22, waiting for transfers between devices, swap_bit(): return lax.ppermute(value, axis, [(i, i ^ bit) for i in range(count)])  53.6 us
    pallas_call x5, Pallas kernels, call(): pl.pallas_call(body, out_shape=[pltpu.VMEM(shape, dtype) for shape, dtype...  25.4 us
    ppermute x22, starting transfers between devices, swap_bit(): return lax.ppermute(value, axis, [(i, i ^ bit) for i in range(count)])  25.2 us
    unnamed x73, local copies, waits for them, and re-layouts  13.7 us
    ppermute x2, starting transfers between devices, beyond(): return lax.ppermute(value, 'sp', hops)  8.81 us
    convert_element_type x6, other arithmetic, add_low(): return total.astype(BF16)  5.81 us
  transfers between devices with their start and end apart: 24, of which 15 were waited for; matrix products, arithmetic and copies ran while one was open for 8% of the time, Pallas kernels for 11%

profile of v5, /device:TPU:0, one launch (start us, length us, event | category | flops | bytes accessed | tf_op | source)
XLA Modules:
  0.0 143.4 jit_solution(9013146808662030099)
XLA Ops:
  0.6 3.0 %collective-permute-start.5 = (bf16[2,256,512]{2,1,0:T(8,128)(2,1)}, bf16[2,256,512]{2,1,0:T(8,128)(2,1)}, u32[]{:S(2)}, u32[]{:S(2)}) collective-permute-start(bf16[2,256,512]{2,1,0:T(8,128)(2,1)} %bitcast.31), channel_id=1, source_target_pairs={{0,4},{4,0},{8,12},{12,8},{16,20},{20,16},{24,28},{28,24},{1,5},{5... | collective-permute-start | bytes 1572872 | tf_op jit(solution)/shard_map/ppermute | solution.py:22
  3.7 1.4 copy-done
  5.1 1.0 copy-done.2
  6.1 0.7 copy-done.20
  6.8 2.7 %shard_map.128 = (bf16[512,1536]{1,0:T(8,128)(2,1)S(1)}, bf16[512,512]{1,0:T(8,128)(2,1)S(1)}, f32[72,512]{1,0:T(8,128)S(1)}) custom-call(bf16[512,512]{1,0:T(8,128)(2,1)S(1)} %bitcast.32, f32[1,512]{1,0:T(1,128)S(1)} %bitcast.37, bf16[512,1536]{1,0:T(8,128)(2,1)S(1)} %copy-done), custom_call_target="tpu_custom_call" | custom-call | tf_op jit(solution)/shard_map/pallas_call | solution.py:477
  9.6 0.8 copy-done.7
  10.4 2.1 %collective-permute-start = (f32[72,512]{1,0:T(8,128)S(1)}, f32[72,512]{1,0:T(8,128)S(1)}, u32[]{:S(2)}, u32[]{:S(2)}) collective-permute-start(f32[72,512]{1,0:T(8,128)S(1)} %get-tuple-element.26), channel_id=1, source_target_pairs={{0,8},{4,12},{8,0},{12,4},{16,24},{20,28},{24,16},{28,20},{1,9},{5... | collective-permute-start | bytes 442376 | tf_op jit(solution)/shard_map/ppermute | solution.py:22
  12.5 3.3 %collective-permute-done = f32[72,512]{1,0:T(8,128)S(1)} collective-permute-done((f32[72,512]{1,0:T(8,128)S(1)}, f32[72,512]{1,0:T(8,128)S(1)}, u32[]{:S(2)}, u32[]{:S(2)}) %collective-permute-start) | collective-permute-done | bytes 147488 | tf_op jit(solution)/shard_map/ppermute | solution.py:22
  15.8 2.9 %collective-permute-start.1 = (f32[72,512]{1,0:T(8,128)S(1)}, f32[72,512]{1,0:T(8,128)S(1)}, u32[]{:S(2)}, u32[]{:S(2)}) collective-permute-start(f32[72,512]{1,0:T(8,128)S(1)} %add.91), channel_id=1, source_target_pairs={{0,16},{4,20},{8,24},{12,28},{16,0},{20,4},{24,8},{28,12},{1,17},{... | collective-permute-start | bytes 442376 | tf_op jit(solution)/shard_map/ppermute | solution.py:22
  18.7 4.3 %collective-permute-start.6 = (bf16[2,256,512]{2,1,0:T(8,128)(2,1)}, bf16[2,256,512]{2,1,0:T(8,128)(2,1)}, u32[]{:S(2)}, u32[]{:S(2)}) collective-permute-start(bf16[2,256,512]{2,1,0:T(8,128)(2,1)} %collective-permute-done.5.near_ref), channel_id=1, source_target_pairs={{12,4},{20,12},{28,20},{0,8},{8,16},{16,24},{13,5},{21,13},{29,21}... | collective-permute-start | bytes 1572872 | tf_op jit(solution)/shard_map/ppermute | solution.py:495
  23.0 1.5 %collective-permute-done.1 = f32[72,512]{1,0:T(8,128)S(1)} collective-permute-done((f32[72,512]{1,0:T(8,128)S(1)}, f32[72,512]{1,0:T(8,128)S(1)}, u32[]{:S(2)}, u32[]{:S(2)}) %collective-permute-start.1) | collective-permute-done | bytes 147488 | tf_op jit(solution)/shard_map/ppermute | solution.py:22
  24.5 2.6 %collective-permute-done.3.near_ref = bf16[2,256,512]{2,1,0:T(8,128)(2,1)} collective-permute-done((bf16[2,256,512]{2,1,0:T(8,128)(2,1)S(1)}, bf16[2,256,512]{2,1,0:T(8,128)(2,1)}, u32[]{:S(2)}, u32[]{:S(2)}) %collective-permute-start.3) | collective-permute-done | bytes 524320 | tf_op jit(solution)/shard_map/ppermute | solution.py:22
  27.1 4.5 %collective-permute-start.4 = (bf16[2,256,512]{2,1,0:T(8,128)(2,1)}, bf16[2,256,512]{2,1,0:T(8,128)(2,1)}, u32[]{:S(2)}, u32[]{:S(2)}) collective-permute-start(bf16[2,256,512]{2,1,0:T(8,128)(2,1)} %collective-permute-done.3.near_ref), channel_id=1, source_target_pairs={{12,4},{20,12},{28,20},{0,8},{8,16},{16,24},{13,5},{21,13},{29,21}... | collective-permute-start | bytes 1572872 | tf_op jit(solution)/shard_map/ppermute | solution.py:495
  31.8 5.1 %collective-permute-done.2 = f32[72,512]{1,0:T(8,128)} collective-permute-done((f32[72,512]{1,0:T(8,128)S(1)}, f32[72,512]{1,0:T(8,128)}, u32[]{:S(2)}, u32[]{:S(2)}) %collective-permute-start.2) | collective-permute-done | bytes 147488 | tf_op jit(solution)/shard_map/ppermute | solution.py:22
  36.9 0.9 add.93.pack_ref
  37.9 1.0 copy-done.3
  39.0 1.0 copy-done.5
  40.0 7.7 %shard_map.129 = (bf16[512,512]{1,0:T(8,128)(2,1)S(1)}, f32[512,512]{1,0:T(8,128)S(1)}, bf16[512,512]{1,0:T(8,128)(2,1)S(1)}, bf16[4,256,512]{2,1,0:T(8,128)(2,1...) custom-call(s32[4]{0:T(128)S(1)} %pad_add_fusion.edge_ref, f32[8]{0:T(128)S(1)} %copy-done.24, ...), custom_call_target="tpu_custom_call" | custom-call | tf_op jit(solution)/shard_map/pallas_call | solution.py:477
  47.7 9.3 %shard_map.130 = (f32[88,512]{1,0:T(8,128)S(1)}, f32[512,512]{1,0:T(8,128)S(1)}, bf16[512,512]{1,0:T(8,128)(2,1)S(1)}, bf16[2,128,1024]{2,1,0:T(8,128)(2,1)S(1)}, bf16[2,128,1024]{2,1,0:T(8,128)(2,1)}) custom-call(s32[4]{0:T(128)S(1)} %pad_add_fusion.edge_ref, f32[8]{0:T(128)S(1)} %copy-done.24, f32[72,512]{1,0:T(8,128)S(1)} %add.93.pack_ref, ...), custom_call_target="tpu_custom_call" | custom-call | tf_op jit(solution)/shard_map/pallas_call | solution.py:477
  57.0 0.9 collective-permute-start.7
  57.9 4.7 %collective-permute-done.7 = f32[88,512]{1,0:T(8,128)S(1)} collective-permute-done((f32[88,512]{1,0:T(8,128)S(1)}, f32[88,512]{1,0:T(8,128)S(1)}, u32[]{:S(2)}, u32[]{:S(2)}) %collective-permute-start.7) | collective-permute-done | bytes 180256 | tf_op jit(solution)/shard_map/ppermute | solution.py:22
  62.6 2.5 %collective-permute-start.8 = (f32[88,512]{1,0:T(8,128)S(1)}, f32[88,512]{1,0:T(8,128)S(1)}, u32[]{:S(2)}, u32[]{:S(2)}) collective-permute-start(f32[88,512]{1,0:T(8,128)S(1)} %add.94), channel_id=1, source_target_pairs={{0,16},{4,20},{8,24},{12,28},{16,0},{20,4},{24,8},{28,12},{1,17},{... | collective-permute-start | bytes 540680 | tf_op jit(solution)/shard_map/ppermute | solution.py:22
  65.2 6.3 %collective-permute-done.8 = f32[88,512]{1,0:T(8,128)S(1)} collective-permute-done((f32[88,512]{1,0:T(8,128)S(1)}, f32[88,512]{1,0:T(8,128)S(1)}, u32[]{:S(2)}, u32[]{:S(2)}) %collective-permute-start.8) | collective-permute-done | bytes 180256 | tf_op jit(solution)/shard_map/ppermute | solution.py:22
  71.7 5.4 %collective-permute-done.9 = f32[88,512]{1,0:T(8,128)S(1)} collective-permute-done((f32[88,512]{1,0:T(8,128)S(1)}, f32[88,512]{1,0:T(8,128)S(1)}, u32[]{:S(2)}, u32[]{:S(2)}) %collective-permute-start.9) | collective-permute-done | bytes 180256 | tf_op jit(solution)/shard_map/ppermute | solution.py:22
  77.1 3.3 %shard_map.131 = (bf16[512,1024]{1,0:T(8,128)(2,1)S(1)}, bf16[2,128,1024]{2,1,0:T(8,128)(2,1)S(1)}, bf16[2,128,1024]{2,1,0:T(8,128)(2,1)}) custom-call(s32[4]{0:T(128)S(1)} %pad_add_fusion.edge_ref, f32[8]{0:T(128)S(1)} %copy-done.24, f32[72,512]{1,0:T(8,128)S(1)} %add.93.pack_ref, f32[88,512]{1,0:T(8,128)S(1)} %add.96.prob_ref, ...), custom_call_target="tpu_custom_call" | custom-call | tf_op jit(solution)/shard_map/pallas_call | solution.py:477
  80.4 1.0 copy-done.11
  81.4 0.8 copy-done.16
  82.2 1.4 %add_convert_fusion = bf16[2,128,1024]{2,1,0:T(8,128)(2,1)S(1)} fusion(bf16[2,128,1024]{2,1,0:T(8,128)(2,1)} %collective-permute-done.12, bf16[2,128,1024]{2,1,0:T(8,128)(2,1)} %copy-done.15), kind=kLoop, calls=%fused_computation | loop fusion | flops 1048576 | bytes 1572864 | tf_op jit(solution)/shard_map/convert_element_type | solution.py:43
  83.6 0.7 constant_dynamic-slice_fusion
  84.4 1.5 %collective-permute-start.13 = (bf16[1,128,1024]{2,1,0:T(8,128)(2,1)}, bf16[1,128,1024]{2,1,0:T(8,128)(2,1)}, u32[]{:S(2)}, u32[]{:S(2)}) collective-permute-start(bf16[1,128,1024]{2,1,0:T(8,128)(2,1)} %constant_dynamic-slice_fusion), channel_id=1, source_target_pairs={{0,2},{1,3},{2,0},{3,1},{4,6},{5,7},{6,4},{7,5},{8,10},{9,11},{10,... | collective-permute-start | bytes 786440 | tf_op jit(solution)/shard_map/ppermute | solution.py:22
  85.9 0.8 copy-done.30
  86.7 1.2 add_convert_fusion.1
  88.5 5.3 %collective-permute-done.13 = bf16[1,128,1024]{2,1,0:T(8,128)(2,1)} collective-permute-done((bf16[1,128,1024]{2,1,0:T(8,128)(2,1)}, bf16[1,128,1024]{2,1,0:T(8,128)(2,1)}, u32[]{:S(2)}, u32[]{:S(2)}) %collective-permute-start.13) | collective-permute-done | bytes 262176 | tf_op jit(solution)/shard_map/ppermute | solution.py:22
  93.8 1.0 add_convert_fusion.2
  94.9 3.9 %collective-permute-done.11 = bf16[1,128,1024]{2,1,0:T(8,128)(2,1)S(1)} collective-permute-done((bf16[1,128,1024]{2,1,0:T(8,128)(2,1)S(1)}, bf16[1,128,1024]{2,1,0:T(8,128)(2,1)S(1)}, u32[]{:S(2)}, u32[]{:S(2)}) %collective-permute-start.11) | collective-permute-done | bytes 262176 | tf_op jit(solution)/shard_map/ppermute | solution.py:22
  98.9 0.8 fusion.2
  99.8 8.0 %collective-permute-done.14 = bf16[64,2048]{1,0:T(8,128)(2,1)} collective-permute-done((bf16[64,2048]{1,0:T(8,128)(2,1)}, bf16[64,2048]{1,0:T(8,128)(2,1)}, u32[]{:S(2)}, u32[]{:S(2)}) %collective-permute-start.14) | collective-permute-done | bytes 262176 | tf_op jit(solution)/shard_map/ppermute | solution.py:22
  107.8 1.1 fusion
  108.9 0.7 copy-done.27
  109.6 0.7 dynamic-slice_bitcast_fusion.2
  110.3 2.6 %collective-permute-start.16 = (bf16[16,2048]{1,0:T(8,128)(2,1)}, bf16[16,2048]{1,0:T(8,128)(2,1)S(1)}, u32[]{:S(2)}, u32[]{:S(2)}) collective-permute-start(bf16[16,2048]{1,0:T(8,128)(2,1)} %get-tuple-element.65), channel_id=1, source_target_pairs={{0,16},{4,20},{8,24},{12,28},{16,0},{20,4},{24,8},{28,12},{1,17},{... | collective-permute-start | bytes 196616 | tf_op jit(solution)/shard_map/ppermute | solution.py:22
  113.0 1.7 %collective-permute-start.17 = (bf16[16,2048]{1,0:T(8,128)(2,1)S(1)}, bf16[16,2048]{1,0:T(8,128)(2,1)}, u32[]{:S(2)}, u32[]{:S(2)}) collective-permute-start(bf16[16,2048]{1,0:T(8,128)(2,1)S(1)} %get-tuple-element.64), channel_id=1, source_target_pairs={{0,24},{4,28},{8,16},{12,20},{16,8},{20,12},{24,0},{28,4},{1,25},{... | collective-permute-start | bytes 196616 | tf_op jit(solution)/shard_map/ppermute | solution.py:22
  114.8 2.4 %collective-permute-done.16 = bf16[16,2048]{1,0:T(8,128)(2,1)S(1)} collective-permute-done((bf16[16,2048]{1,0:T(8,128)(2,1)}, bf16[16,2048]{1,0:T(8,128)(2,1)S(1)}, u32[]{:S(2)}, u32[]{:S(2)}) %collective-permute-start.16) | collective-permute-done | bytes 65568 | tf_op jit(solution)/shard_map/ppermute | solution.py:22
  117.2 2.0 %collective-permute-done.17 = bf16[16,2048]{1,0:T(8,128)(2,1)} collective-permute-done((bf16[16,2048]{1,0:T(8,128)(2,1)S(1)}, bf16[16,2048]{1,0:T(8,128)(2,1)}, u32[]{:S(2)}, u32[]{:S(2)}) %collective-permute-start.17) | collective-permute-done | bytes 65568 | tf_op jit(solution)/shard_map/ppermute | solution.py:22
  119.2 0.9 fusion.7
  120.1 1.8 %collective-permute-start.18 = (bf16[16,2048]{1,0:T(8,128)(2,1)S(1)}, bf16[16,2048]{1,0:T(8,128)(2,1)S(1)}, u32[]{:S(2)}, u32[]{:S(2)}) collective-permute-start(bf16[16,2048]{1,0:T(8,128)(2,1)S(1)} %fusion.7), channel_id=1, source_target_pairs={{0,24},{4,28},{8,16},{12,20},{16,8},{20,12},{24,0},{28,4},{1,25},{... | collective-permute-start | bytes 196616 | tf_op jit(solution)/shard_map/ppermute | solution.py:22
  121.9 2.7 %collective-permute-start.20 = (bf16[16,2048]{1,0:T(8,128)(2,1)S(1)}, bf16[16,2048]{1,0:T(8,128)(2,1)}, u32[]{:S(2)}, u32[]{:S(2)}) collective-permute-start(bf16[16,2048]{1,0:T(8,128)(2,1)S(1)} %fusion.7), channel_id=1, source_target_pairs={{0,8},{4,12},{8,0},{12,4},{16,24},{20,28},{24,16},{28,20},{1,9},{5... | collective-permute-start | bytes 196616 | tf_op jit(solution)/shard_map/ppermute | solution.py:22
  124.6 1.7 %collective-permute-done.18 = bf16[16,2048]{1,0:T(8,128)(2,1)S(1)} collective-permute-done((bf16[16,2048]{1,0:T(8,128)(2,1)S(1)}, bf16[16,2048]{1,0:T(8,128)(2,1)S(1)}, u32[]{:S(2)}, u32[]{:S(2)}) %collective-permute-start.18) | collective-permute-done | bytes 65568 | tf_op jit(solution)/shard_map/ppermute | solution.py:22
  126.3 1.4 collective-permute-done.19
  127.7 0.6 copy-done.33
  128.3 1.0 select_select_fusion.3
  129.3 0.7 pad_maximum_fusion
  130.0 0.9 collective-permute-start.21
  130.9 0.6 slice_add_fusion
  131.5 1.5 %collective-permute-start.23 = (f32[24,512]{1,0:T(8,128)}, f32[24,512]{1,0:T(8,128)S(1)}, u32[]{:S(2)}, u32[]{:S(2)}) collective-permute-start(f32[24,512]{1,0:T(8,128)} %slice_add_fusion), channel_id=1, source_target_pairs={{0,2},{1,3},{2,0},{3,1},{4,6},{5,7},{6,4},{7,5},{8,10},{9,11},{10,... | collective-permute-start | bytes 147464 | tf_op jit(solution)/shard_map/ppermute | solution.py:22
  133.0 1.2 copy-done.12
  134.2 1.0 copy-done.14
  135.3 2.4 %shard_map.132 = bf16[512,512]{1,0:T(8,128)(2,1)S(1)} custom-call(bf16[512,512]{1,0:T(8,128)(2,1)S(1)} %bitcast.34, f32[1,512]{1,0:T(1,128)S(1)} %bitcast.39, bf16[512,1536]{1,0:T(8,128)(2,1)S(1)} %copy-done.1, bf16[512,1024]{1,0:T(8,128)(2,1)S(1)} %copy-done.12, bf16[512,512]{1,0:T(8,128)(2,1)S(1)} %copy-done.14, f32[512,512]{1,0:T(8,128)S(1)} %copy-done.10), custom_call_target="tpu_custom_call" | custom-call | tf_op jit(solution)/shard_map/pallas_call | solution.py:477
  137.7 0.8 copy.18
  138.5 0.8 add.115
  139.9 0.6 copy.17
  140.6 1.1 broadcast_select_fusion.1
  141.6 0.7 maximum_convert_fusion.1
  142.5 0.9 slice.20
  (91 shorter events, 2.2 us)
Async XLA Ops:
  0.6 18.1 %collective-permute-start.5 = (bf16[2,256,512]{2,1,0:T(8,128)(2,1)}, bf16[2,256,512]{2,1,0:T(8,128)(2,1)}, u32[]{:S(2)}, u32[]{:S(2)}) collective-permute-start(bf16[2,256,512]{2,1,0:T(8,128)(2,1)} %bitcast.31), channel_id=1, source_target_pairs={{0,4},{4,0},{8,12},{12,8},{16,20},{20,16},{24,28},{28,24},{1,5},{5... | collective-permute-start | bytes 1572872 | tf_op jit(solution)/shard_map/ppermute | solution.py:22
  3.7 1.4 copy-start
  5.1 1.0 copy-start.2
  6.1 0.7 copy-start.20
  6.8 3.6 %copy-start.18 = (bf16[1,2,256,512]{3,2,1,0:T(8,128)(2,1)S(1)}, bf16[1,2,256,512]{3,2,1,0:T(8,128)(2,1)}, u32[]{:S(2)}) copy-start(bf16[1,2,256,512]{3,2,1,0:T(8,128)(2,1)} %param.10) | copy-start | bytes 1572868
  6.8 24.9 %copy-start.34 = (f32[2,3,3,512]{3,0,2,1:T(2,128)S(1)}, f32[2,3,3,512]{3,0,2,1:T(2,128)}, u32[]{:S(2)}) copy-start(f32[2,3,3,512]{3,0,2,1:T(2,128)} %param.17) | copy-start | bytes 110596
  6.8 31.1 %copy-start.1 = (bf16[512,1536]{1,0:T(8,128)(2,1)S(1)}, bf16[512,1536]{1,0:T(8,128)(2,1)}, u32[]{:S(2)}) copy-start(bf16[512,1536]{1,0:T(8,128)(2,1)} %w_ref.3) | copy-start | bytes 4718596
  6.8 31.1 %copy-start.21 = (f32[512]{0:T(512)S(1)}, f32[512]{0:T(512)}, u32[]{:S(2)}) copy-start(f32[512]{0:T(512)} %param.11) | copy-start | bytes 6148
  6.8 31.1 %copy-start.22 = (f32[2,512]{1,0:T(2,128)S(1)}, f32[2,512]{1,0:T(2,128)}, u32[]{:S(2)}) copy-start(f32[2,512]{1,0:T(2,128)} %factor_ref.3) | copy-start | bytes 12292
  6.8 31.1 %copy-start.23 = (f32[512]{0:T(512)S(1)}, f32[512]{0:T(512)}, u32[]{:S(2)}) copy-start(f32[512]{0:T(512)} %param.16) | copy-start | bytes 6148
  6.8 31.1 %copy-start.24 = (f32[8]{0:T(128)S(1)}, f32[8]{0:T(128)}, u32[]{:S(2)}) copy-start(f32[8]{0:T(128)} %sharp_ref.5) | copy-start | bytes 100
  9.6 0.8 copy-start.7
  10.4 16.8 %collective-permute-start.3 = (bf16[2,256,512]{2,1,0:T(8,128)(2,1)S(1)}, bf16[2,256,512]{2,1,0:T(8,128)(2,1)}, u32[]{:S(2)}, u32[]{:S(2)}) collective-permute-start(bf16[2,256,512]{2,1,0:T(8,128)(2,1)S(1)} %bitcast.35), channel_id=1, source_target_pairs={{0,4},{4,0},{8,12},{12,8},{16,20},{20,16},{24,28},{28,24},{1,5},{5... | collective-permute-start | bytes 1572872 | tf_op jit(solution)/shard_map/ppermute | solution.py:22
  10.4 5.4 %collective-permute-start = (f32[72,512]{1,0:T(8,128)S(1)}, f32[72,512]{1,0:T(8,128)S(1)}, u32[]{:S(2)}, u32[]{:S(2)}) collective-permute-start(f32[72,512]{1,0:T(8,128)S(1)} %get-tuple-element.26), channel_id=1, source_target_pairs={{0,8},{4,12},{8,0},{12,4},{16,24},{20,28},{24,16},{28,20},{1,9},{5... | collective-permute-start | bytes 442376 | tf_op jit(solution)/shard_map/ppermute | solution.py:22
  15.8 8.7 %collective-permute-start.1 = (f32[72,512]{1,0:T(8,128)S(1)}, f32[72,512]{1,0:T(8,128)S(1)}, u32[]{:S(2)}, u32[]{:S(2)}) collective-permute-start(f32[72,512]{1,0:T(8,128)S(1)} %add.91), channel_id=1, source_target_pairs={{0,16},{4,20},{8,24},{12,28},{16,0},{20,4},{24,8},{28,12},{1,17},{... | collective-permute-start | bytes 442376 | tf_op jit(solution)/shard_map/ppermute | solution.py:22
  18.7 19.1 %collective-permute-start.6 = (bf16[2,256,512]{2,1,0:T(8,128)(2,1)}, bf16[2,256,512]{2,1,0:T(8,128)(2,1)}, u32[]{:S(2)}, u32[]{:S(2)}) collective-permute-start(bf16[2,256,512]{2,1,0:T(8,128)(2,1)} %collective-permute-done.5.near_ref), channel_id=1, source_target_pairs={{12,4},{20,12},{28,20},{0,8},{8,16},{16,24},{13,5},{21,13},{29,21}... | collective-permute-start | bytes 1572872 | tf_op jit(solution)/shard_map/ppermute | solution.py:495
  27.1 20.6 %collective-permute-start.4 = (bf16[2,256,512]{2,1,0:T(8,128)(2,1)}, bf16[2,256,512]{2,1,0:T(8,128)(2,1)}, u32[]{:S(2)}, u32[]{:S(2)}) collective-permute-start(bf16[2,256,512]{2,1,0:T(8,128)(2,1)} %collective-permute-done.3.near_ref), channel_id=1, source_target_pairs={{12,4},{20,12},{28,20},{0,8},{8,16},{16,24},{13,5},{21,13},{29,21}... | collective-permute-start | bytes 1572872 | tf_op jit(solution)/shard_map/ppermute | solution.py:495
  31.7 5.2 %collective-permute-start.2 = (f32[72,512]{1,0:T(8,128)S(1)}, f32[72,512]{1,0:T(8,128)}, u32[]{:S(2)}, u32[]{:S(2)}) collective-permute-start(f32[72,512]{1,0:T(8,128)S(1)} %add.92), channel_id=1, source_target_pairs={{0,4},{4,0},{8,12},{12,8},{16,20},{20,16},{24,28},{28,24},{1,5},{5... | collective-permute-start | bytes 442376 | tf_op jit(solution)/shard_map/ppermute | solution.py:22
  37.9 1.0 copy-start.3
  39.0 1.0 copy-start.5
  40.0 7.7 %copy-start.6 = (bf16[512,512]{1,0:T(8,128)(2,1)S(1)}, bf16[512,512]{1,0:T(8,128)(2,1)}, u32[]{:S(2)}) copy-start(bf16[512,512]{1,0:T(8,128)(2,1)} %w_out_ref.3) | copy-start | bytes 1572868
  40.0 7.7 %copy-start.8 = (bf16[512,512]{1,0:T(8,128)(2,1)S(1)}, bf16[512,512]{1,0:T(8,128)(2,1)}, u32[]{:S(2)}) copy-start(bf16[512,512]{1,0:T(8,128)(2,1)} %copy-done.7) | copy-start | bytes 1572868
  40.0 7.7 %copy-start.19 = (bf16[1,2,256,512]{3,2,1,0:T(8,128)(2,1)S(1)}, bf16[1,2,256,512]{3,2,1,0:T(8,128)(2,1)}, u32[]{:S(2)}) copy-start(bf16[1,2,256,512]{3,2,1,0:T(8,128)(2,1)} %param.10) | copy-start | bytes 1572868
  57.0 23.3 %copy-start.9 = (f32[512,512]{1,0:T(8,128)}, f32[512,512]{1,0:T(8,128)S(1)}, u32[]{:S(2)}) copy-start(f32[512,512]{1,0:T(8,128)S(1)} %get-tuple-element.41.d_res_ref) | copy-start | bytes 3145732
  57.0 23.3 %copy-start.13 = (bf16[512,512]{1,0:T(8,128)(2,1)}, bf16[512,512]{1,0:T(8,128)(2,1)S(1)}, u32[]{:S(2)}) copy-start(bf16[512,512]{1,0:T(8,128)(2,1)S(1)} %get-tuple-element.40.d_value_ref) | copy-start | bytes 1572868
  57.0 23.3 %copy-start.15 = (bf16[2,128,1024]{2,1,0:T(8,128)(2,1)}, bf16[2,128,1024]{2,1,0:T(8,128)(2,1)S(1)}, u32[]{:S(2)}) copy-start(bf16[2,128,1024]{2,1,0:T(8,128)(2,1)S(1)} %get-tuple-element.44) | copy-start | bytes 1572868
  57.0 5.6 %collective-permute-start.7 = (f32[88,512]{1,0:T(8,128)S(1)}, f32[88,512]{1,0:T(8,128)S(1)}, u32[]{:S(2)}, u32[]{:S(2)}) collective-permute-start(f32[88,512]{1,0:T(8,128)S(1)} %get-tuple-element.38), channel_id=1, source_target_pairs={{0,8},{4,12},{8,0},{12,4},{16,24},{20,28},{24,16},{28,20},{1,9},{5... | collective-permute-start | bytes 540680 | tf_op jit(solution)/shard_map/ppermute | solution.py:22
  57.9 24.2 %collective-permute-start.12 = (bf16[2,128,1024]{2,1,0:T(8,128)(2,1)}, bf16[2,128,1024]{2,1,0:T(8,128)(2,1)}, u32[]{:S(2)}, u32[]{:S(2)}) collective-permute-start(bf16[2,128,1024]{2,1,0:T(8,128)(2,1)} %get-tuple-element.45), channel_id=1, source_target_pairs={{0,1},{1,0},{2,3},{3,2},{4,5},{5,4},{6,7},{7,6},{8,9},{9,8},{10,11... | collective-permute-start | bytes 1572872 | tf_op jit(solution)/shard_map/ppermute | solution.py:22
  62.6 8.8 %collective-permute-start.8 = (f32[88,512]{1,0:T(8,128)S(1)}, f32[88,512]{1,0:T(8,128)S(1)}, u32[]{:S(2)}, u32[]{:S(2)}) collective-permute-start(f32[88,512]{1,0:T(8,128)S(1)} %add.94), channel_id=1, source_target_pairs={{0,16},{4,20},{8,24},{12,28},{16,0},{20,4},{24,8},{28,12},{1,17},{... | collective-permute-start | bytes 540680 | tf_op jit(solution)/shard_map/ppermute | solution.py:22
  71.5 5.6 %collective-permute-start.9 = (f32[88,512]{1,0:T(8,128)S(1)}, f32[88,512]{1,0:T(8,128)S(1)}, u32[]{:S(2)}, u32[]{:S(2)}) collective-permute-start(f32[88,512]{1,0:T(8,128)S(1)} %add.95), channel_id=1, source_target_pairs={{0,4},{4,0},{8,12},{12,8},{16,20},{20,16},{24,28},{28,24},{1,5},{5... | collective-permute-start | bytes 540680 | tf_op jit(solution)/shard_map/ppermute | solution.py:22
  80.4 1.0 copy-start.11
  81.4 0.8 copy-start.16
  82.2 4.5 %copy-start.17 = (bf16[2,128,1024]{2,1,0:T(8,128)(2,1)S(1)}, bf16[2,128,1024]{2,1,0:T(8,128)(2,1)}, u32[]{:S(2)}) copy-start(bf16[2,128,1024]{2,1,0:T(8,128)(2,1)} %copy-done.16) | copy-start | bytes 1572868
  82.2 3.7 %collective-permute-start.10 = (bf16[2,128,1024]{2,1,0:T(8,128)(2,1)}, bf16[2,128,1024]{2,1,0:T(8,128)(2,1)S(1)}, u32[]{:S(2)}, u32[]{:S(2)}) collective-permute-start(bf16[2,128,1024]{2,1,0:T(8,128)(2,1)} %get-tuple-element.43), channel_id=1, source_target_pairs={{0,1},{1,0},{2,3},{3,2},{4,5},{5,4},{6,7},{7,6},{8,9},{9,8},{10,11... | collective-permute-start | bytes 1572872 | tf_op jit(solution)/shard_map/ppermute | solution.py:22
  84.4 9.5 %collective-permute-start.13 = (bf16[1,128,1024]{2,1,0:T(8,128)(2,1)}, bf16[1,128,1024]{2,1,0:T(8,128)(2,1)}, u32[]{:S(2)}, u32[]{:S(2)}) collective-permute-start(bf16[1,128,1024]{2,1,0:T(8,128)(2,1)} %constant_dynamic-slice_fusion), channel_id=1, source_target_pairs={{0,2},{1,3},{2,0},{3,1},{4,6},{5,7},{6,4},{7,5},{8,10},{9,11},{10,... | collective-permute-start | bytes 786440 | tf_op jit(solution)/shard_map/ppermute | solution.py:22
  85.9 0.8 copy-start.30
  87.9 10.9 %collective-permute-start.11 = (bf16[1,128,1024]{2,1,0:T(8,128)(2,1)S(1)}, bf16[1,128,1024]{2,1,0:T(8,128)(2,1)S(1)}, u32[]{:S(2)}, u32[]{:S(2)}) collective-permute-start(bf16[1,128,1024]{2,1,0:T(8,128)(2,1)S(1)} %constant_dynamic-slice_fusion.1), channel_id=1, source_target_pairs={{0,2},{1,3},{2,0},{3,1},{4,6},{5,7},{6,4},{7,5},{8,10},{9,11},{10,... | collective-permute-start | bytes 786440 | tf_op jit(solution)/shard_map/ppermute | solution.py:22
  94.9 4.0 %copy-start.25 = (bf16[1,128,1024]{2,1,0:T(8,128)(2,1)}, bf16[1,128,1024]{2,1,0:T(8,128)(2,1)S(1)}, u32[]{:S(2)}) copy-start(bf16[1,128,1024]{2,1,0:T(8,128)(2,1)S(1)} %add_convert_fusion.2) | copy-start | bytes 786436
  98.9 0.8 copy-start.26
  99.7 8.1 %collective-permute-start.14 = (bf16[64,2048]{1,0:T(8,128)(2,1)}, bf16[64,2048]{1,0:T(8,128)(2,1)}, u32[]{:S(2)}, u32[]{:S(2)}) collective-permute-start(bf16[64,2048]{1,0:T(8,128)(2,1)} %fusion.2), channel_id=1, source_target_pairs={{0,4},{4,0},{8,12},{12,8},{16,20},{20,16},{24,28},{28,24},{1,5},{5... | collective-permute-start | bytes 786440 | tf_op jit(solution)/shard_map/ppermute | solution.py:22
  99.8 33.2 %copy-start.4 = (bf16[1,2,256,512]{3,2,1,0:T(8,128)(2,1)S(1)}, bf16[1,2,256,512]{3,2,1,0:T(8,128)(2,1)}, u32[]{:S(2)}) copy-start(bf16[1,2,256,512]{3,2,1,0:T(8,128)(2,1)} %param.9) | copy-start | bytes 1572868
  99.8 33.2 %copy-start.10 = (f32[512,512]{1,0:T(8,128)S(1)}, f32[512,512]{1,0:T(8,128)}, u32[]{:S(2)}) copy-start(f32[512,512]{1,0:T(8,128)} %copy-done.9) | copy-start | bytes 3145732
  108.9 0.7 copy-start.27
  110.3 4.5 %collective-permute-start.15 = (bf16[16,2048]{1,0:T(8,128)(2,1)}, bf16[16,2048]{1,0:T(8,128)(2,1)S(1)}, u32[]{:S(2)}, u32[]{:S(2)}) collective-permute-start(bf16[16,2048]{1,0:T(8,128)(2,1)} %get-tuple-element.63), channel_id=1, source_target_pairs={{0,8},{4,12},{8,0},{12,4},{16,24},{20,28},{24,16},{28,20},{1,9},{5... | collective-permute-start | bytes 196616 | tf_op jit(solution)/shard_map/ppermute | solution.py:22
  110.3 6.8 %collective-permute-start.16 = (bf16[16,2048]{1,0:T(8,128)(2,1)}, bf16[16,2048]{1,0:T(8,128)(2,1)S(1)}, u32[]{:S(2)}, u32[]{:S(2)}) collective-permute-start(bf16[16,2048]{1,0:T(8,128)(2,1)} %get-tuple-element.65), channel_id=1, source_target_pairs={{0,16},{4,20},{8,24},{12,28},{16,0},{20,4},{24,8},{28,12},{1,17},{... | collective-permute-start | bytes 196616 | tf_op jit(solution)/shard_map/ppermute | solution.py:22
  113.0 6.2 %collective-permute-start.17 = (bf16[16,2048]{1,0:T(8,128)(2,1)S(1)}, bf16[16,2048]{1,0:T(8,128)(2,1)}, u32[]{:S(2)}, u32[]{:S(2)}) collective-permute-start(bf16[16,2048]{1,0:T(8,128)(2,1)S(1)} %get-tuple-element.64), channel_id=1, source_target_pairs={{0,24},{4,28},{8,16},{12,20},{16,8},{20,12},{24,0},{28,4},{1,25},{... | collective-permute-start | bytes 196616 | tf_op jit(solution)/shard_map/ppermute | solution.py:22
  120.1 7.5 %copy-start.31 = (bf16[16,2048]{1,0:T(8,128)(2,1)}, bf16[16,2048]{1,0:T(8,128)(2,1)S(1)}, u32[]{:S(2)}) copy-start(bf16[16,2048]{1,0:T(8,128)(2,1)S(1)} %fusion.7) | copy-start | bytes 196612
  120.1 6.1 %collective-permute-start.18 = (bf16[16,2048]{1,0:T(8,128)(2,1)S(1)}, bf16[16,2048]{1,0:T(8,128)(2,1)S(1)}, u32[]{:S(2)}, u32[]{:S(2)}) collective-permute-start(bf16[16,2048]{1,0:T(8,128)(2,1)S(1)} %fusion.7), channel_id=1, source_target_pairs={{0,24},{4,28},{8,16},{12,20},{16,8},{20,12},{24,0},{28,4},{1,25},{... | collective-permute-start | bytes 196616 | tf_op jit(solution)/shard_map/ppermute | solution.py:22
  121.9 5.8 %collective-permute-start.19 = (bf16[16,2048]{1,0:T(8,128)(2,1)S(1)}, bf16[16,2048]{1,0:T(8,128)(2,1)S(1)}, u32[]{:S(2)}, u32[]{:S(2)}) collective-permute-start(bf16[16,2048]{1,0:T(8,128)(2,1)S(1)} %fusion.7), channel_id=1, source_target_pairs={{0,16},{4,20},{8,24},{12,28},{16,0},{20,4},{24,8},{28,12},{1,17},{... | collective-permute-start | bytes 196616 | tf_op jit(solution)/shard_map/ppermute | solution.py:22
  121.9 6.4 %collective-permute-start.20 = (bf16[16,2048]{1,0:T(8,128)(2,1)S(1)}, bf16[16,2048]{1,0:T(8,128)(2,1)}, u32[]{:S(2)}, u32[]{:S(2)}) collective-permute-start(bf16[16,2048]{1,0:T(8,128)(2,1)S(1)} %fusion.7), channel_id=1, source_target_pairs={{0,8},{4,12},{8,0},{12,4},{16,24},{20,28},{24,16},{28,20},{1,9},{5... | collective-permute-start | bytes 196616 | tf_op jit(solution)/shard_map/ppermute | solution.py:22
  124.6 6.3 %collective-permute-start.22 = (f32[24,512]{1,0:T(8,128)S(1)}, f32[24,512]{1,0:T(8,128)S(1)}, u32[]{:S(2)}, u32[]{:S(2)}) collective-permute-start(f32[24,512]{1,0:T(8,128)S(1)} %slice.21), channel_id=1, source_target_pairs={{0,1},{1,0},{2,3},{3,2},{4,5},{5,4},{6,7},{7,6},{8,9},{9,8},{10,11... | collective-permute-start | bytes 147464 | tf_op jit(solution)/shard_map/ppermute | solution.py:22
  126.3 1.4 copy-start.32
  127.7 0.6 copy-start.33
  129.3 2.2 %copy-start.28 = (bf16[16,2048]{1,0:T(8,128)(2,1)}, bf16[16,2048]{1,0:T(8,128)(2,1)S(1)}, u32[]{:S(2)}) copy-start(bf16[16,2048]{1,0:T(8,128)(2,1)S(1)} %get-tuple-element.62) | copy-start | bytes 196612
  130.0 10.6 %collective-permute-start.21 = (bf16[64,2048]{1,0:T(8,128)(2,1)}, bf16[64,2048]{1,0:T(8,128)(2,1)}, u32[]{:S(2)}, u32[]{:S(2)}) collective-permute-start(bf16[64,2048]{1,0:T(8,128)(2,1)} %pad_maximum_fusion), channel_id=1, source_target_pairs={{0,4},{4,0},{8,12},{12,8},{16,20},{20,16},{24,28},{28,24},{1,5},{5... | collective-permute-start | bytes 786440 | tf_op jit(solution)/shard_map/ppermute | solution.py:22
  131.5 7.0 %collective-permute-start.23 = (f32[24,512]{1,0:T(8,128)}, f32[24,512]{1,0:T(8,128)S(1)}, u32[]{:S(2)}, u32[]{:S(2)}) collective-permute-start(f32[24,512]{1,0:T(8,128)} %slice_add_fusion), channel_id=1, source_target_pairs={{0,2},{1,3},{2,0},{3,1},{4,6},{5,7},{6,4},{7,5},{8,10},{9,11},{10,... | collective-permute-start | bytes 147464 | tf_op jit(solution)/shard_map/ppermute | solution.py:22
  133.0 1.2 copy-start.12
  134.2 1.0 copy-start.14
  135.3 5.3 %copy-start.29 = (bf16[16,2048]{1,0:T(8,128)(2,1)S(1)}, bf16[16,2048]{1,0:T(8,128)(2,1)}, u32[]{:S(2)}) copy-start(bf16[16,2048]{1,0:T(8,128)(2,1)} %copy-done.28) | copy-start | bytes 196612
